TPU v7x, 32 devices: a whole 2x2x4 slice. The times are simulated.
32 devices in a mesh: dp: 32 (over z, y, x, core).
Axes of the slice: x: 2, y: 2, z: 4, core: 2. Of those that a mesh axis runs over, the one named last changes fastest.
Arguments:
- tokens: bfloat16 [32768, 1024], P('dp'), may hold values from -6 to 6
- lengths: int32 [32], P('dp'), may hold values from 256 to 1024, as said below
- expert_ids: int32 [32768, 2], P('dp'), may hold values from 0 to 15, all different within a row
- slot_order: int32 [32, 1024], P('dp'), may hold values from 0 to 1023, each once within a row
- gain_attn: float32 [1024], replicated, may hold values from 0.1 to 1.9
- w_qkv: bfloat16 [1024, 3072], replicated, may hold values from -0.1875 to 0.1875
- w_out: bfloat16 [1024, 1024], replicated, may hold values from -1.5 to 1.5
- gain_moe: float32 [1024], replicated, may hold values from 0.1 to 1.9
- w_router: bfloat16 [1024, 16], replicated, may hold values from -0.09375 to 0.09375
- w_gate: bfloat16 [32, 1024, 1408], P('dp'), may hold values from -0.1875 to 0.1875
- w_up: bfloat16 [32, 1024, 1408], P('dp'), may hold values from -0.1875 to 0.1875
- w_down: bfloat16 [32, 1408, 1024], P('dp'), may hold values from -0.21875 to 0.21875
- out_grad: bfloat16 [32768, 1024], P('dp'), may hold values from -6 to 6
Outputs:
- block_out: bfloat16 [32768, 1024], P('dp')
- tokens_grad: float32 [32768, 1024], P('dp')
- gain_attn_grad: float32 [1024], P('dp')
- w_qkv_grad: float32 [1024, 3072], P('dp')
- w_out_grad: float32 [1024, 1024], P('dp')
- gain_moe_grad: float32 [1024], P('dp')
- w_router_grad: float32 [1024, 16], P('dp')
- w_gate_grad: float32 [32, 1024, 1408], P('dp')
- w_up_grad: float32 [32, 1024, 1408], P('dp')
- w_down_grad: float32 [32, 1408, 1024], P('dp')
Inputs may be any that keep to these rules, and one draw needn't show every extreme that they name: `lengths`: valid tokens of each sequence, counted from its start; some sequence has 1024. `expert_ids`: a token's two experts differ. `slot_order`: each row is a permutation of the ranks 0 to 1023 of one group's tokens.
All inputs are finite; a program needn't handle non-finite values.
Results may differ from a plain program's by a relative error of at most 0.015.
Values may be sent and summed in bfloat16 or wider, within the bound.
A program may use at most 576 MiB of HBM per device.

v0:
```python
import math

import jax
import jax.numpy as jnp
from jax import lax
from jax.sharding import PartitionSpec as P

HEADS = 16
HEAD_DIM = 64
LEN = 1024


epsilon = 1e-06
mask_fill = -1e30


def inner_rows(left, right):
    return lax.dot_general(
        left, right, (((0,), (0,)), ((), ())), preferred_element_type=jnp.float32
    )


def inner_cols(left, right):
    return lax.dot_general(
        left, right, (((1,), (1,)), ((), ())), preferred_element_type=jnp.float32
    )


def rms_forward(values, gain_vec):
    inverse = lax.rsqrt(jnp.mean(values * values, axis=-1, keepdims=True) + epsilon)
    return (values * inverse * gain_vec, inverse)


def rms_backward(values, inverse, gain_vec, grad_rows):
    scaled = grad_rows * gain_vec
    gain_grad = jnp.sum(values * inverse * grad_rows, axis=0)
    cubed = inverse * inverse * inverse
    input_grad = inverse * scaled - values * cubed * jnp.mean(
        values * scaled, axis=-1, keepdims=True
    )
    return (input_grad, gain_grad)


def routing_slots(expert_ids, valid, ranks, experts, capacity):
    count = ranks.shape[0]
    order = jnp.zeros((count,), jnp.int32).at[ranks].set(jnp.arange(count, dtype=jnp.int32))
    choices_hot = (
        expert_ids[:, :, None] == jnp.arange(experts, dtype=jnp.int32)[None, None, :]
    ).astype(jnp.int32)
    choices_hot = choices_hot * valid[:, None, None].astype(jnp.int32)
    ordered = choices_hot[order]
    first_hot = ordered[:, 0, :]
    second_hot = ordered[:, 1, :]
    first_before = jnp.cumsum(first_hot, axis=0, dtype=jnp.int32) - first_hot
    second_before = jnp.cumsum(second_hot, axis=0, dtype=jnp.int32) - second_hot
    second_before = second_before + jnp.sum(first_hot, axis=0, dtype=jnp.int32)[None, :]
    ranked_slots = jnp.stack(
        [
            jnp.sum(first_before * first_hot, axis=1, dtype=jnp.int32),
            jnp.sum(second_before * second_hot, axis=1, dtype=jnp.int32),
        ],
        axis=1,
    )
    slots = ranked_slots[ranks]
    kept = valid[:, None] & (slots < capacity)
    return (slots, kept)


def shards(
    tokens,
    lengths,
    expert_ids,
    slot_order,
    gain_attn,
    w_qkv,
    w_out,
    gain_moe,
    w_router,
    w_gate,
    w_up,
    w_down,
    out_grad,
):
    tok_dev, width = tokens.shape
    n_dev = lax.axis_size("dp")
    experts = w_router.shape[1]
    split = n_dev // experts
    part_slots = 5 * tok_dev // (4 * n_dev)
    capacity = split * part_slots
    seq_count = lengths.shape[0]
    block_rows = min(512, LEN)
    score_scale = 1.0 / math.sqrt(HEAD_DIM)
    places = jnp.arange(tok_dev, dtype=jnp.int32)
    seq_hot = (places // LEN)[:, None] == jnp.arange(seq_count, dtype=jnp.int32)[None, :]
    token_length = jnp.sum(jnp.where(seq_hot, lengths[None, :], 0), axis=1, dtype=jnp.int32)
    valid = places % LEN < token_length
    valid_f = valid.astype(jnp.float32)[:, None]
    slots, kept = routing_slots(expert_ids, valid, slot_order[0], experts, capacity)
    sentinel = experts * capacity
    flat = jnp.where(kept, expert_ids * capacity + slots, sentinel)
    ids_hot = (
        expert_ids[:, :, None] == jnp.arange(experts, dtype=jnp.int32)[None, None, :]
    ).astype(jnp.float32)

    def place_rows(pair_rows):
        buffer = (
            jnp.zeros((sentinel + 1, width), jnp.bfloat16)
            .at[flat.reshape(-1)]
            .set(pair_rows.reshape(-1, width))
        )
        return buffer[:sentinel].reshape(experts, capacity, width)

    def pick_rows(slot_rows):
        extended = jnp.concatenate([slot_rows, jnp.zeros((1, width), jnp.bfloat16)], axis=0)
        return extended[flat].astype(jnp.float32)

    token_vals = tokens.astype(jnp.float32)
    normed_attn, inverse_attn = rms_forward(token_vals, gain_attn)
    normed_low = normed_attn.astype(jnp.bfloat16)
    projected = jnp.dot(normed_low, w_qkv, preferred_element_type=jnp.float32).astype(jnp.bfloat16)
    shaped = projected.reshape(seq_count, LEN, 3, HEADS, HEAD_DIM)
    queries = shaped[:, :, 0]
    key_rows = shaped[:, :, 1]
    value_rows = shaped[:, :, 2]
    key_places = jnp.arange(LEN, dtype=jnp.int32)

    def masked_scores(query_block, key_block, length_one, row_start):
        scores = (
            jnp.einsum("qhd,khd->hqk", query_block, key_block, preferred_element_type=jnp.float32)
            * score_scale
        )
        query_places = row_start + jnp.arange(query_block.shape[0], dtype=jnp.int32)
        allowed = (key_places[None, :] <= query_places[:, None]) & (
            key_places[None, :] < length_one
        )
        return jnp.where(allowed[None], scores, mask_fill)

    def attend_forward(inputs):
        query_seq, key_seq, value_seq, length_one = inputs
        mixed_parts = []
        norm_parts = []
        for row_start in range(0, LEN, block_rows):
            scores = masked_scores(
                query_seq[row_start : row_start + block_rows], key_seq, length_one, row_start
            )
            highest = jnp.max(scores, axis=-1, keepdims=True)
            raised = jnp.exp(scores - highest)
            summed = jnp.sum(raised, axis=-1, keepdims=True)
            weights_low = (raised / summed).astype(jnp.bfloat16)
            mixed_parts.append(
                jnp.einsum(
                    "hqk,khd->qhd", weights_low, value_seq, preferred_element_type=jnp.float32
                ).astype(jnp.bfloat16)
            )
            norm_parts.append((highest + jnp.log(summed))[:, :, 0])
        return (jnp.concatenate(mixed_parts, axis=0), jnp.concatenate(norm_parts, axis=1))

    mixed, log_norms = lax.map(attend_forward, (queries, key_rows, value_rows, lengths))
    mixed_low = mixed.reshape(tok_dev, width)
    attn_out = jnp.dot(mixed_low, w_out, preferred_element_type=jnp.float32)
    hidden_state = token_vals + valid_f * attn_out
    normed_moe, inverse_moe = rms_forward(hidden_state, gain_moe)
    moe_low = normed_moe.astype(jnp.bfloat16)
    logits = jnp.dot(moe_low, w_router, preferred_element_type=jnp.float32)
    chosen = jnp.sum(logits[:, None, :] * ids_hot, axis=2)
    gates = jax.nn.softmax(chosen, axis=1)
    send_rows = place_rows(jnp.broadcast_to(moe_low[:, None, :], (tok_dev, 2, width)))
    repeated = jnp.broadcast_to(send_rows[:, None], (experts, split, capacity, width)).reshape(
        n_dev, capacity, width
    )
    expert_rows = lax.all_to_all(repeated, "dp", split_axis=0, concat_axis=0, tiled=True).reshape(
        -1, width
    )
    gate_pre = jnp.dot(expert_rows, w_gate[0], preferred_element_type=jnp.float32)
    up_pre = jnp.dot(expert_rows, w_up[0], preferred_element_type=jnp.float32)
    gelu_value, gelu_pull = jax.vjp(jax.nn.gelu, gate_pre)
    hidden_act = (gelu_value * up_pre).astype(jnp.bfloat16)
    partial_out = jnp.dot(hidden_act, w_down[0], preferred_element_type=jnp.float32).astype(
        jnp.bfloat16
    )
    partial_out = partial_out.reshape(n_dev, capacity, width)
    returned = lax.all_to_all(partial_out, "dp", split_axis=0, concat_axis=0, tiled=True)
    slot_out = jnp.sum(
        returned.reshape(experts, split, capacity, width).astype(jnp.float32), axis=1
    )
    slot_out = slot_out.astype(jnp.bfloat16).reshape(-1, width)
    picked = pick_rows(slot_out)
    mixture = jnp.sum(gates[:, :, None] * picked, axis=1)
    block_out = (hidden_state + valid_f * mixture).astype(jnp.bfloat16)
    grad_vals = out_grad.astype(jnp.float32)
    d_mixture = valid_f * grad_vals
    d_gates = jnp.sum(d_mixture[:, None, :] * picked, axis=2)
    d_chosen = gates * (d_gates - jnp.sum(gates * d_gates, axis=1, keepdims=True))
    d_logits = jnp.sum(d_chosen[:, :, None] * ids_hot, axis=1).astype(jnp.bfloat16)
    router_term = inner_rows(moe_low, d_logits)
    d_send = place_rows((gates[:, :, None] * d_mixture[:, None, :]).astype(jnp.bfloat16))
    d_repeated = jnp.broadcast_to(d_send[:, None], (experts, split, capacity, width)).reshape(
        n_dev, capacity, width
    )
    d_expert = lax.all_to_all(d_repeated, "dp", split_axis=0, concat_axis=0, tiled=True).reshape(
        -1, width
    )
    d_hidden = inner_cols(d_expert, w_down[0])
    down_grad = inner_rows(hidden_act, d_expert)
    d_gate_pre = gelu_pull(d_hidden * up_pre)[0].astype(jnp.bfloat16)
    d_up_pre = (d_hidden * gelu_value).astype(jnp.bfloat16)
    gate_grad = inner_rows(expert_rows, d_gate_pre)
    up_grad = inner_rows(expert_rows, d_up_pre)
    d_in_part = (inner_cols(d_gate_pre, w_gate[0]) + inner_cols(d_up_pre, w_up[0])).astype(
        jnp.bfloat16
    )
    d_in_part = d_in_part.reshape(n_dev, capacity, width)
    d_returned = lax.all_to_all(d_in_part, "dp", split_axis=0, concat_axis=0, tiled=True)
    d_in_slots = jnp.sum(
        d_returned.reshape(experts, split, capacity, width).astype(jnp.float32), axis=1
    )
    d_in_slots = d_in_slots.astype(jnp.bfloat16).reshape(-1, width)
    d_moe = inner_cols(d_logits, w_router) + jnp.sum(pick_rows(d_in_slots), axis=1)
    d_hidden_moe, gain_moe_term = rms_backward(hidden_state, inverse_moe, gain_moe, d_moe)
    d_state = grad_vals + d_hidden_moe
    d_attn = (valid_f * d_state).astype(jnp.bfloat16)
    out_term = inner_rows(mixed_low, d_attn)
    d_mixed = (
        inner_cols(d_attn, w_out).astype(jnp.bfloat16).reshape(seq_count, LEN, HEADS, HEAD_DIM)
    )

    def attend_backward(inputs):
        query_seq, key_seq, value_seq, length_one, norm_seq, d_seq = inputs
        d_query_parts = []
        d_key_sum = jnp.zeros((LEN, HEADS, HEAD_DIM), jnp.float32)
        d_value_sum = jnp.zeros((LEN, HEADS, HEAD_DIM), jnp.float32)
        for row_start in range(0, LEN, block_rows):
            row_stop = row_start + block_rows
            query_block = query_seq[row_start:row_stop]
            d_block = d_seq[row_start:row_stop]
            scores = masked_scores(query_block, key_seq, length_one, row_start)
            weights = jnp.exp(scores - norm_seq[:, row_start:row_stop, None])
            d_weights = jnp.einsum(
                "qhd,khd->hqk", d_block, value_seq, preferred_element_type=jnp.float32
            )
            d_value_sum = d_value_sum + jnp.einsum(
                "hqk,qhd->khd",
                weights.astype(jnp.bfloat16),
                d_block,
                preferred_element_type=jnp.float32,
            )
            d_scores = (
                weights * (d_weights - jnp.sum(weights * d_weights, axis=-1, keepdims=True))
            ).astype(jnp.bfloat16)
            d_query_parts.append(
                jnp.einsum("hqk,khd->qhd", d_scores, key_seq, preferred_element_type=jnp.float32)
                * score_scale
            )
            d_key_sum = (
                d_key_sum
                + jnp.einsum(
                    "hqk,qhd->khd", d_scores, query_block, preferred_element_type=jnp.float32
                )
                * score_scale
            )
        d_query = jnp.concatenate(d_query_parts, axis=0)
        return jnp.stack([d_query, d_key_sum, d_value_sum], axis=1)

    d_qkv = lax.map(attend_backward, (queries, key_rows, value_rows, lengths, log_norms, d_mixed))
    d_qkv = d_qkv.reshape(tok_dev, 3 * width).astype(jnp.bfloat16)
    qkv_term = inner_rows(normed_low, d_qkv)
    d_normed_attn = inner_cols(d_qkv, w_qkv)
    d_token_attn, gain_attn_term = rms_backward(token_vals, inverse_attn, gain_attn, d_normed_attn)
    tokens_grad = d_state + d_token_attn
    qkv_grad, out_grad_rows, router_grad, gain_attn_grad, gain_moe_grad = (
        lax.psum_scatter(qkv_term, "dp", scatter_dimension=0, tiled=True),
        lax.psum_scatter(out_term, "dp", scatter_dimension=0, tiled=True),
        lax.psum_scatter(router_term, "dp", scatter_dimension=0, tiled=True),
        lax.psum_scatter(gain_attn_term, "dp", scatter_dimension=0, tiled=True),
        lax.psum_scatter(gain_moe_term, "dp", scatter_dimension=0, tiled=True),
    )
    return (
        block_out,
        tokens_grad,
        gain_attn_grad,
        qkv_grad,
        out_grad_rows,
        gain_moe_grad,
        router_grad,
        gate_grad[None],
        up_grad[None],
        down_grad[None],
    )


def solution(mesh):
    placed = (
        P("dp", None),
        P("dp"),
        P("dp", None),
        P("dp", None),
        P(),
        P(),
        P(),
        P(),
        P(),
        P("dp", None, None),
        P("dp", None, None),
        P("dp", None, None),
        P("dp", None),
    )
    return jax.shard_map(
        shards,
        mesh=mesh,
        in_specs=placed,
        out_specs=(
            P("dp", None),
            P("dp", None),
            P("dp"),
            P("dp", None),
            P("dp", None),
            P("dp"),
            P("dp", None),
            P("dp", None, None),
            P("dp", None, None),
            P("dp", None, None),
        ),
        check_vma=False,
    )
```

profile of v0, /device:TPU:12, one launch (start us, length us, event | category | flops | bytes accessed | tf_op | source)
XLA Modules:
  0.0 1186.8 jit_solution(17971776418950782323)
XLA Ops:
  21.5 8.7 gather_fusion
  42.4 8.0 reduce-window.14
  70.8 12.1 %convolution_convert_fusion.1 = bf16[1024,3072]{1,0:T(8,128)(2,1)} fusion(bf16[1024,3072]{1,0:T(8,128)(2,1)} %param.18, bf16[1024,1024]{0,1:T(8,128)(2,1)} %copy.68, f32[1024]{0:T(1024)S(1)} %copy-done.46, f32[1024]{0:T(1024)S(1)} %get-tuple-element.112), kind=kOutput, calls=%fused_computation.52 | convolution fusion | flops 6449790976 | bytes 14688256 | tf_op jit(solution)/shard_map/dot_general | solution.py:120
  82.9 8.7 copy.69
  92.9 16.1 %fusion.86 = (f32[16,512]{1,0:T(8,128)S(1)}, f32[16,512,1024]{2,1,0:T(8,128)}) fusion(bf16[1,1024,3,16,64]{1,4,3,2,0:T(8,128)(2,1)} %bitcast.167, pred[512,1024]{1,0:T(8,128)(4,1)} %get-tuple-element.116), kind=kOutput, calls=%fused_computation.178 | convolution fusion | flops 1098899456 | bytes 37257216 | tf_op jit(solution)/shard_map/while/body/eval_jaxpr/qhd,khd->hqk/dot_general | solution.py:129
  109.0 14.3 %fusion.1 = f32[16,512]{1,0:T(8,128)S(1)} fusion(f32[16,512,1024]{2,1,0:T(8,128)} %get-tuple-element.118, f32[16,512]{1,0:T(8,128)S(1)} %get-tuple-element.117), kind=kLoop, calls=%fused_computation.20 | loop fusion | flops 16769024 | bytes 33619968 | tf_op jit(solution)/shard_map/while/body/eval_jaxpr/reduce_sum | solution.py:148
  123.4 13.8 %fusion.51 = bf16[512,16,64]{0,2,1:T(8,128)(2,1)} fusion(f32[16,512,1024]{2,1,0:T(8,128)} %get-tuple-element.118, f32[16,512]{1,0:T(8,128)S(1)} %fusion.1, f32[16,512]{1,0:T(8,128)S(1)} %get-tuple-element.117, bf16[1,1024,3,16,64]{1,4,3,2,0:T(8,128)(2,1)S(1)} %bitcast.175), kind=kOutput, calls=%fused_computation.109 | convolution fusion | flops 1099431936 | bytes 36765696 | tf_op jit(solution)/shard_map/while/body/eval_jaxpr/hqk,khd->qhd/dot_general | solution.py:151
  137.1 13.8 %fusion.87 = (f32[16,512]{1,0:T(8,128)S(1)}, f32[16,512,1024]{2,1,0:T(8,128)}) fusion(bf16[1,1024,3,16,64]{1,4,3,2,0:T(8,128)(2,1)S(1)} %bitcast.176, pred[512,1024]{1,0:T(8,128)(4,1)S(1)} %get-tuple-element.115), kind=kOutput, calls=%fused_computation.179 | convolution fusion | flops 1098899456 | bytes 37257216 | tf_op jit(solution)/shard_map/while/body/eval_jaxpr/qhd,khd->hqk/dot_general | solution.py:129
  150.9 14.3 %fusion = f32[16,512]{1,0:T(8,128)S(1)} fusion(f32[16,512,1024]{2,1,0:T(8,128)} %get-tuple-element.120, f32[16,512]{1,0:T(8,128)S(1)} %get-tuple-element.119), kind=kLoop, calls=%fused_computation.19 | loop fusion | flops 16769024 | bytes 33619968 | tf_op jit(solution)/shard_map/while/body/eval_jaxpr/reduce_sum | solution.py:148
  165.3 13.9 %fusion.50 = bf16[512,16,64]{0,2,1:T(8,128)(2,1)S(1)} fusion(f32[16,512,1024]{2,1,0:T(8,128)} %get-tuple-element.120, f32[16,512]{1,0:T(8,128)S(1)} %fusion, f32[16,512]{1,0:T(8,128)S(1)} %get-tuple-element.119, bf16[1,1024,3,16,64]{1,4,3,2,0:T(8,128)(2,1)S(1)} %bitcast.177), kind=kOutput, calls=%fused_computation.108 | convolution fusion | flops 1099431936 | bytes 36765696 | tf_op jit(solution)/shard_map/while/body/eval_jaxpr/hqk,khd->qhd/dot_general | solution.py:151
  204.4 12.2 %scatter_custom_fusion.1 = bf16[1281,1024]{1,0:T(8,128)(2,1)} fusion(s32[2048]{0:T(1024)} %bitcast.207, bf16[2048,1024]{1,0:T(8,128)(2,1)} %reshape.503, bf16[]{:T(256)} %constant.128.clone.1), kind=kCustom, calls=%fused_computation.113 | custom fusion | bytes 2624000 | tf_op jit(solution)/shard_map/scatter | solution.py:109
  248.0 10.9 mul.383
  261.2 15.3 %select_reduce_fusion.1 = f32[1024,2]{1,0:T(8,128)S(1)} fusion(f32[1024,16]{1,0:T(8,128)S(1)} %fusion.88, s32[1024,2]{1,0:T(8,128)} %copy-done.12), kind=kLoop, calls=%fused_computation.118 | loop fusion | flops 96256 | bytes 81920 | tf_op jit(solution)/shard_map/reduce_sum | solution.py:165
  280.2 13.2 %scatter_custom_fusion.2 = bf16[1281,1024]{1,0:T(8,128)(2,1)} fusion(s32[2048]{0:T(1024)} %bitcast.208, f32[2048,1024]{1,0:T(8,128)} %mul.383, f32[2048]{0:T(1024)S(1)} %div.73, bf16[]{:T(256)} %constant.128.clone.1), kind=kCustom, calls=%fused_computation.69 | custom fusion | flops 4194304 | bytes 11020800 | tf_op jit(solution)/shard_map/scatter | solution.py:109
  296.9 43.8 %all-to-all-done = bf16[32,80,1024]{2,1,0:T(8,128)(2,1)} async-done(((bf16[32,80,1024]{2,1,0:T(8,128)(2,1)}), bf16[32,80,1024]{2,1,0:T(8,128)(2,1)}, u32[]{:S(2)}, u32[]{:S(2)}) %all-to-all-start) | async-done | bytes 5242912 | tf_op jit(solution)/shard_map/all_to_all | solution.py:171
  345.7 7.7 all-to-all-start.2
  353.4 14.1 %fusion.34 = f32[2560,1408]{1,0:T(8,128)} fusion(bf16[2560,1024]{1,0:T(8,128)(2,1)} %bitcast.28, bf16[1,1024,1408]{2,1,0:T(8,128)(2,1)} %param.23), kind=kOutput, calls=%fused_computation.83 | convolution fusion | flops 7381975040 | bytes 22544384 | tf_op jit(solution)/shard_map/dot_general | solution.py:175
  367.5 13.3 %fusion.38 = f32[2560,1408]{1,0:T(8,128)} fusion(bf16[2560,1024]{1,0:T(8,128)(2,1)} %bitcast.28, bf16[1,1024,1408]{2,1,0:T(8,128)(2,1)S(1)} %copy-done.50), kind=kOutput, calls=%fused_computation.87 | convolution fusion | flops 7381975040 | bytes 22544384 | tf_op jit(solution)/shard_map/dot_general | solution.py:174
  380.8 85.5 %all-to-all-done.2 = bf16[32,80,1024]{2,1,0:T(8,128)(2,1)} async-done(((bf16[32,80,1024]{2,1,0:T(8,128)(2,1)}), bf16[32,80,1024]{2,1,0:T(8,128)(2,1)}, u32[]{:S(2)}, u32[]{:S(2)}) %all-to-all-start.2) | async-done | bytes 5242912 | tf_op jit(solution)/shard_map/all_to_all | solution.py:200
  466.3 30.2 %multiply_convert_fusion.2 = (bf16[2560,1408]{1,0:T(8,128)(2,1)}, bf16[2560,1408]{1,0:T(8,128)(2,1)}, bf16[2560,1408]{1,0:T(8,128)(2,1)}) fusion(f32[2560,1408]{1,0:T(8,128)} %fusion.38, f32[2560,1408]{1,0:T(8,128)} %fusion.34, bf16[2560,1024]{1,0:T(8,128)(2,1)} %bitcast.37, bf16[1,1408,1024]{2,1,0:T(8,128)(2,1)S(1)} %copy-done), kind=kOutput, calls=%fused_computation.38 | convolution fusion | flops 7475691520 | bytes 58589184 | tf_op jit(solution)/shard_map/dot_general | solution.py:24
  496.5 12.4 %convolution_convert_fusion = bf16[2560,1024]{1,0:T(8,128)(2,1)} fusion(bf16[2560,1408]{1,0:T(8,128)(2,1)} %get-tuple-element.103, bf16[1,1408,1024]{2,1,0:T(8,128)(2,1)S(1)} %copy-done), kind=kOutput, calls=%fused_computation.51 | convolution fusion | flops 7384596480 | bytes 15335424 | tf_op jit(solution)/shard_map/dot_general | solution.py:178
  516.4 10.9 fusion.36
  527.3 12.4 %add_convert_fusion = bf16[2560,1024]{1,0:T(8,128)(2,1)} fusion(f32[2560,1024]{1,0:T(8,128)S(1)} %fusion.36, bf16[2560,1408]{1,0:T(8,128)(2,1)} %get-tuple-element.101, bf16[1,1024,1408]{2,1,0:T(8,128)(2,1)S(1)} %copy-done.52), kind=kOutput, calls=%fused_computation.41 | convolution fusion | flops 7387217920 | bytes 25821184 | tf_op jit(solution)/shard_map/dot_general | solution.py:24
  539.7 89.6 %all-to-all-done.1 = bf16[32,80,1024]{2,1,0:T(8,128)(2,1)} async-done(((bf16[32,80,1024]{2,1,0:T(8,128)(2,1)}), bf16[32,80,1024]{2,1,0:T(8,128)(2,1)}, u32[]{:S(2)}, u32[]{:S(2)}) %all-to-all-start.1) | async-done | bytes 5242912 | tf_op jit(solution)/shard_map/all_to_all | solution.py:182
  629.4 7.5 all-to-all-start.3
  641.5 9.8 gather_fusion.2
  651.3 9.8 reshape.520
  661.1 19.1 %multiply_reduce_fusion.2 = (f32[1024,2]{1,0:T(8,128)}, f32[1024,1024]{1,0:T(8,128)}) fusion(f32[1024,2,1024]{2,1,0:T(2,128)} %reshape.520, f32[1024,1024]{1,0:T(8,128)} %copy.86, f32[1024,2]{1,0:T(8,128)S(1)} %copy-done.15), kind=kLoop, calls=%fused_computation.43 | loop fusion | flops 7337984 | bytes 16793600 | tf_op jit(solution)/shard_map/reduce_sum | solution.py:192
  696.1 53.8 %all-to-all-done.3 = bf16[32,80,1024]{2,1,0:T(8,128)(2,1)} async-done(((bf16[32,80,1024]{2,1,0:T(8,128)(2,1)}), bf16[32,80,1024]{2,1,0:T(8,128)(2,1)}, u32[]{:S(2)}, u32[]{:S(2)}) %all-to-all-start.3) | async-done | bytes 5242912 | tf_op jit(solution)/shard_map/all_to_all | solution.py:213
  754.2 9.8 gather_fusion.3
  764.1 9.7 reshape.521
  773.8 13.0 %reduce_sum.227 = f32[1024,1024]{1,0:T(8,128)} reduce(f32[1024,2,1024]{2,1,0:T(2,128)} %reshape.521, f32[]{:T(128)} %constant.121.clone.1), dimensions={1}, to_apply=%region_25.26 | reduce | flops 1048576 | bytes 12582916 | tf_op jit(solution)/shard_map/reduce_sum | solution.py:218
  805.7 22.4 %multiply_reduce_fusion.1 = (f32[16,512]{1,0:T(8,128)S(1)}, f32[16,512,1024]{2,1,0:T(8,128)}) fusion(f32[16,512,1024]{2,1,0:T(8,128)} %get-tuple-element.120, f32[16,512]{1,0:T(8,128)S(1)} %log_add_fusion.1, bf16[512,16,64]{0,2,1:T(8,128)(2,1)S(1)} %bitcast.183, bf16[1,1024,3,16,64]{1,4,3,2,0:T(8,128)(2,1)S(1)} %bitcast.180), kind=kOutput, calls=%fused_computation.11 | convolution fusion | flops 1098899456 | bytes 70320128 | tf_op jit(solution)/shard_map/while/body/eval_jaxpr/qhd,khd->hqk/dot_general | solution.py:238
  828.1 28.1 %multiply_convert_fusion.1 = bf16[16,512,1024]{2,1,0:T(8,128)(2,1)} fusion(f32[16,512,1024]{2,1,0:T(8,128)} %get-tuple-element.125, f32[16,512,1024]{2,1,0:T(8,128)} %get-tuple-element.120, f32[16,512]{1,0:T(8,128)S(1)} %get-tuple-element.124, f32[16,512]{1,0:T(8,128)S(1)} %log_add_fusion.1), kind=kLoop, calls=%fused_computation.10 | loop fusion | flops 33554432 | bytes 83951616 | tf_op jit(solution)/shard_map/while/body/eval_jaxpr/convert_element_type | solution.py:249
  856.2 12.6 %fusion.48 = bf16[512,16,64]{0,2,1:T(8,128)(2,1)} fusion(bf16[16,512,1024]{2,1,0:T(8,128)(2,1)} %multiply_convert_fusion.1, bf16[1,1024,3,16,64]{1,4,3,2,0:T(8,128)(2,1)} %bitcast.168), kind=kOutput, calls=%fused_computation.106 | convolution fusion | flops 1074790400 | bytes 19922944 | tf_op jit(solution)/shard_map/while/body/eval_jaxpr/hqk,khd->qhd/dot_general | solution.py:251
  876.1 23.2 %multiply_reduce_fusion = (f32[16,512]{1,0:T(8,128)S(1)}, f32[16,512,1024]{2,1,0:T(8,128)}) fusion(f32[16,512,1024]{2,1,0:T(8,128)} %get-tuple-element.118, f32[16,512]{1,0:T(8,128)S(1)} %log_add_fusion, bf16[512,16,64]{0,2,1:T(8,128)(2,1)S(1)} %bitcast.185, bf16[1,1024,3,16,64]{1,4,3,2,0:T(8,128)(2,1)} %bitcast.169), kind=kOutput, calls=%fused_computation.8 | convolution fusion | flops 1098899456 | bytes 70320128 | tf_op jit(solution)/shard_map/while/body/eval_jaxpr/qhd,khd->hqk/dot_general | solution.py:238
  899.3 28.1 %multiply_convert_fusion = bf16[16,512,1024]{2,1,0:T(8,128)(2,1)} fusion(f32[16,512,1024]{2,1,0:T(8,128)} %get-tuple-element.127, f32[16,512,1024]{2,1,0:T(8,128)} %get-tuple-element.118, f32[16,512]{1,0:T(8,128)S(1)} %get-tuple-element.126, f32[16,512]{1,0:T(8,128)S(1)} %log_add_fusion), kind=kLoop, calls=%fused_computation.7 | loop fusion | flops 33554432 | bytes 83951616 | tf_op jit(solution)/shard_map/while/body/eval_jaxpr/convert_element_type | solution.py:249
  927.4 12.6 %fusion.49 = bf16[512,16,64]{0,2,1:T(8,128)(2,1)} fusion(bf16[16,512,1024]{2,1,0:T(8,128)(2,1)} %multiply_convert_fusion, bf16[1,1024,3,16,64]{1,4,3,2,0:T(8,128)(2,1)} %bitcast.170), kind=kOutput, calls=%fused_computation.107 | convolution fusion | flops 1074790400 | bytes 19922944 | tf_op jit(solution)/shard_map/while/body/eval_jaxpr/hqk,khd->qhd/dot_general | solution.py:251
  943.3 11.4 fusion.58
  961.9 15.6 %fusion.4 = f32[16,64,1024]{2,1,0:T(8,128)} fusion(bf16[512,16,64]{0,2,1:T(8,128)(2,1)S(1)} %bitcast.186, f32[16,512,1024]{2,1,0:T(8,128)} %get-tuple-element.118, f32[16,512]{1,0:T(8,128)S(1)} %log_add_fusion), kind=kOutput, calls=%fused_computation.25 | convolution fusion | flops 1090519040 | bytes 38830080 | tf_op jit(solution)/shard_map/while/body/eval_jaxpr/hqk,qhd->khd/dot_general | solution.py:241
  977.5 16.3 %fusion.40 = bf16[1024,1,16,64]{0,3,2,1:T(8,128)(2,1)} fusion(f32[16,64,1024]{2,1,0:T(8,128)} %fusion.4, bf16[512,16,64]{0,2,1:T(8,128)(2,1)S(1)} %bitcast.184, f32[16,512,1024]{2,1,0:T(8,128)} %get-tuple-element.120, f32[16,512]{1,0:T(8,128)S(1)} %log_add_fusion.1), kind=kOutput, calls=%fused_computation.90 | convolution fusion | flops 1092616192 | bytes 40927232 | tf_op jit(solution)/shard_map/while/body/eval_jaxpr/hqk,qhd->khd/dot_general | solution.py:241
  1000.1 9.3 fusion.60
  1009.4 14.4 %convolution_bitcast_fusion.1 = f32[1,1024,1408]{2,1,0:T(8,128)} fusion(bf16[2560,1024]{1,0:T(8,128)(2,1)} %bitcast.28, bf16[2560,1408]{1,0:T(8,128)(2,1)} %get-tuple-element.101), kind=kOutput, calls=%fused_computation.60 | convolution fusion | flops 7381975040 | bytes 18219008 | tf_op jit(solution)/shard_map/dot_general | solution.py:18
  1023.8 14.1 %convolution_bitcast_fusion.2 = f32[1,1024,1408]{2,1,0:T(8,128)} fusion(bf16[2560,1024]{1,0:T(8,128)(2,1)} %bitcast.28, bf16[2560,1408]{1,0:T(8,128)(2,1)} %get-tuple-element.102), kind=kOutput, calls=%fused_computation.61 | convolution fusion | flops 7381975040 | bytes 18219008 | tf_op jit(solution)/shard_map/dot_general | solution.py:18
  1037.9 11.6 convolution_bitcast_fusion
  1053.6 13.2 %fusion.22 = (f32[1024]{0:T(1024)S(1)}, f32[1024]{0:T(1024)S(1)}, f32[1024,1024]{0,1:T(8,128)}) fusion(bf16[1024,1024]{0,1:T(8,128)(2,1)S(1)} %copy-done.9, f32[1024]{0:T(1024)S(1)} %copy-done.44, f32[1024]{0:T(1024)S(1)} %copy-done.47, bf16[1024,3072]{1,0:T(8,128)(2,1)} %param.18, bf16[1024,3072]{0,1:T(8,128)(2,1)} %bitcast.192), kind=kOutput, calls=%fused_computation.63 | convolution fusion | flops 6449788928 | bytes 18890752 | tf_op jit(solution)/shard_map/dot_general | solution.py:24
  1066.8 47.6 %all-reduce.4 = (f32[1024]{0:T(1024)S(1)}, f32[1024]{0:T(1024)S(1)}) all-reduce(f32[1024]{0:T(1024)S(1)} %get-tuple-element.95, f32[1024]{0:T(1024)S(1)} %copy-done.41), channel_id=2, replica_groups=mesh['dp'=32] {'dp'}, use_global_device_ids=true, to_apply=%region_31.32.clone | all-reduce | flops 2048 | bytes 16384
  1129.7 50.1 %reduce-scatter.6.cloned.1.call-done = f32[32,3072]{1,0:T(8,128)} async-done(((f32[1024,3072]{1,0:T(8,128)}), f32[32,3072]{1,0:T(8,128)}) %reduce-scatter.6.cloned.1.call-update) | async-done | bytes 393232 | tf_op jit(solution)/shard_map/reduce_scatter | solution.py:271
  (237 shorter events, 212.7 us)
Async XLA Ops:
  7.2 459.1 %copy-start = (bf16[1,1408,1024]{2,1,0:T(8,128)(2,1)S(1)}, bf16[1,1408,1024]{2,1,0:T(8,128)(2,1)}, u32[]{:S(2)}) copy-start(bf16[1,1408,1024]{2,1,0:T(8,128)(2,1)} %param.24) | copy-start | bytes 8650756
  9.0 43.1 %copy-start.12 = (s32[1024,2]{1,0:T(8,128)}, s32[1024,2]{1,0:T(8,128)S(1)}, u32[]{:S(2)}) copy-start(s32[1024,2]{1,0:T(8,128)S(1)} %copy.70) | copy-start | bytes 24580
  52.2 8.2 copy-start.49
  60.4 10.4 copy-start.46
  82.9 8.7 copy-start.48
  91.6 31.7 %slice-start.4 = ((s8[6291456]{0:T(1024)(128)(4,1)}), s8[4194304]{0:T(1024)(128)(4,1)S(1)}, s32[]{:S(2)}) async-start(s8[6291456]{0:T(1024)(128)(4,1)} %bitcast.173), calls=%async_computation.14 | async-start | bytes 8388608
  92.9 30.4 %slice-start.5 = ((s8[6291456]{0:T(1024)(128)(4,1)}), s8[2097152]{0:T(1024)(128)(4,1)S(1)}, s32[]{:S(2)}) async-start(s8[6291456]{0:T(1024)(128)(4,1)} %bitcast.173), calls=%async_computation.15 | async-start | bytes 4194304
  109.0 14.3 %copy-start.21 = (f32[16,512]{1,0:T(8,128)}, f32[16,512]{1,0:T(8,128)S(1)}, u32[]{:S(2)}) copy-start(f32[16,512]{1,0:T(8,128)S(1)} %get-tuple-element.117) | copy-start | bytes 98308
  123.4 13.8 %copy-start.27 = (f32[16,512]{1,0:T(8,128)}, f32[16,512]{1,0:T(8,128)S(1)}, u32[]{:S(2)}) copy-start(f32[16,512]{1,0:T(8,128)S(1)} %fusion.1) | copy-start | bytes 98308
  150.9 14.3 %copy-start.23 = (f32[16,512]{1,0:T(8,128)}, f32[16,512]{1,0:T(8,128)S(1)}, u32[]{:S(2)}) copy-start(f32[16,512]{1,0:T(8,128)S(1)} %get-tuple-element.119) | copy-start | bytes 98308
  165.2 13.9 %copy-start.29 = (f32[16,512]{1,0:T(8,128)}, f32[16,512]{1,0:T(8,128)S(1)}, u32[]{:S(2)}) copy-start(f32[16,512]{1,0:T(8,128)S(1)} %fusion) | copy-start | bytes 98308
  165.2 13.9 %copy-start.20 = (bf16[512,16,64]{0,2,1:T(8,128)(2,1)S(1)}, bf16[512,16,64]{0,2,1:T(8,128)(2,1)}, u32[]{:S(2)}) copy-start(bf16[512,16,64]{0,2,1:T(8,128)(2,1)} %fusion.51) | copy-start | bytes 3145732
  165.2 14.2 %copy-start.53 = (bf16[1024,1024]{1,0:T(8,128)(2,1)S(1)}, bf16[1024,1024]{1,0:T(8,128)(2,1)}, u32[]{:S(2)}) copy-start(bf16[1024,1024]{1,0:T(8,128)(2,1)} %param.19) | copy-start | bytes 6291460
  221.4 119.3 %all-to-all-start = ((bf16[32,80,1024]{2,1,0:T(8,128)(2,1)}), bf16[32,80,1024]{2,1,0:T(8,128)(2,1)}, u32[]{:S(2)}, u32[]{:S(2)}) async-start(bf16[32,80,1024]{2,1,0:T(8,128)(2,1)} %bitcast.181), calls=%async_computation | async-start | bytes 10485760 | tf_op jit(solution)/shard_map/all_to_all | solution.py:171
  248.0 10.9 copy-start.25
  276.6 16.8 %copy-start.5 = (f32[1024,2]{1,0:T(8,128)}, f32[1024,2]{1,0:T(8,128)S(1)}, u32[]{:S(2)}) copy-start(f32[1024,2]{1,0:T(8,128)S(1)} %select_reduce_fusion.1) | copy-start | bytes 24580
  276.8 16.6 %copy-start.31 = (f32[1024]{0:T(1024)}, f32[1024]{0:T(1024)S(1)}, u32[]{:S(2)}) copy-start(f32[1024]{0:T(1024)S(1)} %reduce_max.31) | copy-start | bytes 12292
  345.7 120.6 %all-to-all-start.2 = ((bf16[32,80,1024]{2,1,0:T(8,128)(2,1)}), bf16[32,80,1024]{2,1,0:T(8,128)(2,1)}, u32[]{:S(2)}, u32[]{:S(2)}) async-start(bf16[32,80,1024]{2,1,0:T(8,128)(2,1)} %bitcast.182), calls=%async_computation.2 | async-start | bytes 10485760 | tf_op jit(solution)/shard_map/all_to_all | solution.py:200
  353.4 14.1 %copy-start.50 = (bf16[1,1024,1408]{2,1,0:T(8,128)(2,1)S(1)}, bf16[1,1024,1408]{2,1,0:T(8,128)(2,1)}, u32[]{:S(2)}) copy-start(bf16[1,1024,1408]{2,1,0:T(8,128)(2,1)} %param.22) | copy-start | bytes 8650756
  508.9 7.4 copy-start.51
  508.9 120.5 %all-to-all-start.1 = ((bf16[32,80,1024]{2,1,0:T(8,128)(2,1)}), bf16[32,80,1024]{2,1,0:T(8,128)(2,1)}, u32[]{:S(2)}, u32[]{:S(2)}) async-start(bf16[32,80,1024]{2,1,0:T(8,128)(2,1)} %bitcast.194), calls=%async_computation.1 | async-start | bytes 10485760 | tf_op jit(solution)/shard_map/all_to_all | solution.py:182
  516.3 11.0 copy-start.52
  629.4 7.6 copy-start.19
  629.4 7.8 copy-start.22
  629.4 7.8 copy-start.28
  629.4 7.9 copy-start.24
  629.4 7.9 copy-start.30
  629.4 120.6 %all-to-all-start.3 = ((bf16[32,80,1024]{2,1,0:T(8,128)(2,1)}), bf16[32,80,1024]{2,1,0:T(8,128)(2,1)}, u32[]{:S(2)}, u32[]{:S(2)}) async-start(bf16[32,80,1024]{2,1,0:T(8,128)(2,1)} %bitcast.193), calls=%async_computation.3 | async-start | bytes 10485760 | tf_op jit(solution)/shard_map/all_to_all | solution.py:213
  636.9 491.5 %reduce-scatter.10.cloned.1.call-start = ((), (), s32[]{:S(2)}) async-start(), calls=%async_computation.9 | async-start | bytes 540672
  651.3 9.8 copy-start.15
  680.1 8.6 copy-start.13
  680.2 14.4 %copy-start.4 = (bf16[1024,1024]{0,1:T(8,128)(2,1)S(1)}, bf16[1024,1024]{0,1:T(8,128)(2,1)}, u32[]{:S(2)}) copy-start(bf16[1024,1024]{0,1:T(8,128)(2,1)} %multiply_convert_fusion.8) | copy-start | bytes 6291460
  694.5 59.4 %copy-start.16 = (bf16[1024,16]{1,0:T(8,128)(2,1)}, bf16[1024,16]{1,0:T(8,128)(2,1)S(1)}, u32[]{:S(2)}) copy-start(bf16[1024,16]{1,0:T(8,128)(2,1)S(1)} %select_reduce_fusion) | copy-start | bytes 98308
  696.1 433.6 %reduce-scatter.8.cloned.1.call-start = ((), (), s32[]{:S(2)}) async-start(), calls=%async_computation.8 | async-start | bytes 4325376 | tf_op jit(solution)/shard_map/reduce_scatter | solution.py:272
  792.3 6.6 copy-start.10
  792.3 6.6 copy-start.40
  792.3 6.6 copy-start.45
  798.8 6.3 slice-start.6
  876.0 303.8 %reduce-scatter.6.cloned.1.call-start = ((), (), s32[]{:S(2)}) async-start(), calls=%async_computation.7 | async-start | bytes 12976128 | tf_op jit(solution)/shard_map/reduce_scatter | solution.py:271
  940.0 14.7 %slice-start = ((s8[16777216]{0:T(1024)(128)(4,1)}), s8[4194304]{0:T(1024)(128)(4,1)S(1)}, s32[]{:S(2)}) async-start(s8[16777216]{0:T(1024)(128)(4,1)} %bitcast.165), calls=%async_computation.10 | async-start | bytes 8388608
  943.3 11.4 slice-start.1
  943.3 11.4 slice-start.2
  943.3 11.4 slice-start.3
  1009.4 28.5 %slice-start.9 = ((s8[7208960]{0:T(1024)(128)(4,1)}), s8[4194304]{0:T(1024)(128)(4,1)S(1)}, s32[]{:S(2)}) async-start(s8[7208960]{0:T(1024)(128)(4,1)} %bitcast.209), calls=%async_computation.19 | async-start | bytes 8388608
  1023.8 14.1 %slice-start.10 = ((s8[7208960]{0:T(1024)(128)(4,1)}), s8[3014656]{0:T(1024)(128)(4,1)S(1)}, s32[]{:S(2)}) async-start(s8[7208960]{0:T(1024)(128)(4,1)} %bitcast.209), calls=%async_computation.20 | async-start | bytes 6029312
  1053.6 13.2 %copy-start.41 = (f32[1024]{0:T(1024)S(1)}, f32[1024]{0:T(1024)}, u32[]{:S(2)}) copy-start(f32[1024]{0:T(1024)} %get-tuple-element.91) | copy-start | bytes 12292
  1053.6 62.0 %copy-start.42 = (f32[1024]{0:T(1024)S(1)}, f32[1024]{0:T(1024)}, u32[]{:S(2)}) copy-start(f32[1024]{0:T(1024)} %get-tuple-element.111) | copy-start | bytes 12292
  1115.6 64.3 %copy-start.1 = (bf16[1,1408,1024]{2,1,0:T(8,128)(2,1)S(1)}, bf16[1,1408,1024]{2,1,0:T(8,128)(2,1)}, u32[]{:S(2)}) copy-start(bf16[1,1408,1024]{2,1,0:T(8,128)(2,1)} %param.24) | copy-start | bytes 8650756
  (25 other events, 101.1 us)
Sparse Core Ops, SparseCore 0:
  696.2 117.2 reduce-scatter.9
  876.1 115.6 reduce-scatter.7
  1009.5 170.2 reduce-scatter.5
where the time goes:
time: 1200 us; the launch traced here: 1190 us
  matrix products  369 us (31%)
  waiting for transfers between devices  323 us (27%)
  other arithmetic  223 us (19%)
  local copies, waits for them, and re-layouts  180 us (15%)
  blocking collectives  47.6 us (4%)
  starting transfers between devices  29.1 us (2%)
  between operations  15.6 us (1%)
    all_to_all x1, waiting for transfers between devices, shards(): lax.all_to_all(partial_out, 'dp', split_axis=0, concat_axis=0, tiled=True)  89.6 us
    all_to_all x1, waiting for transfers between devices, shards(): lax.all_to_all(d_repeated, 'dp', split_axis=0, concat_axis=0, tiled=True)  85.5 us
    dot_general x6, matrix products, inner_cols(): lax.dot_general(left, right, (((1,), (1,)), ((), ())), preferred_element_...  74.7 us
    dot_general x5, matrix products, inner_rows(): lax.dot_general(left, right, (((0,), (0,)), ((), ())), preferred_element_...  56.6 us
    convert_element_type x2, other arithmetic, attend_backward(): d_scores = (weights * (d_weights - jnp.sum(weights * d_weights, axis=-1,...  56.2 us
    all_to_all x1, waiting for transfers between devices, shards(): lax.all_to_all(d_in_part, 'dp', split_axis=0, concat_axis=0, tiled=True)  53.8 us
    reduce_scatter x1, waiting for transfers between devices, shards(): lax.psum_scatter(qkv_term, 'dp', scatter_dimension=0, tiled=True)  50.1 us
    unnamed x1, blocking collectives  47.6 us
  transfers between devices with their start and end apart: 7, of which 5 were waited for; matrix products, arithmetic and copies ran while one was open for 43% of the time, Pallas kernels for 0%

commit v1 on v0

v1 whole, which is shorter than its diff:
```python
import functools
import math

import jax
import jax.numpy as jnp
from jax import lax
from jax.experimental import pallas as pl
from jax.experimental.pallas import tpu as pltpu
from jax.sharding import PartitionSpec as P

HEADS = 16
HEAD_DIM = 64
LEN = 1024
LANES = 128
MIB = 1 << 20

epsilon = 1e-06
mask_fill = -1e30
f32 = jnp.float32
bf16 = jnp.bfloat16


def dot_nn(left, right, **kw):
    return lax.dot_general(left, right, (((1,), (0,)), ((), ())), preferred_element_type=f32, **kw)


def dot_nt(left, right, **kw):
    return lax.dot_general(left, right, (((1,), (1,)), ((), ())), preferred_element_type=f32, **kw)


def dot_tn(left, right, **kw):
    return lax.dot_general(left, right, (((0,), (0,)), ((), ())), preferred_element_type=f32, **kw)


def iota(shape, dim):
    return lax.broadcasted_iota(jnp.int32, shape, dim)


def params(mib, **kw):
    return pltpu.CompilerParams(vmem_limit_bytes=mib * MIB, **kw)


def cost(flops, nbytes, trans=0):
    return pl.CostEstimate(flops=int(flops), bytes_accessed=int(nbytes), transcendentals=int(trans))


def slot_kernel(capacity, experts, len_ref, ids_ref, rank_col_ref, rank_row_ref, col_ref, row_ref):
    count = ids_ref.shape[0]
    length = len_ref[0]
    ids = ids_ref[...]
    first, second = ids[:, 0:1], ids[:, 1:2]
    lane = iota((count, LANES), 1)
    place = iota((count, LANES), 0)
    hot0 = (lane == first) & (lane < experts)
    hot1 = (lane == second + experts) & (lane >= experts) & (lane < 2 * experts)
    valid = place < length
    hot = jnp.where((hot0 | hot1) & valid, 1.0, 0.0).astype(bf16)
    before = (rank_row_ref[...] < rank_col_ref[...]).astype(f32).astype(bf16)
    counts = dot_nn(before, hot)
    shifted = (lane == first + experts) & (lane >= experts) & (lane < 2 * experts) & valid
    totals = jnp.sum(jnp.where(shifted, 1.0, 0.0), axis=0, keepdims=True)
    slot0 = jnp.sum(jnp.where(hot0, counts, 0.0), axis=1, keepdims=True).astype(jnp.int32)
    slot1 = jnp.sum(jnp.where(hot1, counts + totals, 0.0), axis=1, keepdims=True).astype(jnp.int32)
    sentinel = experts * capacity
    ok = valid[:, 0:1]
    flat0 = jnp.where(ok & (slot0 < capacity), first * capacity + slot0, sentinel)
    flat1 = jnp.where(ok & (slot1 < capacity), second * capacity + slot1, sentinel)
    col = jnp.where(lane == 0, flat0, 0) + jnp.where(lane == 1, flat1, 0)
    col = col + jnp.where(lane == 2, first, 0) + jnp.where(lane == 3, second, 0)
    col = col + jnp.where(lane == 4, ok.astype(jnp.int32), 0)
    col_ref[...] = col
    row_ref[...] = jnp.transpose(col.astype(f32))[0:8, :].astype(jnp.int32)


def make_slots(lengths, expert_ids, slot_order, experts, capacity):
    count = expert_ids.shape[0]
    return pl.pallas_call(
        functools.partial(slot_kernel, capacity, experts),
        out_shape=(
            jax.ShapeDtypeStruct((count, LANES), jnp.int32),
            jax.ShapeDtypeStruct((8, count), jnp.int32),
        ),
        in_specs=[
            pl.BlockSpec(memory_space=pltpu.SMEM),
            pl.BlockSpec(memory_space=pltpu.VMEM),
            pl.BlockSpec(memory_space=pltpu.VMEM),
            pl.BlockSpec(memory_space=pltpu.VMEM),
        ],
        out_specs=(pl.BlockSpec(memory_space=pltpu.VMEM), pl.BlockSpec(memory_space=pltpu.VMEM)),
        compiler_params=params(40),
        cost_estimate=cost(2 * count * count * LANES, 4 * count * LANES),
        name="slots",
    )(lengths, expert_ids, slot_order.reshape(count, 1), slot_order)


def dispatch_kernel(rows, row_ref, data_ref, out_ref):
    count = data_ref.shape[0]
    slot = pl.program_id(0) * rows + iota((rows, count), 0)
    hot = (slot == row_ref[0:1, :]) | (slot == row_ref[1:2, :])
    out_ref[...] = dot_nn(jnp.where(hot, 1.0, 0.0).astype(bf16), data_ref[...]).astype(bf16)


def dispatch(row, data, slots):
    count, width = data.shape
    rows = 256
    return pl.pallas_call(
        functools.partial(dispatch_kernel, rows),
        out_shape=jax.ShapeDtypeStruct((slots, width), bf16),
        grid=(slots // rows,),
        in_specs=[
            pl.BlockSpec((8, count), lambda i: (0, 0)),
            pl.BlockSpec((count, width), lambda i: (0, 0)),
        ],
        out_specs=pl.BlockSpec((rows, width), lambda i: (i, 0)),
        compiler_params=params(40),
        cost_estimate=cost(2 * slots * count * width, 2 * (slots + count) * width),
        name="dispatch",
    )(row, data)


def dispatch_grad_kernel(rows, row_ref, data_ref, out_ref):
    count, width = data_ref.shape
    slot = pl.program_id(0) * rows + iota((rows, count), 0)
    hot0 = slot == row_ref[0:1, :]
    hot1 = slot == row_ref[1:2, :]
    both = jnp.where(hot0 | hot1, 1.0, 0.0).astype(bf16)
    out_ref[:, 0:width] = dot_nn(both, data_ref[...]).astype(bf16)
    other = jnp.where(hot0, row_ref[3:4, :], 0) + jnp.where(hot1, row_ref[2:3, :], 0)
    other = jnp.sum(other.astype(f32), axis=1, keepdims=True)
    out_ref[:, width:] = jnp.broadcast_to(other, (rows, LANES)).astype(bf16)


def dispatch_grad(row, data, slots):
    count, width = data.shape
    rows = 256
    return pl.pallas_call(
        functools.partial(dispatch_grad_kernel, rows),
        out_shape=jax.ShapeDtypeStruct((slots, width + LANES), bf16),
        grid=(slots // rows,),
        in_specs=[
            pl.BlockSpec((8, count), lambda i: (0, 0)),
            pl.BlockSpec((count, width), lambda i: (0, 0)),
        ],
        out_specs=pl.BlockSpec((rows, width + LANES), lambda i: (i, 0)),
        compiler_params=params(40),
        cost_estimate=cost(2 * slots * count * width, 2 * (slots + count) * width),
        name="dispatch_grad",
    )(row, data)


SCALE2 = math.log2(math.e) / math.sqrt(HEAD_DIM)
QB = 256


def attend_kernel(q_ref, k_ref, v_ref, mixed_ref, lse_ref):
    lane = iota((QB, LANES), 1)
    wide = jnp.concatenate([v_ref[...], jnp.ones_like(v_ref)], axis=1)
    causal = iota((QB, QB), 1) <= iota((QB, QB), 0)
    for block in range(LEN // QB):
        start, stop = block * QB, (block + 1) * QB
        query = q_ref[start:stop, :]
        halves, norms = [], []
        for head in range(2):
            mine = (lane // HEAD_DIM) == head
            scores = dot_nt(jnp.where(mine, query, jnp.zeros_like(query)), k_ref[0:stop, :])
            tail = jnp.where(causal, scores[:, start:stop], mask_fill)
            scores = tail if block == 0 else jnp.concatenate([scores[:, 0:start], tail], axis=1)
            highest = jnp.max(scores, axis=1, keepdims=True) * SCALE2
            raised = jnp.exp2(scores * SCALE2 - highest)
            out = dot_nn(raised.astype(bf16), wide[0:stop, :])
            summed = out[:, LANES:]
            halves.append(out[:, 0:LANES] / summed)
            norms.append(highest + jnp.log2(summed))
        mixed_ref[start:stop, :] = jnp.where(lane < HEAD_DIM, halves[0], halves[1]).astype(bf16)
        norm = jnp.where(lane == 0, norms[0], norms[1])
        lse_ref[0, :, start:stop] = jnp.transpose(norm)[0:8, :]


def attend(qkv):
    count, width3 = qkv.shape
    width = width3 // 3
    pairs = width // LANES
    return pl.pallas_call(
        attend_kernel,
        out_shape=(
            jax.ShapeDtypeStruct((count, width), bf16),
            jax.ShapeDtypeStruct((pairs, 8, count), f32),
        ),
        grid=(pairs,),
        in_specs=[
            pl.BlockSpec((count, LANES), lambda i: (0, i)),
            pl.BlockSpec((count, LANES), lambda i: (0, i + pairs)),
            pl.BlockSpec((count, LANES), lambda i: (0, i + 2 * pairs)),
        ],
        out_specs=(
            pl.BlockSpec((count, LANES), lambda i: (0, i)),
            pl.BlockSpec((1, 8, count), lambda i: (i, 0, 0)),
        ),
        compiler_params=params(40),
        cost_estimate=cost(2 * 4 * count * count * width, 8 * count * width, 8 * count * count),
        name="attend",
    )(qkv, qkv, qkv)


def attend_back_kernel(q_ref, k_ref, v_ref, o_ref, do_ref, lse_ref, out_ref, dk_sc, dv_sc):
    lane = iota((QB, LANES), 1)
    keep = iota((QB, QB), 0) <= iota((QB, QB), 1)
    dk_sc[...] = jnp.zeros_like(dk_sc)
    dv_sc[...] = jnp.zeros_like(dv_sc)
    sub = iota((8, LANES), 0)
    picks = jnp.where(iota((8, LANES), 1) // HEAD_DIM == sub, 1.0, 0.0)
    low = (iota((LEN, LANES), 1) // HEAD_DIM) == 0
    key = k_ref[...]
    none = jnp.zeros_like(key)
    keys = (jnp.where(low, key, none), jnp.where(low, none, key))
    for block in range(LEN // QB):
        start, stop = block * QB, (block + 1) * QB
        query = q_ref[start:stop, :]
        d_out = do_ref[start:stop, :]
        product = d_out.astype(f32) * o_ref[start:stop, :].astype(f32)
        delta = dot_nt(picks, product, precision=lax.Precision.HIGHEST)
        d_query = jnp.zeros((QB, LANES), f32)
        for head in range(2):
            mine = (lane // HEAD_DIM) == head
            query_one = jnp.where(mine, query, jnp.zeros_like(query))
            d_one = jnp.where(mine, d_out, jnp.zeros_like(d_out))
            scores = dot_nt(k_ref[0:stop, :], query_one)
            tail = jnp.where(keep, scores[start:stop, :], mask_fill)
            scores = tail if block == 0 else jnp.concatenate([scores[0:start, :], tail], axis=0)
            probs = jnp.exp2(scores * SCALE2 - lse_ref[0, head : head + 1, start:stop])
            d_probs = dot_nt(v_ref[0:stop, :], d_one)
            d_scores = (probs * (d_probs - delta[head : head + 1, :])).astype(bf16)
            dv_sc[0:stop, :] += dot_nn(probs.astype(bf16), d_one)
            dk_sc[0:stop, :] += dot_nn(d_scores, query_one)
            d_query = d_query + dot_tn(d_scores, keys[head][0:stop, :])
        out_ref[0, start:stop, :] = (d_query * (1.0 / math.sqrt(HEAD_DIM))).astype(bf16)
    out_ref[1, :, :] = (dk_sc[...] * (1.0 / math.sqrt(HEAD_DIM))).astype(bf16)
    out_ref[2, :, :] = dv_sc[...].astype(bf16)


def attend_back(qkv, mixed, d_mixed, lse):
    count, width = mixed.shape
    pairs = width // LANES
    return pl.pallas_call(
        attend_back_kernel,
        out_shape=jax.ShapeDtypeStruct((3, count, width), bf16),
        grid=(pairs,),
        in_specs=[
            pl.BlockSpec((count, LANES), lambda i: (0, i)),
            pl.BlockSpec((count, LANES), lambda i: (0, i + pairs)),
            pl.BlockSpec((count, LANES), lambda i: (0, i + 2 * pairs)),
            pl.BlockSpec((count, LANES), lambda i: (0, i)),
            pl.BlockSpec((count, LANES), lambda i: (0, i)),
            pl.BlockSpec((1, 8, count), lambda i: (i, 0, 0)),
        ],
        out_specs=pl.BlockSpec((3, count, LANES), lambda i: (0, 0, i)),
        scratch_shapes=[pltpu.VMEM((count, LANES), f32), pltpu.VMEM((count, LANES), f32)],
        compiler_params=params(40),
        cost_estimate=cost(5 * 4 * count * count * width, 16 * count * width, 8 * count * count),
        name="attend_back",
    )(qkv, qkv, qkv, mixed, d_mixed, lse)


def middle_kernel(experts, mixed_ref, w_out_ref, tok_ref, gain_ref, wr_ref, col_ref, h_ref, low_ref, gate_ref):
    rows = mixed_ref.shape[0]
    col = col_ref[...]
    first, second, valid = col[:, 2:3], col[:, 3:4], col[:, 4:5].astype(f32)
    attn = dot_nn(mixed_ref[...], w_out_ref[...])
    hidden = tok_ref[...].astype(f32) + valid * attn
    h_ref[...] = hidden
    inverse = lax.rsqrt(jnp.mean(hidden * hidden, axis=1, keepdims=True) + epsilon)
    low = (hidden * inverse * gain_ref[...]).astype(bf16)
    low_ref[...] = low
    logits = dot_nn(low, wr_ref[...])
    lane = iota((rows, LANES), 1)
    own = jnp.sum(jnp.where(lane == first, logits, 0.0), axis=1, keepdims=True)
    alt = jnp.sum(jnp.where(lane == second, logits, 0.0), axis=1, keepdims=True)
    gate0 = 1.0 / (1.0 + jnp.exp(alt - own))
    gate1 = 1.0 / (1.0 + jnp.exp(own - alt))
    gate_ref[...] = jnp.where(lane == 0, gate0, 0.0) + jnp.where(lane == 1, gate1, 0.0)


def middle(mixed, w_out, tokens, gain, wr, col, experts):
    count, width = mixed.shape
    rows = 256
    whole = lambda i: (0, 0)
    part = lambda i: (i, 0)
    return pl.pallas_call(
        functools.partial(middle_kernel, experts),
        out_shape=(
            jax.ShapeDtypeStruct((count, width), f32),
            jax.ShapeDtypeStruct((count, width), bf16),
            jax.ShapeDtypeStruct((count, LANES), f32),
        ),
        grid=(count // rows,),
        in_specs=[
            pl.BlockSpec((rows, width), part),
            pl.BlockSpec((width, width), whole),
            pl.BlockSpec((rows, width), part),
            pl.BlockSpec((1, width), whole),
            pl.BlockSpec((width, LANES), whole),
            pl.BlockSpec((rows, LANES), part),
        ],
        out_specs=(
            pl.BlockSpec((rows, width), part),
            pl.BlockSpec((rows, width), part),
            pl.BlockSpec((rows, LANES), part),
        ),
        compiler_params=params(40),
        cost_estimate=cost(2 * count * width * width, 12 * count * width),
        name="middle",
    )(mixed, w_out, tokens, gain.reshape(1, width), wr, col)


GELU_C = math.sqrt(2.0 / math.pi)


def expert_kernel(
    split, x_ref, g_ref, wg_ref, wu_ref, wd_ref, wr_ref, act_ref, dgp_ref, dup_ref, de_ref, part_ref, din_ref
):
    rows, width = x_ref.shape
    me = lax.axis_index("dp")
    expert, part = me // split, lax.rem(me, split)
    x = x_ref[...]
    lane = iota((rows, LANES), 1)
    logits = dot_nn(x, wr_ref[...])
    own = jnp.sum(jnp.where(lane == expert, logits, 0.0), axis=1, keepdims=True)
    other = g_ref[:, width:].astype(f32).astype(jnp.int32)
    alt = jnp.sum(jnp.where(lane == other, logits, 0.0), axis=1, keepdims=True)
    gate = 1.0 / (1.0 + jnp.exp(alt - own))
    d_rows = (g_ref[:, 0:width].astype(f32) * gate).astype(bf16)
    de_ref[...] = d_rows
    pre = dot_nn(x, wg_ref[...])
    up = dot_nn(x, wu_ref[...])
    d_hidden = dot_nt(d_rows, wd_ref[...])
    square = pre * pre
    bent = jnp.tanh(GELU_C * pre * (1.0 + 0.044715 * square))
    half = 0.5 * (1.0 + bent)
    gelu = pre * half
    slope = half + 0.5 * pre * (1.0 - bent * bent) * (GELU_C * (1.0 + 3 * 0.044715 * square))
    act = (gelu * up).astype(bf16)
    act_ref[...] = act
    dgp = (d_hidden * up * slope).astype(bf16)
    dup = (d_hidden * gelu).astype(bf16)
    dgp_ref[...] = dgp
    dup_ref[...] = dup
    pull = jnp.sum(act.astype(f32) * d_hidden, axis=1, keepdims=True)
    pull_high = pull.astype(bf16)
    pull_low = (pull - pull_high.astype(f32)).astype(bf16)
    part_ref[...] = dot_nn(act, wd_ref[...]).astype(bf16)
    din_ref[:, 0:width] = (dot_nt(dgp, wg_ref[...]) + dot_nt(dup, wu_ref[...])).astype(bf16)
    extra = jnp.where(lane == 2 * part, pull_high.astype(f32), 0.0)
    extra = extra + jnp.where(lane == 2 * part + 1, pull_low.astype(f32), 0.0)
    din_ref[:, width:] = extra.astype(bf16)


def expert_pass(x, g, wg, wu, wd, wr, split):
    count, width = x.shape
    ff = wg.shape[1]
    rows = 256
    whole = lambda i: (0, 0)
    part = lambda i: (i, 0)
    once = dict(pipeline_mode=pl.Buffered(1))
    return pl.pallas_call(
        functools.partial(expert_kernel, split),
        out_shape=(
            jax.ShapeDtypeStruct((count, ff), bf16),
            jax.ShapeDtypeStruct((count, ff), bf16),
            jax.ShapeDtypeStruct((count, ff), bf16),
            jax.ShapeDtypeStruct((count, width), bf16),
            jax.ShapeDtypeStruct((count, width), bf16),
            jax.ShapeDtypeStruct((count, width + LANES), bf16),
        ),
        grid=(count // rows,),
        in_specs=[
            pl.BlockSpec((rows, width), part),
            pl.BlockSpec((rows, width + LANES), part),
            pl.BlockSpec((width, ff), whole, **once),
            pl.BlockSpec((width, ff), whole, **once),
            pl.BlockSpec((ff, width), whole, **once),
            pl.BlockSpec((width, LANES), whole),
        ],
        out_specs=(
            pl.BlockSpec((rows, ff), part),
            pl.BlockSpec((rows, ff), part),
            pl.BlockSpec((rows, ff), part),
            pl.BlockSpec((rows, width), part),
            pl.BlockSpec((rows, width), part),
            pl.BlockSpec((rows, width + LANES), part),
        ),
        compiler_params=params(56),
        cost_estimate=cost(12 * count * width * ff, 2 * count * (3 * ff + 5 * width), count * ff),
        name="experts",
    )(x, g, wg, wu, wd, wr)


def hot_rows(col, k, rows, slots):
    return jnp.where(iota((rows, slots), 1) == col[:, k : k + 1], 1.0, 0.0).astype(bf16)


def state_kernel(
    col_ref, gate_ref, din_ref, h_ref, og_ref, gain_ref, wr_ref, dstate_ref, dattn_ref, dlog_ref, gterm_ref
):
    rows, width = h_ref.shape
    slots = din_ref.shape[0]
    col = col_ref[...]
    valid = col[:, 4:5].astype(f32)
    hot0, hot1 = hot_rows(col, 0, rows, slots), hot_rows(col, 1, rows, slots)
    pulls = din_ref[:, width:]
    pull0 = jnp.sum(dot_nn(hot0, pulls), axis=1, keepdims=True)
    pull1 = jnp.sum(dot_nn(hot1, pulls), axis=1, keepdims=True)
    gathered = dot_nn(hot0 + hot1, din_ref[:, 0:width])
    gate0, gate1 = gate_ref[:, 0:1], gate_ref[:, 1:2]
    total = pull0 + pull1
    lane = iota((rows, LANES), 1)
    d_log = jnp.where(lane == col[:, 2:3], pull0 - gate0 * total, 0.0)
    d_log = d_log + jnp.where(lane == col[:, 3:4], pull1 - gate1 * total, 0.0)
    d_log = d_log.astype(bf16)
    dlog_ref[...] = d_log
    d_moe = gathered + dot_nt(d_log, wr_ref[...])
    hidden = h_ref[...]
    inverse = lax.rsqrt(jnp.mean(hidden * hidden, axis=1, keepdims=True) + epsilon)
    normal = hidden * inverse
    scaled = gain_ref[...] * d_moe
    share = jnp.mean(normal * scaled, axis=1, keepdims=True)
    d_state = og_ref[...].astype(f32) + inverse * (scaled - normal * share)
    dstate_ref[...] = d_state
    dattn_ref[...] = (valid * d_state).astype(bf16)
    term = jnp.sum((normal * d_moe).reshape(rows // 8, 8, width), axis=0)

    @pl.when(pl.program_id(0) == 0)
    def _():
        gterm_ref[...] = jnp.zeros_like(gterm_ref)

    gterm_ref[...] += term


def state_back(col, gates, din, hidden, out_grad, gain, wr):
    count, width = hidden.shape
    slots = din.shape[0]
    rows = 256
    whole = lambda i: (0, 0)
    part = lambda i: (i, 0)
    return pl.pallas_call(
        state_kernel,
        out_shape=(
            jax.ShapeDtypeStruct((count, width), f32),
            jax.ShapeDtypeStruct((count, width), bf16),
            jax.ShapeDtypeStruct((count, LANES), bf16),
            jax.ShapeDtypeStruct((8, width), f32),
        ),
        grid=(count // rows,),
        in_specs=[
            pl.BlockSpec((rows, LANES), part),
            pl.BlockSpec((rows, LANES), part),
            pl.BlockSpec((slots, width + LANES), whole),
            pl.BlockSpec((rows, width), part),
            pl.BlockSpec((rows, width), part),
            pl.BlockSpec((1, width), whole),
            pl.BlockSpec((width, LANES), whole),
        ],
        out_specs=(
            pl.BlockSpec((rows, width), part),
            pl.BlockSpec((rows, width), part),
            pl.BlockSpec((rows, LANES), part),
            pl.BlockSpec((8, width), whole),
        ),
        compiler_params=params(48),
        cost_estimate=cost(2 * slots * count * width, 14 * count * width),
        name="state_back",
    )(col, gates, din, hidden, out_grad, gain.reshape(1, width), wr)


def block_out_kernel(col_ref, gate_ref, rows_ref, h_ref, out_ref):
    rows, width = h_ref.shape
    slots = rows_ref.shape[0]
    col = col_ref[...]
    pick0 = dot_nn(hot_rows(col, 0, rows, slots), rows_ref[...])
    pick1 = dot_nn(hot_rows(col, 1, rows, slots), rows_ref[...])
    out_ref[...] = (h_ref[...] + gate_ref[:, 0:1] * pick0 + gate_ref[:, 1:2] * pick1).astype(bf16)


def make_block_out(col, gates, slot_rows, hidden):
    count, width = hidden.shape
    slots = slot_rows.shape[0]
    rows = 256
    whole = lambda i: (0, 0)
    part = lambda i: (i, 0)
    return pl.pallas_call(
        block_out_kernel,
        out_shape=jax.ShapeDtypeStruct((count, width), bf16),
        grid=(count // rows,),
        in_specs=[
            pl.BlockSpec((rows, LANES), part),
            pl.BlockSpec((rows, LANES), part),
            pl.BlockSpec((slots, width), whole),
            pl.BlockSpec((rows, width), part),
        ],
        out_specs=pl.BlockSpec((rows, width), part),
        compiler_params=params(40),
        cost_estimate=cost(4 * slots * count * width, 9 * count * width),
        name="block_out",
    )(col, gates, slot_rows, hidden)


def input_kernel(d_ref, w_ref, tok_ref, gain_ref, dstate_ref, grad_ref, gterm_ref):
    rows, width = tok_ref.shape
    d_normed = dot_nt(d_ref[0], w_ref[:, 0:width])
    for i in range(1, 3):
        d_normed = d_normed + dot_nt(d_ref[i], w_ref[:, i * width : (i + 1) * width])
    values = tok_ref[...].astype(f32)
    inverse = lax.rsqrt(jnp.mean(values * values, axis=1, keepdims=True) + epsilon)
    normal = values * inverse
    scaled = gain_ref[...] * d_normed
    share = jnp.mean(normal * scaled, axis=1, keepdims=True)
    grad_ref[...] = dstate_ref[...] + inverse * (scaled - normal * share)
    term = jnp.sum((normal * d_normed).reshape(rows // 8, 8, width), axis=0)

    @pl.when(pl.program_id(0) == 0)
    def _():
        gterm_ref[...] = jnp.zeros_like(gterm_ref)

    gterm_ref[...] += term


def input_back(d_qkv, w_qkv, tokens, gain, d_state):
    count, width = tokens.shape
    rows = 256
    whole = lambda i: (0, 0)
    part = lambda i: (i, 0)
    return pl.pallas_call(
        input_kernel,
        out_shape=(
            jax.ShapeDtypeStruct((count, width), f32),
            jax.ShapeDtypeStruct((8, width), f32),
        ),
        grid=(count // rows,),
        in_specs=[
            pl.BlockSpec((3, rows, width), lambda i: (0, i, 0)),
            pl.BlockSpec((width, 3 * width), whole),
            pl.BlockSpec((rows, width), part),
            pl.BlockSpec((1, width), whole),
            pl.BlockSpec((rows, width), part),
        ],
        out_specs=(pl.BlockSpec((rows, width), part), pl.BlockSpec((8, width), whole)),
        compiler_params=params(48),
        cost_estimate=cost(6 * count * width * width, 22 * count * width),
        name="input_back",
    )(d_qkv, w_qkv, tokens, gain.reshape(1, width), d_state)


def shards(
    tokens,
    lengths,
    expert_ids,
    slot_order,
    gain_attn,
    w_qkv,
    w_out,
    gain_moe,
    w_router,
    w_gate,
    w_up,
    w_down,
    out_grad,
):
    tok_dev, width = tokens.shape
    n_dev = lax.axis_size("dp")
    experts = w_router.shape[1]
    split = n_dev // experts
    capacity = split * (5 * tok_dev // (4 * n_dev))
    slots = experts * capacity
    me = lax.axis_index("dp")
    part = lax.rem(me, split)
    same_part = [[e * split + p for e in range(experts)] for p in range(split)]
    same_expert = [[e * split + p for p in range(split)] for e in range(experts)]
    swap = [(d, d ^ 1) for d in range(n_dev)]

    def across(blocks):
        return lax.all_to_all(blocks, "dp", 0, 0, axis_index_groups=same_part, tiled=True)

    def share(rows):
        if split == 2:
            return jnp.concatenate([rows, lax.ppermute(rows, "dp", swap)], axis=0)
        return lax.all_gather(rows, "dp", axis_index_groups=same_expert, tiled=True)

    def settle(pieces):
        if split == 2:
            theirs = lax.ppermute(pieces[1], "dp", swap)
            return (pieces[0].astype(f32) + theirs.astype(f32)).astype(bf16)
        got = lax.all_to_all(pieces, "dp", 0, 0, axis_index_groups=same_expert, tiled=True)
        return jnp.sum(got.astype(f32), axis=0).astype(bf16)

    def send_in(rows):
        return share(across(rows.reshape(experts, capacity, -1)).reshape(slots, -1))

    def send_back(rows):
        summed = settle(rows.reshape(split, slots, -1))
        return across(summed.reshape(experts, capacity, -1)).reshape(slots, -1)

    def reduce_rows(term):
        pieces = term.reshape(experts, split, -1, term.shape[-1])
        if split == 2:
            mine = lax.dynamic_index_in_dim(pieces, part, 1, keepdims=False)
            theirs = lax.dynamic_index_in_dim(pieces, 1 - part, 1, keepdims=False)
            theirs = lax.ppermute(theirs.astype(bf16), "dp", swap)
            summed = (mine + theirs.astype(f32)).astype(bf16)
        else:
            pieces = jnp.moveaxis(pieces, 1, 0).astype(bf16)
            got = lax.all_to_all(pieces, "dp", 0, 0, axis_index_groups=same_expert, tiled=True)
            summed = jnp.sum(got.astype(f32), axis=0).astype(bf16)
        return jnp.sum(across(summed).astype(f32), axis=0)

    wr = jnp.pad(w_router, ((0, 0), (0, LANES - experts)))
    col, row = make_slots(lengths, expert_ids, slot_order, experts, capacity)
    grad_in = send_in(dispatch_grad(row, out_grad, slots))

    token_vals = tokens.astype(f32)
    inverse_attn = lax.rsqrt(jnp.mean(token_vals * token_vals, axis=-1, keepdims=True) + epsilon)
    normed_low = (token_vals * inverse_attn * gain_attn).astype(bf16)
    qkv = jnp.dot(normed_low, w_qkv, preferred_element_type=f32).astype(bf16)
    mixed, lse = attend(qkv)
    hidden, moe_low, gates = middle(mixed, w_out, tokens, gain_moe, wr, col, experts)

    rows_in = send_in(dispatch(row, moe_low, slots))
    act, d_pre, d_up, d_rows, partial_out, d_in = expert_pass(
        rows_in, grad_in, w_gate[0], w_up[0], w_down[0], wr, split
    )
    d_in_back = send_back(d_in)
    slot_out = send_back(partial_out)

    d_state, d_attn, d_log, gain_moe_rows = state_back(
        col, gates, d_in_back, hidden, out_grad, gain_moe, wr
    )
    out_term = dot_tn(mixed, d_attn)
    router_term = dot_tn(moe_low, d_log)
    gain_moe_term = jnp.sum(gain_moe_rows, axis=0)
    d_mixed = dot_nt(d_attn, w_out).astype(bf16)
    d_qkv = attend_back(qkv, mixed, d_mixed, lse)
    tokens_grad, gain_attn_rows = input_back(d_qkv, w_qkv, tokens, gain_attn, d_state)
    qkv_term = jnp.concatenate([dot_tn(normed_low, d_qkv[i]) for i in range(3)], axis=1)
    gain_attn_term = jnp.sum(gain_attn_rows, axis=0)

    lane = jnp.arange(LANES, dtype=jnp.int32)[None, :]
    extra = jnp.where(lane == experts, gain_moe_term[:, None], router_term)
    early = reduce_rows(jnp.concatenate([out_term, extra], axis=1))
    late_extra = jnp.where(lane == 0, gain_attn_term[:, None], 0.0)
    late = reduce_rows(jnp.concatenate([qkv_term, late_extra], axis=1))

    down_grad = dot_tn(act, d_rows)
    gate_grad = dot_tn(rows_in, d_pre)
    up_grad = dot_tn(rows_in, d_up)
    block_out = make_block_out(col, gates, slot_out, hidden)
    return (
        block_out,
        tokens_grad,
        late[:, 3 * width],
        late[:, 0 : 3 * width],
        early[:, 0:width],
        early[:, width + experts],
        early[:, width : width + experts],
        gate_grad[None],
        up_grad[None],
        down_grad[None],
    )


def solution(mesh):
    rows, one = P("dp", None), P("dp")
    cube = P("dp", None, None)
    return jax.shard_map(
        shards,
        mesh=mesh,
        in_specs=(rows, one, rows, rows, P(), P(), P(), P(), P(), cube, cube, cube, rows),
        out_specs=(rows, rows, one, rows, rows, one, rows, cube, cube, cube),
        check_vma=False,
    )
```

time: 1200 us -> 609 us (0.51)
  matrix products: 369 us -> 66.4 us
  other arithmetic: 223 us -> 44.2 us
  Pallas kernels: 0 us -> 172 us
  local copies, waits for them, and re-layouts: 180 us -> 47.8 us
  waiting for transfers between devices: 323 us -> 230 us
  blocking collectives: 47.6 us -> 0 us
  between operations: 15.6 us -> 2.26 us
    dot_general x29 -> x10, matrix products: 367 us -> 66.4 us  [the longest x8 54.4 us: dot_tn(): lax.dot_general(left, right, (((0,), (0,)), ((), ())), preferred_element_...]
    pallas_call x0 -> x10, Pallas kernels: none -> 172 us  [the longest x1 61.1 us: expert_pass(): pl.pallas_call(functools.partial(expert_kernel, split), out_shape=(jax.Sh...]
    reduce_sum x13 -> x5, other arithmetic: 96.4 us -> 4.69 us  [the longest x2 2.59 us: reduce_rows(): return jnp.sum(across(summed).astype(f32), axis=0)]
    all_to_all x4 -> x6, waiting for transfers between devices: 273 us -> 217 us  [across(): lax.all_to_all(blocks, 'dp', 0, 0, axis_index_groups=same_part, tiled=True)]
    reduce_scatter x2 -> x0, waiting for transfers between devices: 50.1 us -> none  [the longest x1 50.1 us: shards(): lax.psum_scatter(qkv_term, 'dp', scatter_dimension=0, tiled=True)]
    unnamed x1 -> x0, blocking collectives: 47.6 us -> none
    convert_element_type x4, other arithmetic: 58.5 us -> 16.8 us  [the longest x2 9.12 us: reduce_rows(): summed = (mine + theirs.astype(f32)).astype(bf16)]
    gather x4 -> x0, local copies, waits for them, and re-layouts: 32.4 us -> none  [the longest x2 19.6 us: pick_rows(): return extended[flat].astype(jnp.float32)]
  transfers between devices with their start and end apart: 7 -> 12, of which waited for: 5 -> 9; matrix products, arithmetic and copies ran while one was open for 43% -> 20% of each run, Pallas kernels for 0% -> 13%
where the time goes in v1:
time: 609 us; the launch traced here: 600 us
  waiting for transfers between devices  230 us (38%)
  Pallas kernels  172 us (28%)
  matrix products  66.4 us (11%)
  local copies, waits for them, and re-layouts  47.8 us (8%)
  other arithmetic  44.2 us (7%)
  starting transfers between devices  37.4 us (6%)
    all_to_all x6, waiting for transfers between devices, across(): lax.all_to_all(blocks, 'dp', 0, 0, axis_index_groups=same_part, tiled=True)  217 us
    pallas_call x1, Pallas kernels, expert_pass(): pl.pallas_call(functools.partial(expert_kernel, split), out_shape=(jax.Sh...  61.1 us
    dot_general x8, matrix products, dot_tn(): lax.dot_general(left, right, (((0,), (0,)), ((), ())), preferred_element_...  54.4 us
    pallas_call x1, Pallas kernels, attend_back(): pl.pallas_call(attend_back_kernel, out_shape=jax.ShapeDtypeStruct((3, cou...  38.9 us
    all_to_all x6, starting transfers between devices, across(): lax.all_to_all(blocks, 'dp', 0, 0, axis_index_groups=same_part, tiled=True)  36.4 us
    pallas_call x1, Pallas kernels, attend(): pl.pallas_call(attend_kernel, out_shape=(jax.ShapeDtypeStruct((count, wid...  23.5 us
    concatenate x1, local copies, waits for them, and re-layouts, shards(): late = reduce_rows(jnp.concatenate([qkv_term, late_extra], axis=1))  13.9 us
    pallas_call x1, Pallas kernels, input_back(): pl.pallas_call(input_kernel, out_shape=(jax.ShapeDtypeStruct((count, widt...  13.1 us
  transfers between devices with their start and end apart: 12, of which 9 were waited for; matrix products, arithmetic and copies ran while one was open for 20% of the time, Pallas kernels for 13%

profile of v1, /device:TPU:12, one launch (start us, length us, event | category | flops | bytes accessed | tf_op | source)
XLA Modules:
  0.0 600.3 jit_solution(13427190654543679381)
XLA Ops:
  1.3 2.1 fusion.1
  6.2 9.6 %convolution_convert_fusion.q_ref.k_ref.v_ref = bf16[1024,3072]{1,0:T(8,128)(2,1)S(1)} fusion(bf16[1024,3072]{1,0:T(8,128)(2,1)} %w_ref.1, bf16[1024,1024]{1,0:T(8,128)(2,1)} %tok_ref.3, f32[1024]{0:T(1024)} %param.17, f32[1024]{0:T(1024)S(1)} %add_rsqrt_fusion), kind=kOutput, calls=%fused_computation.7 | convolution fusion | flops 6449790976 | bytes 14688256 | tf_op jit(solution)/shard_map/dot_general | solution.py:621
  15.8 23.5 %attend.1 = (bf16[1024,1024]{1,0:T(8,128)(2,1)S(1)}, f32[8,8,1024]{2,1,0:T(8,128)S(1)}) custom-call(bf16[1024,3072]{1,0:T(8,128)(2,1)S(1)} %convolution_convert_fusion.q_ref.k_ref.v_ref, bf16[1024,3072]{1,0:T(8,128)(2,1)S(1)} %convolution_convert_fusion.q_ref.k_ref.v_ref, bf16[1024,3072]{1,0:T(8,128)(2,1)S(1)} %convolution_convert_fusion.q_ref.k_ref.v_ref), custom_call_target="tpu_custom_call" | custom-call | flops 8589934592 | bytes 8388608 | tf_op jit(solution)/shard_map/attend/pallas_call | solution.py:183
  41.4 4.8 middle.1
  46.3 3.7 dispatch.1
  51.5 7.2 %all-to-all-start = ((bf16[16,80,1024]{2,1,0:T(8,128)(2,1)}), bf16[16,80,1024]{2,1,0:T(8,128)(2,1)}, u32[]{:S(2)}, u32[]{:S(2)}) async-start(bf16[16,80,1024]{2,1,0:T(8,128)(2,1)} %bitcast.55), calls=%async_computation | async-start | bytes 5242880 | tf_op jit(solution)/shard_map/all_to_all | solution.py:580
  60.2 4.0 dispatch_grad.1
  65.8 52.1 %all-to-all-done = bf16[16,80,1024]{2,1,0:T(8,128)(2,1)} async-done(((bf16[16,80,1024]{2,1,0:T(8,128)(2,1)}), bf16[16,80,1024]{2,1,0:T(8,128)(2,1)}, u32[]{:S(2)}, u32[]{:S(2)}) %all-to-all-start) | async-done | bytes 2621472 | tf_op jit(solution)/shard_map/all_to_all | solution.py:580
  117.9 5.5 all-to-all-start.1
  123.5 65.4 %all-to-all-done.1 = bf16[16,80,1152]{2,1,0:T(8,128)(2,1)} async-done(((bf16[16,80,1152]{2,1,0:T(8,128)(2,1)}), bf16[16,80,1152]{2,1,0:T(8,128)(2,1)}, u32[]{:S(2)}, u32[]{:S(2)}) %all-to-all-start.1) | async-done | bytes 2949152 | tf_op jit(solution)/shard_map/all_to_all | solution.py:580
  189.0 5.5 pad_maximum_fusion.2.x_ref
  194.5 4.8 pad_maximum_fusion.1.g_ref
  199.3 61.1 %experts.1 = (bf16[2560,1408]{1,0:T(8,128)(2,1)}, bf16[2560,1408]{1,0:T(8,128)(2,1)}, bf16[2560,1408]{1,0:T(8,128)(2,1)}, bf16[2560,1024]{1,0:T(8,128)(2,1)}, bf...) custom-call(bf16[2560,1024]{1,0:T(8,128)(2,1)} %pad_maximum_fusion.2.x_ref, ...), custom_call_target="tpu_custom_call" | custom-call | flops 44291850240 | bytes 47841280 | tf_op jit(solution)/shard_map/experts/pallas_call | solution.py:364
  260.4 2.2 slice.43
  263.1 5.0 collective-permute-done.3
  268.1 2.4 add_convert_fusion
  270.5 4.9 all-to-all-start.3
  275.4 3.5 slice.41
  278.9 5.2 collective-permute-done.2
  284.1 5.3 add_convert_fusion.1
  289.4 53.4 %all-to-all-done.3 = bf16[16,80,1152]{2,1,0:T(8,128)(2,1)} async-done(((bf16[16,80,1152]{2,1,0:T(8,128)(2,1)}), bf16[16,80,1152]{2,1,0:T(8,128)(2,1)}, u32[]{:S(2)}, u32[]{:S(2)}) %all-to-all-start.3) | async-done | bytes 2949152 | tf_op jit(solution)/shard_map/all_to_all | solution.py:580
  342.7 6.4 %all-to-all-start.2 = ((bf16[16,80,1024]{2,1,0:T(8,128)(2,1)}), bf16[16,80,1024]{2,1,0:T(8,128)(2,1)}, u32[]{:S(2)}, u32[]{:S(2)}) async-start(bf16[16,80,1024]{2,1,0:T(8,128)(2,1)} %bitcast.65), calls=%async_computation.2 | async-start | bytes 5242880 | tf_op jit(solution)/shard_map/all_to_all | solution.py:580
  350.8 12.1 %state_back.1 = (f32[1024,1024]{1,0:T(8,128)}, bf16[1024,1024]{1,0:T(8,128)(2,1)S(1)}, bf16[1024,128]{1,0:T(8,128)(2,1)S(1)}, f32[8,1024]{1,0:T(8,128)S(1)}) custom-call(s32[1024,128]{1,0:T(8,128)S(1)} %copy-done.12, f32[1024,128]{1,0:T(8,128)S(1)} %copy-done.14, bf16[1280,1152]{1,0:T(8,128)(2,1)} %bitcast.12.din_ref, f32[1024,1024]{1,0:T(8,128)} %copy-done, ...), custom_call_target="tpu_custom_call" | custom-call | flops 2684354560 | bytes 14680064 | tf_op jit(solution)/shard_map/state_back/pallas_call | solution.py:444
  363.0 2.4 convolution_convert_fusion.1.do_ref
  365.4 38.9 %attend_back.1.d_ref = bf16[3,1024,1024]{2,1,0:T(8,128)(2,1)S(1)} custom-call(bf16[1024,3072]{1,0:T(8,128)(2,1)} %copy-done.28, bf16[1024,3072]{1,0:T(8,128)(2,1)} %copy-done.28, bf16[1024,3072]{1,0:T(8,128)(2,1)} %copy-done.28, bf16[1024,1024]{1,0:T(8,128)(2,1)S(1)} %copy-done.25, bf16[1024,1024]{1,0:T(8,128)(2,1)S(1)} %convolution_convert_fusion.1.do_ref, ...), custom_call_target="tpu_custom_call" | custom-call | flops 21474836480 | bytes 16777216 | tf_op jit(solution)/shard_map/attend_back/pallas_call | solution.py:244
  404.3 4.5 fusion.6
  408.9 4.5 fusion.7
  413.4 4.6 fusion.8
  419.6 13.1 %input_back.1 = (f32[1024,1024]{1,0:T(8,128)}, f32[8,1024]{1,0:T(8,128)S(1)}) custom-call(bf16[3,1024,1024]{2,1,0:T(8,128)(2,1)} %copy-done.27, bf16[1024,3072]{1,0:T(8,128)(2,1)} %w_ref.1, bf16[1024,1024]{1,0:T(8,128)(2,1)S(1)} %copy-done.8, f32[1,1024]{1,0:T(1,128)S(1)} %bitcast.59, f32[1024,1024]{1,0:T(8,128)} %get-tuple-element.39.dstate_ref), custom_call_target="tpu_custom_call" | custom-call | flops 6442450944 | bytes 23068672 | tf_op jit(solution)/shard_map/input_back/pallas_call | solution.py:531
  432.9 9.6 %pad_maximum_fusion = f32[1024,3200]{0,1:T(8,128)} fusion(f32[1024,128]{0,1:T(8,128)S(1)} %broadcast_select_fusion, f32[1024,1024]{0,1:T(8,128)} %fusion.6, f32[1024,1024]{0,1:T(8,128)} %fusion.7, f32[1024,1024]{0,1:T(8,128)} %fusion.8), kind=kLoop, calls=%fused_computation | loop fusion | flops 9830400 | bytes 26214400 | tf_op jit(solution)/shard_map/concatenate | solution.py:648
  442.5 13.9 %copy.41 = f32[1024,3200]{1,0:T(8,128)} copy(f32[1024,3200]{0,1:T(8,128)} %pad_maximum_fusion) | data formatting | bytes 26214400 | tf_op jit(solution)/shard_map/concatenate | solution.py:648
  456.4 5.1 fusion.4
  462.0 2.5 fusion.14
  464.5 2.8 pad_maximum_fusion.3
  467.3 6.0 %copy.42 = f32[1024,1152]{1,0:T(8,128)} copy(f32[1024,1152]{0,1:T(8,128)} %pad_maximum_fusion.3) | data formatting | bytes 9437184 | tf_op jit(solution)/shard_map/concatenate | solution.py:646
  473.3 2.8 fusion.9
  476.7 2.7 collective-permute-done.5
  479.3 2.9 fusion.5
  482.3 6.9 %all-to-all-start.5 = ((bf16[16,32,1152]{2,1,0:T(8,128)(2,1)}), bf16[16,32,1152]{2,1,0:T(8,128)(2,1)S(1)}, u32[]{:S(2)}, u32[]{:S(2)}) async-start(bf16[16,32,1152]{2,1,0:T(8,128)(2,1)} %fusion.5), calls=%async_computation.5 | async-start | bytes 2359296 | tf_op jit(solution)/shard_map/all_to_all | solution.py:580
  489.2 6.2 %fusion = bf16[16,32,3200]{2,1,0:T(8,128)(2,1)} fusion(bf16[16,32,3200]{2,1,0:T(8,128)(2,1)} %collective-permute-done.4, f32[16,2,32,3200]{3,2,1,0:T(8,128)} %bitcast.61, s32[]{:T(128)S(6)} %select_n.19), kind=kLoop, calls=%fused_computation.2 | loop fusion | flops 4915200 | bytes 13107204 | tf_op jit(solution)/shard_map/convert_element_type | solution.py:607
  495.4 22.6 %all-to-all-done.5 = bf16[16,32,1152]{2,1,0:T(8,128)(2,1)S(1)} async-done(((bf16[16,32,1152]{2,1,0:T(8,128)(2,1)}), bf16[16,32,1152]{2,1,0:T(8,128)(2,1)S(1)}, u32[]{:S(2)}, u32[]{:S(2)}) %all-to-all-start.5) | async-done | bytes 1179680 | tf_op jit(solution)/shard_map/all_to_all | solution.py:580
  518.0 5.4 all-to-all-start.4
  523.4 14.1 %convolution_bitcast_fusion.2 = f32[1,1024,1408]{2,1,0:T(8,128)} fusion(bf16[2560,1408]{1,0:T(8,128)(2,1)} %get-tuple-element.44, bf16[1280,1024]{1,0:T(8,128)(2,1)} %collective-permute-done, bf16[1280,1024]{1,0:T(8,128)(2,1)} %bitcast.3), kind=kOutput, calls=%fused_computation.15 | convolution fusion | flops 7392460800 | bytes 18219008 | tf_op jit(solution)/shard_map/dot_general | solution.py:32
  537.6 14.1 %convolution_bitcast_fusion.1 = f32[1,1024,1408]{2,1,0:T(8,128)} fusion(bf16[2560,1408]{1,0:T(8,128)(2,1)} %get-tuple-element.45, bf16[1280,1024]{1,0:T(8,128)(2,1)} %collective-permute-done, bf16[1280,1024]{1,0:T(8,128)(2,1)} %bitcast.3), kind=kOutput, calls=%fused_computation.14 | convolution fusion | flops 7392460800 | bytes 18219008 | tf_op jit(solution)/shard_map/dot_general | solution.py:32
  551.8 9.5 %convolution_bitcast_fusion = f32[1,1408,1024]{2,1,0:T(8,128)} fusion(bf16[2560,1408]{1,0:T(8,128)(2,1)S(1)} %bitcast.70, bf16[2560,1024]{1,0:T(8,128)(2,1)S(1)} %bitcast.72), kind=kOutput, calls=%fused_computation.13 | convolution fusion | flops 7381975040 | bytes 18219008 | tf_op jit(solution)/shard_map/dot_general | solution.py:32
  561.3 8.9 %block_out.1 = bf16[1024,1024]{1,0:T(8,128)(2,1)} custom-call(s32[1024,128]{1,0:T(8,128)S(1)} %copy-done.12, f32[1024,128]{1,0:T(8,128)S(1)} %copy-done.14, bf16[1280,1024]{1,0:T(8,128)(2,1)} %bitcast.10.rows_ref, f32[1024,1024]{1,0:T(8,128)S(1)} %copy-done.1), custom_call_target="tpu_custom_call" | custom-call | flops 5368709120 | bytes 9437184 | tf_op jit(solution)/shard_map/block_out/pallas_call | solution.py:489
  572.4 23.7 %all-to-all-done.4 = bf16[16,32,3200]{2,1,0:T(8,128)(2,1)} async-done(((bf16[16,32,3200]{2,1,0:T(8,128)(2,1)}), bf16[16,32,3200]{2,1,0:T(8,128)(2,1)}, u32[]{:S(2)}, u32[]{:S(2)}) %all-to-all-start.4) | async-done | bytes 3276832 | tf_op jit(solution)/shard_map/all_to_all | solution.py:580
  596.1 2.4 convert_reduce_fusion
  (103 shorter events, 18.2 us)
Async XLA Ops:
  15.7 23.5 %copy-start.28 = (bf16[1024,3072]{1,0:T(8,128)(2,1)}, bf16[1024,3072]{1,0:T(8,128)(2,1)S(1)}, u32[]{:S(2)}) copy-start(bf16[1024,3072]{1,0:T(8,128)(2,1)S(1)} %convolution_convert_fusion.q_ref.k_ref.v_ref) | copy-start | bytes 18874372
  15.7 23.6 %copy-start.17 = (s32[1,1024]{1,0:T(1,128)S(1)}, s32[1,1024]{1,0:T(1,128)}, u32[]{:S(2)}) copy-start(s32[1,1024]{1,0:T(1,128)} %rank_row_ref.1) | copy-start | bytes 12292
  15.8 25.6 %copy-start.6 = (bf16[1024,1024]{1,0:T(8,128)(2,1)S(1)}, bf16[1024,1024]{1,0:T(8,128)(2,1)}, u32[]{:S(2)}) copy-start(bf16[1024,1024]{1,0:T(8,128)(2,1)} %tok_ref.3) | copy-start | bytes 6291460
  15.8 25.6 %copy-start.18 = (f32[1024]{0:T(1024)S(1)}, f32[1024]{0:T(1024)}, u32[]{:S(2)}) copy-start(f32[1024]{0:T(1024)} %param.20) | copy-start | bytes 12292
  15.8 25.6 %copy-start.19 = (bf16[1024,1024]{1,0:T(8,128)(2,1)S(1)}, bf16[1024,1024]{1,0:T(8,128)(2,1)}, u32[]{:S(2)}) copy-start(bf16[1024,1024]{1,0:T(8,128)(2,1)} %w_out_ref.1) | copy-start | bytes 6291460
  39.3 7.0 %copy-start.24 = (bf16[1024,1024]{1,0:T(8,128)(2,1)}, bf16[1024,1024]{1,0:T(8,128)(2,1)S(1)}, u32[]{:S(2)}) copy-start(bf16[1024,1024]{1,0:T(8,128)(2,1)S(1)} %get-tuple-element.30.mixed_ref.o_ref) | copy-start | bytes 6291460
  39.3 7.0 %copy-start.29 = (f32[8,8,1024]{2,1,0:T(8,128)}, f32[8,8,1024]{2,1,0:T(8,128)S(1)}, u32[]{:S(2)}) copy-start(f32[8,8,1024]{2,1,0:T(8,128)S(1)} %get-tuple-element.38.lse_ref) | copy-start | bytes 786436
  39.4 6.9 %copy-start.9 = (bf16[1024,128]{1,0:T(8,128)(2,1)}, bf16[1024,128]{1,0:T(8,128)(2,1)S(1)}, u32[]{:S(2)}) copy-start(bf16[1024,128]{1,0:T(8,128)(2,1)S(1)} %pad.4.wr_ref) | copy-start | bytes 786436
  41.4 8.6 %copy-start.11 = (s32[1024,128]{1,0:T(8,128)}, s32[1024,128]{1,0:T(8,128)S(1)}, u32[]{:S(2)}) copy-start(s32[1024,128]{1,0:T(8,128)S(1)} %get-tuple-element.29.col_ref) | copy-start | bytes 1572868
  46.3 3.7 copy-start
  46.3 3.7 copy-start.13
  50.0 1.5 copy-start.3
  51.5 66.4 %all-to-all-start = ((bf16[16,80,1024]{2,1,0:T(8,128)(2,1)}), bf16[16,80,1024]{2,1,0:T(8,128)(2,1)}, u32[]{:S(2)}, u32[]{:S(2)}) async-start(bf16[16,80,1024]{2,1,0:T(8,128)(2,1)} %bitcast.55), calls=%async_computation | async-start | bytes 5242880 | tf_op jit(solution)/shard_map/all_to_all | solution.py:580
  58.6 1.6 copy-start.4
  64.2 1.6 copy-start.2
  117.9 71.0 %all-to-all-start.1 = ((bf16[16,80,1152]{2,1,0:T(8,128)(2,1)}), bf16[16,80,1152]{2,1,0:T(8,128)(2,1)}, u32[]{:S(2)}, u32[]{:S(2)}) async-start(bf16[16,80,1152]{2,1,0:T(8,128)(2,1)} %bitcast.54), calls=%async_computation.1 | async-start | bytes 5898240 | tf_op jit(solution)/shard_map/all_to_all | solution.py:580
  123.4 65.5 %collective-permute-start = (bf16[1280,1024]{1,0:T(8,128)(2,1)}, bf16[1280,1024]{1,0:T(8,128)(2,1)}, u32[]{:S(2)}, u32[]{:S(2)}) collective-permute-start(bf16[1280,1024]{1,0:T(8,128)(2,1)} %bitcast.3), channel_id=1, source_target_pairs={{0,1},{1,0},{2,3},{3,2},{4,5},{5,4},{6,7},{7,6},{8,9},{9,8},{10,11... | collective-permute-start | bytes 7864328 | tf_op jit(solution)/shard_map/ppermute | solution.py:584
  188.9 5.6 collective-permute-start.1
  260.4 7.7 %copy-start.31 = (bf16[2560,1152]{1,0:T(8,128)(2,1)S(1)}, bf16[2560,1152]{1,0:T(8,128)(2,1)}, u32[]{:S(2)}) copy-start(bf16[2560,1152]{1,0:T(8,128)(2,1)} %get-tuple-element.36) | copy-start | bytes 17694724
  262.6 5.5 collective-permute-start.3
  270.5 72.2 %all-to-all-start.3 = ((bf16[16,80,1152]{2,1,0:T(8,128)(2,1)}), bf16[16,80,1152]{2,1,0:T(8,128)(2,1)}, u32[]{:S(2)}, u32[]{:S(2)}) async-start(bf16[16,80,1152]{2,1,0:T(8,128)(2,1)} %bitcast.64), calls=%async_computation.3 | async-start | bytes 5898240 | tf_op jit(solution)/shard_map/all_to_all | solution.py:580
  278.8 5.3 collective-permute-start.2
  289.3 59.8 %copy-start.10 = (bf16[1024,128]{1,0:T(8,128)(2,1)S(1)}, bf16[1024,128]{1,0:T(8,128)(2,1)}, u32[]{:S(2)}) copy-start(bf16[1024,128]{1,0:T(8,128)(2,1)} %copy-done.9) | copy-start | bytes 786436
  289.3 59.8 %copy-start.12 = (s32[1024,128]{1,0:T(8,128)S(1)}, s32[1024,128]{1,0:T(8,128)}, u32[]{:S(2)}) copy-start(s32[1024,128]{1,0:T(8,128)} %copy-done.11) | copy-start | bytes 1572868
  289.3 59.9 %copy-start.14 = (f32[1024,128]{1,0:T(8,128)S(1)}, f32[1024,128]{1,0:T(8,128)}, u32[]{:S(2)}) copy-start(f32[1024,128]{1,0:T(8,128)} %copy-done.13) | copy-start | bytes 1572868
  342.7 139.5 %all-to-all-start.2 = ((bf16[16,80,1024]{2,1,0:T(8,128)(2,1)}), bf16[16,80,1024]{2,1,0:T(8,128)(2,1)}, u32[]{:S(2)}, u32[]{:S(2)}) async-start(bf16[16,80,1024]{2,1,0:T(8,128)(2,1)} %bitcast.65), calls=%async_computation.2 | async-start | bytes 5242880 | tf_op jit(solution)/shard_map/all_to_all | solution.py:580
  349.2 1.6 copy-start.5
  350.8 12.1 %copy-start.20 = (bf16[1024,1024]{1,0:T(8,128)(2,1)S(1)}, bf16[1024,1024]{1,0:T(8,128)(2,1)}, u32[]{:S(2)}) copy-start(bf16[1024,1024]{1,0:T(8,128)(2,1)} %w_out_ref.1) | copy-start | bytes 6291460
  362.9 2.4 copy-start.15
  362.9 2.4 copy-start.21
  363.0 2.4 copy-start.25
  363.0 2.4 copy-start.30
  365.4 38.9 %copy-start.7 = (bf16[1024,1024]{1,0:T(8,128)(2,1)S(1)}, bf16[1024,1024]{1,0:T(8,128)(2,1)}, u32[]{:S(2)}) copy-start(bf16[1024,1024]{1,0:T(8,128)(2,1)} %tok_ref.3) | copy-start | bytes 6291460
  365.4 38.9 %copy-start.23 = (f32[1024]{0:T(1024)S(1)}, f32[1024]{0:T(1024)}, u32[]{:S(2)}) copy-start(f32[1024]{0:T(1024)} %param.17) | copy-start | bytes 12292
  404.3 9.1 %copy-start.27 = (bf16[3,1024,1024]{2,1,0:T(8,128)(2,1)}, bf16[3,1024,1024]{2,1,0:T(8,128)(2,1)S(1)}, u32[]{:S(2)}) copy-start(bf16[3,1024,1024]{2,1,0:T(8,128)(2,1)S(1)} %attend_back.1.d_ref) | copy-start | bytes 18874372
  418.0 1.6 copy-start.8
  456.4 5.1 copy-start.16
  456.4 5.6 copy-start.22
  456.4 5.6 copy-start.26
  461.5 27.7 %collective-permute-start.4 = (bf16[16,32,3200]{2,1,0:T(8,128)(2,1)}, bf16[16,32,3200]{2,1,0:T(8,128)(2,1)}, u32[]{:S(2)}, u32[]{:S(2)}) collective-permute-start(bf16[16,32,3200]{2,1,0:T(8,128)(2,1)} %fusion.4), channel_id=1, source_target_pairs={{0,1},{1,0},{2,3},{3,2},{4,5},{5,4},{6,7},{7,6},{8,9},{9,8},{10,11... | collective-permute-start | bytes 9830408 | tf_op jit(solution)/shard_map/ppermute | solution.py:606
  476.2 3.2 collective-permute-start.5
  482.3 35.7 %all-to-all-start.5 = ((bf16[16,32,1152]{2,1,0:T(8,128)(2,1)}), bf16[16,32,1152]{2,1,0:T(8,128)(2,1)S(1)}, u32[]{:S(2)}, u32[]{:S(2)}) async-start(bf16[16,32,1152]{2,1,0:T(8,128)(2,1)} %fusion.5), calls=%async_computation.5 | async-start | bytes 2359296 | tf_op jit(solution)/shard_map/all_to_all | solution.py:580
  518.0 78.1 %all-to-all-start.4 = ((bf16[16,32,3200]{2,1,0:T(8,128)(2,1)}), bf16[16,32,3200]{2,1,0:T(8,128)(2,1)}, u32[]{:S(2)}, u32[]{:S(2)}) async-start(bf16[16,32,3200]{2,1,0:T(8,128)(2,1)} %fusion), calls=%async_computation.4 | async-start | bytes 6553600 | tf_op jit(solution)/shard_map/all_to_all | solution.py:580
  523.4 28.3 %slice-start = ((s8[7208960]{0:T(1024)(128)(4,1)}), s8[4194304]{0:T(1024)(128)(4,1)S(1)}, s32[]{:S(2)}) async-start(s8[7208960]{0:T(1024)(128)(4,1)} %bitcast.69), calls=%async_computation.6 | async-start | bytes 8388608
  523.4 28.3 %slice-start.2 = ((s8[5242880]{0:T(1024)(128)(4,1)}), s8[4194304]{0:T(1024)(128)(4,1)S(1)}, s32[]{:S(2)}) async-start(s8[5242880]{0:T(1024)(128)(4,1)} %bitcast.71), calls=%async_computation.8 | async-start | bytes 8388608
  537.6 14.2 %slice-start.1 = ((s8[7208960]{0:T(1024)(128)(4,1)}), s8[3014656]{0:T(1024)(128)(4,1)S(1)}, s32[]{:S(2)}) async-start(s8[7208960]{0:T(1024)(128)(4,1)} %bitcast.69), calls=%async_computation.7 | async-start | bytes 6029312
  537.6 14.2 %slice-start.3 = ((s8[5242880]{0:T(1024)(128)(4,1)}), s8[1048576]{0:T(1024)(128)(4,1)S(1)}, s32[]{:S(2)}) async-start(s8[5242880]{0:T(1024)(128)(4,1)} %bitcast.71), calls=%async_computation.9 | async-start | bytes 2097152
  551.8 9.5 %copy-start.1 = (f32[1024,1024]{1,0:T(8,128)S(1)}, f32[1024,1024]{1,0:T(8,128)}, u32[]{:S(2)}) copy-start(f32[1024,1024]{1,0:T(8,128)} %copy-done) | copy-start | bytes 12582916

commit v2 on v1

--- a/solution.py
+++ b/solution.py
@@ -148,6 +148,83 @@
     )(row, data)
 
 
+MESH = pl.DeviceIdType.MESH
+
+
+def flip(chip, bits, experts):
+    out, b = chip, 1
+    while b < experts:
+        if isinstance(bits, int):
+            out = out + (bits // b % 2) * (b - 2 * b * lax.rem(lax.div(chip, b), 2))
+        else:
+            mine, theirs = lax.rem(lax.div(chip, b), 2), lax.rem(lax.div(bits, b), 2)
+            out = out + b * theirs * (1 - 2 * mine)
+        b *= 2
+    return out
+
+
+def greet(peers):
+    barrier = pltpu.get_barrier_semaphore()
+    for peer in peers:
+        pl.semaphore_signal(barrier, inc=1, device_id=(peer,), device_id_type=MESH)
+    pl.semaphore_wait(barrier, len(peers))
+
+
+def exchange_copies(src, dst, send_sem, recv_sem, local_sem):
+    experts = src.shape[0]
+    me = lax.axis_index("dp")
+    chip, core = lax.div(me, 2), lax.rem(me, 2)
+    copies = [pltpu.make_async_copy(src.at[chip], dst.at[chip], local_sem)]
+    peers = []
+    half = experts // 2
+    for place in range(1, experts):
+        step = half + place // 2 if place % 2 else place // 2
+        peer = flip(chip, step, experts)
+        peers.append(2 * peer + core)
+        copies.append(
+            pltpu.make_async_remote_copy(
+                src_ref=src.at[peer],
+                dst_ref=dst.at[chip],
+                send_sem=send_sem.at[step],
+                recv_sem=recv_sem.at[step],
+                device_id=(2 * peer + core,),
+                device_id_type=MESH,
+            )
+        )
+    return peers, copies
+
+
+def exchange_sems(experts):
+    return [
+        pltpu.SemaphoreType.DMA((experts,)),
+        pltpu.SemaphoreType.DMA((experts,)),
+        pltpu.SemaphoreType.DMA,
+    ]
+
+
+def riding(body, n_in, n_out):
+    def kernel(*refs):
+        ins, src = refs[:n_in], refs[n_in]
+        outs, dst = refs[n_in + 1 : n_in + 1 + n_out], refs[n_in + 1 + n_out]
+        rest, sems = refs[n_in + n_out + 2 : -3], refs[-3:]
+        peers, copies = exchange_copies(src, dst, *sems)
+
+        @pl.when(pl.program_id(0) == 0)
+        def _():
+            greet(peers)
+            for copy in copies:
+                copy.start()
+
+        body(*ins, *outs, *rest)
+
+        @pl.when(pl.program_id(0) == pl.num_programs(0) - 1)
+        def _():
+            for copy in copies:
+                copy.wait()
+
+    return kernel
+
+
 SCALE2 = math.log2(math.e) / math.sqrt(HEAD_DIM)
 QB = 256
 
@@ -176,30 +253,43 @@
         lse_ref[0, :, start:stop] = jnp.transpose(norm)[0:8, :]
 
 
-def attend(qkv):
+def attend(qkv, blocks=None):
     count, width3 = qkv.shape
     width = width3 // 3
     pairs = width // LANES
+    in_specs = [
+        pl.BlockSpec((count, LANES), lambda i: (0, i)),
+        pl.BlockSpec((count, LANES), lambda i: (0, i + pairs)),
+        pl.BlockSpec((count, LANES), lambda i: (0, i + 2 * pairs)),
+    ]
+    out_specs = [
+        pl.BlockSpec((count, LANES), lambda i: (0, i)),
+        pl.BlockSpec((1, 8, count), lambda i: (i, 0, 0)),
+    ]
+    out_shape = [
+        jax.ShapeDtypeStruct((count, width), bf16),
+        jax.ShapeDtypeStruct((pairs, 8, count), f32),
+    ]
+    body, args, scratch, extra = attend_kernel, [qkv, qkv, qkv], [], {}
+    if blocks is not None:
+        body = riding(attend_kernel, len(in_specs), len(out_specs))
+        in_specs.append(pl.BlockSpec(memory_space=pl.ANY))
+        out_specs.append(pl.BlockSpec(memory_space=pl.ANY))
+        out_shape.append(jax.ShapeDtypeStruct(blocks.shape, blocks.dtype))
+        args.append(blocks)
+        scratch = exchange_sems(blocks.shape[0])
+        extra = dict(collective_id=0, has_side_effects=True)
     return pl.pallas_call(
-        attend_kernel,
-        out_shape=(
-            jax.ShapeDtypeStruct((count, width), bf16),
-            jax.ShapeDtypeStruct((pairs, 8, count), f32),
-        ),
+        body,
+        out_shape=out_shape,
         grid=(pairs,),
-        in_specs=[
-            pl.BlockSpec((count, LANES), lambda i: (0, i)),
-            pl.BlockSpec((count, LANES), lambda i: (0, i + pairs)),
-            pl.BlockSpec((count, LANES), lambda i: (0, i + 2 * pairs)),
-        ],
-        out_specs=(
-            pl.BlockSpec((count, LANES), lambda i: (0, i)),
-            pl.BlockSpec((1, 8, count), lambda i: (i, 0, 0)),
-        ),
-        compiler_params=params(40),
+        in_specs=in_specs,
+        out_specs=out_specs,
+        scratch_shapes=scratch,
+        compiler_params=params(40, **extra),
         cost_estimate=cost(2 * 4 * count * count * width, 8 * count * width, 8 * count * count),
         name="attend",
-    )(qkv, qkv, qkv)
+    )(*args)
 
 
 def attend_back_kernel(q_ref, k_ref, v_ref, o_ref, do_ref, lse_ref, out_ref, dk_sc, dv_sc):
@@ -238,27 +328,40 @@
     out_ref[2, :, :] = dv_sc[...].astype(bf16)
 
 
-def attend_back(qkv, mixed, d_mixed, lse):
+def attend_back(qkv, mixed, d_mixed, lse, blocks=None):
     count, width = mixed.shape
     pairs = width // LANES
+    in_specs = [
+        pl.BlockSpec((count, LANES), lambda i: (0, i)),
+        pl.BlockSpec((count, LANES), lambda i: (0, i + pairs)),
+        pl.BlockSpec((count, LANES), lambda i: (0, i + 2 * pairs)),
+        pl.BlockSpec((count, LANES), lambda i: (0, i)),
+        pl.BlockSpec((count, LANES), lambda i: (0, i)),
+        pl.BlockSpec((1, 8, count), lambda i: (i, 0, 0)),
+    ]
+    out_specs = [pl.BlockSpec((3, count, LANES), lambda i: (0, 0, i))]
+    out_shape = [jax.ShapeDtypeStruct((3, count, width), bf16)]
+    body, args, extra = attend_back_kernel, [qkv, qkv, qkv, mixed, d_mixed, lse], {}
+    scratch = [pltpu.VMEM((count, LANES), f32), pltpu.VMEM((count, LANES), f32)]
+    if blocks is not None:
+        body = riding(attend_back_kernel, len(in_specs), len(out_specs))
+        in_specs.append(pl.BlockSpec(memory_space=pl.ANY))
+        out_specs.append(pl.BlockSpec(memory_space=pl.ANY))
+        out_shape.append(jax.ShapeDtypeStruct(blocks.shape, blocks.dtype))
+        args.append(blocks)
+        scratch = scratch + exchange_sems(blocks.shape[0])
+        extra = dict(collective_id=1, has_side_effects=True)
     return pl.pallas_call(
-        attend_back_kernel,
-        out_shape=jax.ShapeDtypeStruct((3, count, width), bf16),
+        body,
+        out_shape=out_shape,
         grid=(pairs,),
-        in_specs=[
-            pl.BlockSpec((count, LANES), lambda i: (0, i)),
-            pl.BlockSpec((count, LANES), lambda i: (0, i + pairs)),
-            pl.BlockSpec((count, LANES), lambda i: (0, i + 2 * pairs)),
-            pl.BlockSpec((count, LANES), lambda i: (0, i)),
-            pl.BlockSpec((count, LANES), lambda i: (0, i)),
-            pl.BlockSpec((1, 8, count), lambda i: (i, 0, 0)),
-        ],
-        out_specs=pl.BlockSpec((3, count, LANES), lambda i: (0, 0, i)),
-        scratch_shapes=[pltpu.VMEM((count, LANES), f32), pltpu.VMEM((count, LANES), f32)],
-        compiler_params=params(40),
+        in_specs=in_specs,
+        out_specs=out_specs,
+        scratch_shapes=scratch,
+        compiler_params=params(40, **extra),
         cost_estimate=cost(5 * 4 * count * count * width, 16 * count * width, 8 * count * count),
         name="attend_back",
-    )(qkv, qkv, qkv, mixed, d_mixed, lse)
+    )(*args)
 
 
 def middle_kernel(experts, mixed_ref, w_out_ref, tok_ref, gain_ref, wr_ref, col_ref, h_ref, low_ref, gate_ref):
@@ -394,6 +497,293 @@
     )(x, g, wg, wu, wd, wr)
 
 
+def expert_exchange_kernel(
+    group, x_ref, g_ref, wg_hbm, wu_hbm, wd_hbm, wr_ref,
+    act_ref, dgp_ref, dup_ref, de_ref, xs_ref, slot_ref, back_ref,
+    xb, gb, ds, rd, pd, sp, rp, pp, st_act, st_dgp, st_dup, st_de, wg_ref, wu_ref, wd_ref,
+    w_sem, x_send, x_recv, f_send, f_recv, g_own, g_send, g_recv,
+    d_send, d_recv, p_send, p_recv, b_send, b_recv, o_sem, s_sem, l_sem,
+):
+    experts, capacity, width = x_ref.shape
+    steps = experts // group
+    pair = 2 * capacity
+    half = experts // 2
+    me = lax.axis_index("dp")
+    chip, core = lax.div(me, 2), lax.rem(me, 2)
+    mate = 2 * chip + 1 - core
+
+    def bits(place):
+        if isinstance(place, int):
+            return half + place // 2 if place % 2 else place // 2
+        odd = lax.rem(place, 2)
+        return odd * half + lax.div(place, 2)
+
+    def chip_at(place):
+        return flip(chip, bits(place), experts)
+
+    def remote(src, dst, send, recv, device):
+        return pltpu.make_async_remote_copy(
+            src_ref=src, dst_ref=dst, send_sem=send, recv_sem=recv, device_id=(device,), device_id_type=MESH
+        )
+
+    def own(buf, q, g):
+        return buf.at[q, g * pair : g * pair + capacity]
+
+    def theirs(buf, q, g):
+        return buf.at[q, g * pair + capacity : (g + 1) * pair]
+
+    def x_copy(place):
+        q, g = place // group, place % group
+        peer = chip_at(place)
+        return remote(x_ref.at[peer], own(xb, q, g), x_send.at[place], x_recv.at[place], 2 * peer + core)
+
+    def x_arrival(q, g):
+        place = q * group + g
+        return remote(x_ref.at[chip], own(xb, q, g), x_send.at[place], x_recv.at[place], mate)
+
+    def forward(q, g):
+        place = q * group + g
+        return remote(own(xb, q, g), theirs(xb, q, g), f_send.at[place], f_recv.at[place], mate)
+
+    def g_mine(q, g):
+        place = q * group + g
+        return pltpu.make_async_copy(g_ref.at[chip_at(place)], own(gb, q, g), g_own.at[place])
+
+    def g_mate(q, g):
+        place = q * group + g
+        return remote(g_ref.at[chip_at(place)], theirs(gb, q, g), g_send.at[place], g_recv.at[place], mate)
+
+    def d_copy(q, g):
+        place = q * group + g
+        return remote(pd.at[lax.rem(q, 2), g], rd.at[place], d_send.at[place], d_recv.at[place], mate)
+
+    def p_copy(q, g):
+        place = q * group + g
+        return remote(pp.at[lax.rem(q, 2), g], rp.at[place], p_send.at[place], p_recv.at[place], mate)
+
+    def back_copy(q, g):
+        place = q * group + g
+        return remote(ds.at[place], back_ref.at[chip], b_send.at[place], b_recv.at[place], 2 * chip_at(place) + core)
+
+    def slot_copy(q, g):
+        place = q * group + g
+        return pltpu.make_async_copy(sp.at[place], slot_ref.at[chip_at(place)], s_sem.at[place])
+
+    def stage_copies(q):
+        slot = lax.rem(q, 2)
+        return (
+            pltpu.make_async_copy(st_act.at[slot], act_ref.at[q], o_sem.at[slot, 0]),
+            pltpu.make_async_copy(st_dgp.at[slot], dgp_ref.at[q], o_sem.at[slot, 1]),
+            pltpu.make_async_copy(st_dup.at[slot], dup_ref.at[q], o_sem.at[slot, 2]),
+            pltpu.make_async_copy(st_de.at[slot], de_ref.at[q], o_sem.at[slot, 3]),
+        )
+
+    def xs_copy(q):
+        return pltpu.make_async_copy(xb.at[q], xs_ref.at[q], l_sem.at[1 + q])
+
+    weights = [
+        pltpu.make_async_copy(src, dst, w_sem.at[i])
+        for i, (src, dst) in enumerate(((wg_hbm, wg_ref), (wu_hbm, wu_ref), (wd_hbm, wd_ref)))
+    ]
+    self_x = pltpu.make_async_copy(x_ref.at[chip], own(xb, 0, 0), l_sem.at[0])
+    self_back = pltpu.make_async_copy(ds.at[0], back_ref.at[chip], l_sem.at[1 + steps])
+
+    for copy in weights:
+        copy.start()
+    self_x.start()
+    greet([2 * chip_at(place) + core for place in range(1, experts)] + [mate])
+    for place in range(1, group):
+        x_copy(place).start()
+    for q in range(steps):
+        for g in range(group):
+            g_mine(q, g).start()
+            g_mate(q, g).start()
+        for g in range(group):
+            place = (q + 1) * group + g
+            if place < experts:
+                x_copy(place).start()
+    self_x.wait()
+    forward(0, 0).start()
+    for g in range(1, group):
+        x_arrival(0, g).wait_recv()
+        forward(0, g).start()
+    for copy in weights:
+        copy.wait()
+
+    def finish(q):
+        for g in range(group):
+            place = q * group + g
+            d_copy(q, g).wait_recv()
+            ds[place] = (ds[place].astype(f32) + rd[place].astype(f32)).astype(bf16)
+            if g == 0:
+
+                @pl.when(q == 0)
+                def _():
+                    self_back.start()
+
+                @pl.when(q > 0)
+                def _():
+                    back_copy(q, g).start()
+
+            else:
+                back_copy(q, g).start()
+        for g in range(group):
+            place = q * group + g
+            p_copy(q, g).wait_recv()
+            sp[place] = (sp[place].astype(f32) + rp[place].astype(f32)).astype(bf16)
+            slot_copy(q, g).start()
+
+    def step(q, carry):
+        for g in range(group):
+            g_mine(q, g).wait()
+            g_mate(q, g).wait_recv()
+            forward(q, g).wait_recv()
+        xs_copy(q).start()
+        x = xb[q]
+        rows = group * pair
+        lane = iota((rows, LANES), 1)
+        logits = dot_nn(x, wr_ref[...])
+        mine = jnp.sum(jnp.where(lane == chip, logits, 0.0), axis=1, keepdims=True)
+        other = gb[q, :, width:].astype(f32).astype(jnp.int32)
+        alt = jnp.sum(jnp.where(lane == other, logits, 0.0), axis=1, keepdims=True)
+        gate = 1.0 / (1.0 + jnp.exp(alt - mine))
+        d_rows = (gb[q, :, 0:width].astype(f32) * gate).astype(bf16)
+        pre = dot_nn(x, wg_ref[...])
+        up = dot_nn(x, wu_ref[...])
+        d_hidden = dot_nt(d_rows, wd_ref[...])
+        square = pre * pre
+        bent = jnp.tanh(GELU_C * pre * (1.0 + 0.044715 * square))
+        hill = 0.5 * (1.0 + bent)
+        gelu = pre * hill
+        slope = hill + 0.5 * pre * (1.0 - bent * bent) * (GELU_C * (1.0 + 3 * 0.044715 * square))
+        act = (gelu * up).astype(bf16)
+        dgp = (d_hidden * up * slope).astype(bf16)
+        dup = (d_hidden * gelu).astype(bf16)
+        pull = jnp.sum(act.astype(f32) * d_hidden, axis=1, keepdims=True)
+
+        @pl.when(q >= 2)
+        def _():
+            for copy in stage_copies(q - 2):
+                copy.wait()
+            for g in range(group):
+                d_copy(q - 2, g).wait_send()
+                p_copy(q - 2, g).wait_send()
+
+        slot = lax.rem(q, 2)
+        st_act[slot] = act
+        st_dgp[slot] = dgp
+        st_dup[slot] = dup
+        st_de[slot] = d_rows
+        for copy in stage_copies(q):
+            copy.start()
+
+        @pl.when(q + 1 < steps)
+        def _():
+            for g in range(group):
+                x_arrival(q + 1, g).wait_recv()
+                forward(q + 1, g).start()
+
+        @pl.when(q >= 1)
+        def _():
+            finish(q - 1)
+
+        d_in = (dot_nt(dgp, wg_ref[...]) + dot_nt(dup, wu_ref[...])).astype(bf16)
+        pull_high = pull.astype(bf16).astype(f32)
+        extra = jnp.where(lane == 2 * core, pull_high, 0.0)
+        extra = (extra + jnp.where(lane == 2 * core + 1, pull - pull_high, 0.0)).astype(bf16)
+        for g in range(group):
+            place = q * group + g
+            low, mid, high = g * pair, g * pair + capacity, (g + 1) * pair
+            ds[place, :, 0:width] = d_in[low:mid]
+            ds[place, :, width:] = extra[low:mid]
+            pd[slot, g, :, 0:width] = d_in[mid:high]
+            pd[slot, g, :, width:] = extra[mid:high]
+            d_copy(q, g).start()
+        partial = dot_nn(act, wd_ref[...]).astype(bf16)
+        for g in range(group):
+            place = q * group + g
+            low, mid, high = g * pair, g * pair + capacity, (g + 1) * pair
+            sp[place] = partial[low:mid]
+            pp[slot, g] = partial[mid:high]
+            p_copy(q, g).start()
+        return carry
+
+    lax.fori_loop(0, steps, step, 0)
+    finish(steps - 1)
+    for q in (steps - 2, steps - 1):
+        for copy in stage_copies(q):
+            copy.wait()
+        for g in range(group):
+            d_copy(q, g).wait_send()
+            p_copy(q, g).wait_send()
+    self_back.wait()
+    for q in range(steps):
+        xs_copy(q).wait()
+        for g in range(group):
+            place = q * group + g
+            slot_copy(q, g).wait()
+            forward(q, g).wait_send()
+            g_mate(q, g).wait_send()
+            if place:
+                x_copy(place).wait_send()
+                back_copy(q, g).wait()
+
+
+def expert_exchange(x, g, wg, wu, wd, wr):
+    experts, capacity, width = x.shape
+    ff = wg.shape[1]
+    group = 2
+    steps = experts // group
+    rows = 2 * capacity * group
+    wide = width + LANES
+    anywhere = pl.BlockSpec(memory_space=pl.ANY)
+    vmem, dma = pltpu.VMEM, pltpu.SemaphoreType.DMA
+    each = dma((experts,))
+    count = rows * steps
+    outs = pl.pallas_call(
+        functools.partial(expert_exchange_kernel, group),
+        out_shape=(
+            jax.ShapeDtypeStruct((steps, rows, ff), bf16),
+            jax.ShapeDtypeStruct((steps, rows, ff), bf16),
+            jax.ShapeDtypeStruct((steps, rows, ff), bf16),
+            jax.ShapeDtypeStruct((steps, rows, width), bf16),
+            jax.ShapeDtypeStruct((steps, rows, width), bf16),
+            jax.ShapeDtypeStruct((experts, capacity, width), bf16),
+            jax.ShapeDtypeStruct((experts, capacity, wide), bf16),
+        ),
+        in_specs=[anywhere] * 5 + [pl.BlockSpec(memory_space=vmem)],
+        out_specs=(anywhere,) * 7,
+        scratch_shapes=[
+            vmem((steps, rows, width), bf16),
+            vmem((steps, rows, wide), bf16),
+            vmem((experts, capacity, wide), bf16),
+            vmem((experts, capacity, wide), bf16),
+            vmem((2, group, capacity, wide), bf16),
+            vmem((experts, capacity, width), bf16),
+            vmem((experts, capacity, width), bf16),
+            vmem((2, group, capacity, width), bf16),
+            vmem((2, rows, ff), bf16),
+            vmem((2, rows, ff), bf16),
+            vmem((2, rows, ff), bf16),
+            vmem((2, rows, width), bf16),
+            vmem((width, ff), bf16),
+            vmem((width, ff), bf16),
+            vmem((ff, width), bf16),
+            dma((3,)),
+            each, each, each, each, each, each, each,
+            each, each, each, each, each, each,
+            dma((2, 4)),
+            each,
+            dma((2 + steps,)),
+        ],
+        compiler_params=params(60, collective_id=2, has_side_effects=True),
+        cost_estimate=cost(12 * count * width * ff, 2 * count * (3 * ff + 5 * width), count * ff),
+        name="experts",
+    )(x, g, wg, wu, wd, wr)
+    act, d_pre, d_up, d_rows, rows_in = (a.reshape(count, a.shape[-1]) for a in outs[:5])
+    return act, d_pre, d_up, d_rows, rows_in, outs[5], outs[6]
+
+
 def hot_rows(col, k, rows, slots):
     return jnp.where(iota((rows, slots), 1) == col[:, k : k + 1], 1.0, 0.0).astype(bf16)
 
@@ -613,21 +1003,33 @@
 
     wr = jnp.pad(w_router, ((0, 0), (0, LANES - experts)))
     col, row = make_slots(lengths, expert_ids, slot_order, experts, capacity)
-    grad_in = send_in(dispatch_grad(row, out_grad, slots))
+    direct = split == 2 and experts & (experts - 1) == 0 and experts >= 4
+    grad_out = dispatch_grad(row, out_grad, slots)
 
     token_vals = tokens.astype(f32)
     inverse_attn = lax.rsqrt(jnp.mean(token_vals * token_vals, axis=-1, keepdims=True) + epsilon)
     normed_low = (token_vals * inverse_attn * gain_attn).astype(bf16)
     qkv = jnp.dot(normed_low, w_qkv, preferred_element_type=f32).astype(bf16)
-    mixed, lse = attend(qkv)
+    if direct:
+        mixed, lse, grad_in = attend(qkv, grad_out.reshape(experts, capacity, -1))
+    else:
+        mixed, lse = attend(qkv)
+        grad_in = send_in(grad_out)
     hidden, moe_low, gates = middle(mixed, w_out, tokens, gain_moe, wr, col, experts)
 
-    rows_in = send_in(dispatch(row, moe_low, slots))
-    act, d_pre, d_up, d_rows, partial_out, d_in = expert_pass(
-        rows_in, grad_in, w_gate[0], w_up[0], w_down[0], wr, split
-    )
-    d_in_back = send_back(d_in)
-    slot_out = send_back(partial_out)
+    rows_out = dispatch(row, moe_low, slots)
+    if direct:
+        act, d_pre, d_up, d_rows, rows_in, slot_part, d_in_back = expert_exchange(
+            rows_out.reshape(experts, capacity, -1), grad_in, w_gate[0], w_up[0], w_down[0], wr
+        )
+        d_in_back = d_in_back.reshape(slots, -1)
+    else:
+        rows_in = send_in(rows_out)
+        act, d_pre, d_up, d_rows, partial_out, d_in = expert_pass(
+            rows_in, grad_in, w_gate[0], w_up[0], w_down[0], wr, split
+        )
+        d_in_back = send_back(d_in)
+        slot_out = send_back(partial_out)
 
     d_state, d_attn, d_log, gain_moe_rows = state_back(
         col, gates, d_in_back, hidden, out_grad, gain_moe, wr
@@ -636,7 +1038,11 @@
     router_term = dot_tn(moe_low, d_log)
     gain_moe_term = jnp.sum(gain_moe_rows, axis=0)
     d_mixed = dot_nt(d_attn, w_out).astype(bf16)
-    d_qkv = attend_back(qkv, mixed, d_mixed, lse)
+    if direct:
+        d_qkv, slot_out = attend_back(qkv, mixed, d_mixed, lse, slot_part)
+        slot_out = slot_out.reshape(slots, -1)
+    else:
+        (d_qkv,) = attend_back(qkv, mixed, d_mixed, lse)
     tokens_grad, gain_attn_rows = input_back(d_qkv, w_qkv, tokens, gain_attn, d_state)
     qkv_term = jnp.concatenate([dot_tn(normed_low, d_qkv[i]) for i in range(3)], axis=1)
     gain_attn_term = jnp.sum(gain_attn_rows, axis=0)

time: 609 us -> 524 us (0.86)
  waiting for transfers between devices: 230 us -> 46.2 us
  Pallas kernels: 172 us -> 316 us
  starting transfers between devices: 37.4 us -> 10.7 us
  other arithmetic: 44.2 us -> 26.1 us
    all_to_all x6 -> x2, waiting for transfers between devices: 217 us -> 43.7 us  [across(): lax.all_to_all(blocks, 'dp', 0, 0, axis_index_groups=same_part, tiled=True)]
    pallas_call x3, Pallas kernels: 123 us -> 269 us  [the longest x1 136 us: expert_exchange(): pl.pallas_call(functools.partial(expert_exchange_kernel, group), out_shap...]
    all_to_all x6 -> x2, starting transfers between devices: 36.4 us -> 10.1 us  [across(): lax.all_to_all(blocks, 'dp', 0, 0, axis_index_groups=same_part, tiled=True)]
    ppermute x4 -> x0, waiting for transfers between devices: 10.4 us -> none  [the longest x2 10.2 us: settle(): theirs = lax.ppermute(pieces[1], 'dp', swap)]
    concatenate x2 -> x0, other arithmetic: 10.2 us -> none  [share(): return jnp.concatenate([rows, lax.ppermute(rows, 'dp', swap)], axis=0)]
    unnamed x75 -> x73, local copies, waits for them, and re-layouts: 10.5 us -> 18.8 us
    convert_element_type x2 -> x0, other arithmetic: 7.67 us -> none  [settle(): return (pieces[0].astype(f32) + theirs.astype(f32)).astype(bf16)]
  transfers between devices with their start and end apart: 12 -> 4, of which waited for: 9 -> 3; matrix products, arithmetic and copies ran while one was open for 20% -> 12% of each run, Pallas kernels for 13% -> 1%
where the time goes in v2:
time: 524 us; the launch traced here: 519 us
  Pallas kernels  316 us (60%)
  matrix products  68.6 us (13%)
  local copies, waits for them, and re-layouts  49.3 us (9%)
  waiting for transfers between devices  46.2 us (9%)
  other arithmetic  26.1 us (5%)
  starting transfers between devices  10.7 us (2%)
    pallas_call x1, Pallas kernels, expert_exchange(): pl.pallas_call(functools.partial(expert_exchange_kernel, group), out_shap...  136 us
    pallas_call x1, Pallas kernels, attend(): pl.pallas_call(body, out_shape=out_shape, grid=(pairs,), in_specs=in_spec...  70.3 us
    pallas_call x1, Pallas kernels, attend_back(): pl.pallas_call(body, out_shape=out_shape, grid=(pairs,), in_specs=in_spec...  62.6 us
    dot_general x8, matrix products, dot_tn(): lax.dot_general(left, right, (((0,), (0,)), ((), ())), preferred_element_...  59 us
    all_to_all x2, waiting for transfers between devices, across(): lax.all_to_all(blocks, 'dp', 0, 0, axis_index_groups=same_part, tiled=True)  43.7 us
    unnamed x73, local copies, waits for them, and re-layouts  18.8 us
    concatenate x1, local copies, waits for them, and re-layouts, shards(): late = reduce_rows(jnp.concatenate([qkv_term, late_extra], axis=1))  13.9 us
    pallas_call x1, Pallas kernels, input_back(): pl.pallas_call(input_kernel, out_shape=(jax.ShapeDtypeStruct((count, widt...  13.1 us
  transfers between devices with their start and end apart: 4, of which 3 were waited for; matrix products, arithmetic and copies ran while one was open for 12% of the time, Pallas kernels for 1%

profile of v2, /device:TPU:12, one launch (start us, length us, event | category | flops | bytes accessed | tf_op | source)
XLA Modules:
  0.0 518.7 jit_solution(4823673344647908126)
XLA Ops:
  1.5 2.1 fusion.1
  3.5 0.9 copy.40
  4.5 0.9 copy.38.ids_ref
  5.4 0.9 copy.39.rank_col_ref
  7.1 2.0 slots.1
  9.1 4.0 dispatch_grad.1
  13.1 7.2 %convolution_convert_fusion.refs_0_.refs_1_.refs_2_ = bf16[1024,3072]{1,0:T(8,128)(2,1)S(1)} fusion(bf16[1024,3072]{1,0:T(8,128)(2,1)S(1)} %copy-done.29, bf16[1024,1024]{1,0:T(8,128)(2,1)S(1)} %copy-done.4, f32[1024]{0:T(1024)S(1)} %copy-done.17, f32[1024]{0:T(1024)S(1)} %add_rsqrt_fusion), kind=kOutput, calls=%fused_computation.5 | convolution fusion | flops 6449790976 | bytes 14688256 | tf_op jit(solution)/shard_map/dot_general | solution.py:1012
  20.4 70.3 %attend.1 = (bf16[1024,1024]{1,0:T(8,128)(2,1)S(1)}, f32[8,8,1024]{2,1,0:T(8,128)S(1)}, bf16[16,80,1152]{2,1,0:T(8,128)(2,1)S(1)}) custom-call(bf16[1024,3072]{1,0:T(8,128)(2,1)S(1)} %convolution_convert_fusion.refs_0_.refs_1_.refs_2_, bf16[1024,3072]{1,0:T(8,128)(2,1)S(1)} %convolution_convert_fusion.refs_0_.refs_1_.refs_2_, ...), custom_call_target="tpu_custom_call" | custom-call | flops 8589934592 | bytes 8388608 | tf_op jit(solution)/shard_map/attend/pallas_call | solution.py:282
  90.6 1.3 copy-done.21
  92.0 1.6 copy-done.26
  93.6 1.6 copy-done.22
  95.2 4.8 middle.1
  100.0 3.6 dispatch.1
  103.7 1.5 copy-done.20
  105.2 135.8 %experts.1 = (bf16[8,320,1408]{2,1,0:T(8,128)(2,1)}, bf16[8,320,1408]{2,1,0:T(8,128)(2,1)}, bf16[8,320,1408]{2,1,0:T(8,128)(2,1)}, bf16[8,320,1024]{2,1,0:T(8,12...) custom-call(bf16[16,80,1024]{2,1,0:T(8,128)(2,1)} %bitcast.61, ...), custom_call_target="tpu_custom_call" | custom-call | flops 44291850240 | bytes 47841280 | tf_op jit(solution)/shard_map/experts/pallas_call | solution.py:743
  241.0 1.6 copy-done.3
  242.6 12.1 %state_back.1 = (f32[1024,1024]{1,0:T(8,128)}, bf16[1024,1024]{1,0:T(8,128)(2,1)S(1)}, bf16[1024,128]{1,0:T(8,128)(2,1)S(1)}, f32[8,1024]{1,0:T(8,128)S(1)}) custom-call(s32[1024,128]{1,0:T(8,128)S(1)} %copy-done.10, f32[1024,128]{1,0:T(8,128)S(1)} %get-tuple-element.36.gate_ref, bf16[1280,1152]{1,0:T(8,128)(2,1)} %bitcast.66, f32[1024,1024]{1,0:T(8,128)} %copy-done, ...), custom_call_target="tpu_custom_call" | custom-call | flops 2684354560 | bytes 14680064 | tf_op jit(solution)/shard_map/state_back/pallas_call | solution.py:834
  254.8 2.4 convolution_convert_fusion.1.refs_4_
  257.1 0.7 copy-done.27
  257.9 62.6 %attend_back.1 = (bf16[3,1024,1024]{2,1,0:T(8,128)(2,1)}, bf16[16,80,1024]{2,1,0:T(8,128)(2,1)S(1)}) custom-call(bf16[1024,3072]{1,0:T(8,128)(2,1)} %copy-done.25, bf16[1024,3072]{1,0:T(8,128)(2,1)} %copy-done.25, bf16[1024,3072]{1,0:T(8,128)(2,1)} %copy-done.25, bf16[1024,1024]{1,0:T(8,128)(2,1)S(1)} %copy-done.23, ...), custom_call_target="tpu_custom_call" | custom-call | flops 21474836480 | bytes 16777216 | tf_op jit(solution)/shard_map/attend_back/pallas_call | solution.py:354
  320.5 7.1 %fusion.6 = f32[1024,1024]{0,1:T(8,128)} fusion(bf16[3,1024,1024]{2,1,0:T(8,128)(2,1)} %get-tuple-element.45.d_ref, bf16[1024,1024]{1,0:T(8,128)(2,1)S(1)} %copy-done.5, f32[1024]{0:T(1024)S(1)} %copy-done.17, f32[1024]{0:T(1024)S(1)} %add_rsqrt_fusion), kind=kOutput, calls=%fused_computation.20 | convolution fusion | flops 2151677952 | bytes 8396800 | tf_op jit(solution)/shard_map/dot_general | solution.py:32
  327.6 4.5 fusion.8
  332.1 4.5 fusion.10
  336.6 1.6 copy-done.6
  338.2 13.1 %input_back.1 = (f32[1024,1024]{1,0:T(8,128)}, f32[8,1024]{1,0:T(8,128)S(1)}) custom-call(bf16[3,1024,1024]{2,1,0:T(8,128)(2,1)} %get-tuple-element.45.d_ref, bf16[1024,3072]{1,0:T(8,128)(2,1)} %w_ref.1, bf16[1024,1024]{1,0:T(8,128)(2,1)S(1)} %copy-done.6, f32[1,1024]{1,0:T(1,128)S(1)} %bitcast.58, f32[1024,1024]{1,0:T(8,128)} %get-tuple-element.46.dstate_ref), custom_call_target="tpu_custom_call" | custom-call | flops 6442450944 | bytes 23068672 | tf_op jit(solution)/shard_map/input_back/pallas_call | solution.py:921
  351.5 9.6 %pad_maximum_fusion = f32[1024,3200]{0,1:T(8,128)} fusion(f32[1024,128]{0,1:T(8,128)S(1)} %broadcast_select_fusion, f32[1024,1024]{0,1:T(8,128)} %fusion.6, f32[1024,1024]{0,1:T(8,128)} %fusion.8, f32[1024,1024]{0,1:T(8,128)} %fusion.10), kind=kLoop, calls=%fused_computation | loop fusion | flops 9830400 | bytes 26214400 | tf_op jit(solution)/shard_map/concatenate | solution.py:1054
  361.1 13.9 %copy.41 = f32[1024,3200]{1,0:T(8,128)} copy(f32[1024,3200]{0,1:T(8,128)} %pad_maximum_fusion) | data formatting | bytes 26214400 | tf_op jit(solution)/shard_map/concatenate | solution.py:1054
  375.0 5.0 fusion.4
  380.1 4.5 fusion.20
  385.1 1.7 copy-done.28
  386.7 2.6 pad_maximum_fusion.1
  389.3 6.0 %copy.42 = f32[1024,1152]{1,0:T(8,128)} copy(f32[1024,1152]{0,1:T(8,128)} %pad_maximum_fusion.1) | data formatting | bytes 9437184 | tf_op jit(solution)/shard_map/concatenate | solution.py:1052
  395.3 1.8 fusion.15
  397.7 2.5 collective-permute-done.1
  400.2 2.9 fusion.5
  403.1 4.3 all-to-all-start.1
  407.4 2.2 copy-done.1
  409.6 1.7 copy-done.19
  411.3 7.2 %block_out.1 = bf16[1024,1024]{1,0:T(8,128)(2,1)} custom-call(s32[1024,128]{1,0:T(8,128)S(1)} %copy-done.10, f32[1024,128]{1,0:T(8,128)S(1)} %get-tuple-element.36.gate_ref, bf16[1280,1024]{1,0:T(8,128)(2,1)S(1)} %bitcast.60, f32[1024,1024]{1,0:T(8,128)S(1)} %copy-done.1), custom_call_target="tpu_custom_call" | custom-call | flops 5368709120 | bytes 9437184 | tf_op jit(solution)/shard_map/block_out/pallas_call | solution.py:879
  418.5 6.2 %fusion = bf16[16,32,3200]{2,1,0:T(8,128)(2,1)} fusion(bf16[16,32,3200]{2,1,0:T(8,128)(2,1)} %collective-permute-done, f32[16,2,32,3200]{3,2,1,0:T(8,128)} %bitcast.63, s32[]{:T(128)S(6)} %select_n.19), kind=kLoop, calls=%fused_computation.2 | loop fusion | flops 4915200 | bytes 13107204 | tf_op jit(solution)/shard_map/convert_element_type | solution.py:997
  424.7 11.5 %all-to-all-done.1 = bf16[16,32,1152]{2,1,0:T(8,128)(2,1)S(1)} async-done(((bf16[16,32,1152]{2,1,0:T(8,128)(2,1)}), bf16[16,32,1152]{2,1,0:T(8,128)(2,1)S(1)}, u32[]{:S(2)}, u32[]{:S(2)}) %all-to-all-start.1) | async-done | bytes 1179680 | tf_op jit(solution)/shard_map/all_to_all | solution.py:970
  436.1 5.8 %all-to-all-start = ((bf16[16,32,3200]{2,1,0:T(8,128)(2,1)}), bf16[16,32,3200]{2,1,0:T(8,128)(2,1)}, u32[]{:S(2)}, u32[]{:S(2)}) async-start(bf16[16,32,3200]{2,1,0:T(8,128)(2,1)} %fusion), calls=%async_computation | async-start | bytes 6553600 | tf_op jit(solution)/shard_map/all_to_all | solution.py:970
  442.0 14.1 %convolution_bitcast_fusion.2 = f32[1,1024,1408]{2,1,0:T(8,128)} fusion(bf16[8,320,1024]{2,1,0:T(8,128)(2,1)} %get-tuple-element.51, bf16[8,320,1408]{2,1,0:T(8,128)(2,1)} %get-tuple-element.52), kind=kOutput, calls=%fused_computation.11 | convolution fusion | flops 7381975040 | bytes 18219008 | tf_op jit(solution)/shard_map/dot_general | solution.py:32
  456.1 14.1 %convolution_bitcast_fusion.1 = f32[1,1024,1408]{2,1,0:T(8,128)} fusion(bf16[8,320,1024]{2,1,0:T(8,128)(2,1)} %get-tuple-element.51, bf16[8,320,1408]{2,1,0:T(8,128)(2,1)} %get-tuple-element.53), kind=kOutput, calls=%fused_computation.10 | convolution fusion | flops 7381975040 | bytes 18219008 | tf_op jit(solution)/shard_map/dot_general | solution.py:32
  470.3 9.7 %convolution_bitcast_fusion = f32[1,1408,1024]{2,1,0:T(8,128)} fusion(bf16[8,320,1408]{2,1,0:T(8,128)(2,1)S(1)} %bitcast.71, bf16[8,320,1024]{2,1,0:T(8,128)(2,1)S(1)} %bitcast.73), kind=kOutput, calls=%fused_computation.9 | convolution fusion | flops 7381975040 | bytes 18219008 | tf_op jit(solution)/shard_map/dot_general | solution.py:32
  482.2 32.2 %all-to-all-done = bf16[16,32,3200]{2,1,0:T(8,128)(2,1)} async-done(((bf16[16,32,3200]{2,1,0:T(8,128)(2,1)}), bf16[16,32,3200]{2,1,0:T(8,128)(2,1)}, u32[]{:S(2)}, u32[]{:S(2)}) %all-to-all-start) | async-done | bytes 3276832 | tf_op jit(solution)/shard_map/all_to_all | solution.py:970
  514.4 2.4 convert_reduce_fusion
  517.5 0.8 slice.33
  (79 shorter events, 4.9 us)
Async XLA Ops:
  0.6 8.4 %copy-start.2 = (bf16[1024,1024]{1,0:T(8,128)(2,1)S(1)}, bf16[1024,1024]{1,0:T(8,128)(2,1)}, u32[]{:S(2)}) copy-start(bf16[1024,1024]{1,0:T(8,128)(2,1)} %og_ref.1) | copy-start | bytes 6291460
  6.4 0.7 copy-start.11
  7.1 86.5 %copy-start.7 = (bf16[1024,128]{1,0:T(8,128)(2,1)}, bf16[1024,128]{1,0:T(8,128)(2,1)S(1)}, u32[]{:S(2)}) copy-start(bf16[1024,128]{1,0:T(8,128)(2,1)S(1)} %pad.4.wr_ref) | copy-start | bytes 786436
  9.0 84.5 %copy-start.9 = (s32[1024,128]{1,0:T(8,128)}, s32[1024,128]{1,0:T(8,128)S(1)}, u32[]{:S(2)}) copy-start(s32[1024,128]{1,0:T(8,128)S(1)} %get-tuple-element.33.col_ref) | copy-start | bytes 1572868
  9.1 4.0 copy-start.4
  9.1 4.0 copy-start.17
  9.1 4.0 copy-start.29
  20.3 70.3 %copy-start.25 = (bf16[1024,3072]{1,0:T(8,128)(2,1)}, bf16[1024,3072]{1,0:T(8,128)(2,1)S(1)}, u32[]{:S(2)}) copy-start(bf16[1024,3072]{1,0:T(8,128)(2,1)S(1)} %convolution_convert_fusion.refs_0_.refs_1_.refs_2_) | copy-start | bytes 18874372
  20.3 73.2 %copy-start.12 = (f32[1024]{0:T(1024)S(1)}, f32[1024]{0:T(1024)}, u32[]{:S(2)}) copy-start(f32[1024]{0:T(1024)} %param.20) | copy-start | bytes 12292
  20.3 73.2 %copy-start.13 = (bf16[1024,1024]{1,0:T(8,128)(2,1)S(1)}, bf16[1024,1024]{1,0:T(8,128)(2,1)}, u32[]{:S(2)}) copy-start(bf16[1024,1024]{1,0:T(8,128)(2,1)} %w_out_ref.1) | copy-start | bytes 6291460
  90.6 1.3 copy-start.21
  92.0 1.6 copy-start.26
  93.6 1.6 copy-start.22
  100.0 3.7 copy-start
  103.7 1.5 copy-start.20
  105.2 135.8 %copy-start.8 = (bf16[1024,128]{1,0:T(8,128)(2,1)S(1)}, bf16[1024,128]{1,0:T(8,128)(2,1)}, u32[]{:S(2)}) copy-start(bf16[1024,128]{1,0:T(8,128)(2,1)} %copy-done.7) | copy-start | bytes 786436
  105.2 135.8 %copy-start.10 = (s32[1024,128]{1,0:T(8,128)S(1)}, s32[1024,128]{1,0:T(8,128)}, u32[]{:S(2)}) copy-start(s32[1024,128]{1,0:T(8,128)} %copy-done.9) | copy-start | bytes 1572868
  241.0 1.6 copy-start.3
  242.6 12.1 %copy-start.14 = (bf16[1024,1024]{1,0:T(8,128)(2,1)S(1)}, bf16[1024,1024]{1,0:T(8,128)(2,1)}, u32[]{:S(2)}) copy-start(bf16[1024,1024]{1,0:T(8,128)(2,1)} %w_out_ref.1) | copy-start | bytes 6291460
  254.7 2.4 copy-start.15
  254.7 2.4 copy-start.23
  254.7 3.1 copy-start.27
  257.9 62.6 %copy-start.5 = (bf16[1024,1024]{1,0:T(8,128)(2,1)S(1)}, bf16[1024,1024]{1,0:T(8,128)(2,1)}, u32[]{:S(2)}) copy-start(bf16[1024,1024]{1,0:T(8,128)(2,1)} %tok_ref.3) | copy-start | bytes 6291460
  320.5 7.1 %copy-start.18 = (bf16[16,80,1024]{2,1,0:T(8,128)(2,1)}, bf16[16,80,1024]{2,1,0:T(8,128)(2,1)S(1)}, u32[]{:S(2)}) copy-start(bf16[16,80,1024]{2,1,0:T(8,128)(2,1)S(1)} %get-tuple-element.44) | copy-start | bytes 7864324
  320.5 7.1 %copy-start.30 = (bf16[3,1024,1024]{2,1,0:T(8,128)(2,1)S(1)}, bf16[3,1024,1024]{2,1,0:T(8,128)(2,1)}, u32[]{:S(2)}) copy-start(bf16[3,1024,1024]{2,1,0:T(8,128)(2,1)} %get-tuple-element.45.d_ref) | copy-start | bytes 18874372
  336.6 1.6 copy-start.6
  375.0 5.1 copy-start.16
  375.0 5.1 copy-start.24
  380.1 38.4 %collective-permute-start = (bf16[16,32,3200]{2,1,0:T(8,128)(2,1)}, bf16[16,32,3200]{2,1,0:T(8,128)(2,1)}, u32[]{:S(2)}, u32[]{:S(2)}) collective-permute-start(bf16[16,32,3200]{2,1,0:T(8,128)(2,1)} %fusion.4), channel_id=1, source_target_pairs={{0,1},{1,0},{2,3},{3,2},{4,5},{5,4},{6,7},{7,6},{8,9},{9,8},{10,11... | collective-permute-start | bytes 9830408 | tf_op jit(solution)/shard_map/ppermute | solution.py:996
  384.5 2.2 copy-start.28
  397.1 3.0 collective-permute-start.1
  403.1 33.0 %all-to-all-start.1 = ((bf16[16,32,1152]{2,1,0:T(8,128)(2,1)}), bf16[16,32,1152]{2,1,0:T(8,128)(2,1)S(1)}, u32[]{:S(2)}, u32[]{:S(2)}) async-start(bf16[16,32,1152]{2,1,0:T(8,128)(2,1)} %fusion.5), calls=%async_computation.1 | async-start | bytes 2359296 | tf_op jit(solution)/shard_map/all_to_all | solution.py:970
  407.4 2.2 copy-start.1
  409.6 1.7 copy-start.19
  436.1 78.2 %all-to-all-start = ((bf16[16,32,3200]{2,1,0:T(8,128)(2,1)}), bf16[16,32,3200]{2,1,0:T(8,128)(2,1)}, u32[]{:S(2)}, u32[]{:S(2)}) async-start(bf16[16,32,3200]{2,1,0:T(8,128)(2,1)} %fusion), calls=%async_computation | async-start | bytes 6553600 | tf_op jit(solution)/shard_map/all_to_all | solution.py:970
  442.0 28.3 %slice-start = ((s8[7208960]{0:T(1024)(128)(4,1)}), s8[4194304]{0:T(1024)(128)(4,1)S(1)}, s32[]{:S(2)}) async-start(s8[7208960]{0:T(1024)(128)(4,1)} %bitcast.70), calls=%async_computation.2 | async-start | bytes 8388608
  442.0 28.3 %slice-start.2 = ((s8[5242880]{0:T(1024)(128)(4,1)}), s8[4194304]{0:T(1024)(128)(4,1)S(1)}, s32[]{:S(2)}) async-start(s8[5242880]{0:T(1024)(128)(4,1)} %bitcast.72), calls=%async_computation.4 | async-start | bytes 8388608
  456.1 14.2 %slice-start.1 = ((s8[7208960]{0:T(1024)(128)(4,1)}), s8[3014656]{0:T(1024)(128)(4,1)S(1)}, s32[]{:S(2)}) async-start(s8[7208960]{0:T(1024)(128)(4,1)} %bitcast.70), calls=%async_computation.3 | async-start | bytes 6029312
  456.1 14.2 %slice-start.3 = ((s8[5242880]{0:T(1024)(128)(4,1)}), s8[1048576]{0:T(1024)(128)(4,1)S(1)}, s32[]{:S(2)}) async-start(s8[5242880]{0:T(1024)(128)(4,1)} %bitcast.72), calls=%async_computation.5 | async-start | bytes 2097152

commit v3 on v2

--- a/solution.py
+++ b/solution.py
@@ -328,40 +328,239 @@
     out_ref[2, :, :] = dv_sc[...].astype(bf16)
 
 
-def attend_back(qkv, mixed, d_mixed, lse, blocks=None):
+def attend_back(qkv, mixed, d_mixed, lse):
     count, width = mixed.shape
     pairs = width // LANES
-    in_specs = [
-        pl.BlockSpec((count, LANES), lambda i: (0, i)),
-        pl.BlockSpec((count, LANES), lambda i: (0, i + pairs)),
-        pl.BlockSpec((count, LANES), lambda i: (0, i + 2 * pairs)),
-        pl.BlockSpec((count, LANES), lambda i: (0, i)),
-        pl.BlockSpec((count, LANES), lambda i: (0, i)),
-        pl.BlockSpec((1, 8, count), lambda i: (i, 0, 0)),
-    ]
-    out_specs = [pl.BlockSpec((3, count, LANES), lambda i: (0, 0, i))]
-    out_shape = [jax.ShapeDtypeStruct((3, count, width), bf16)]
-    body, args, extra = attend_back_kernel, [qkv, qkv, qkv, mixed, d_mixed, lse], {}
-    scratch = [pltpu.VMEM((count, LANES), f32), pltpu.VMEM((count, LANES), f32)]
-    if blocks is not None:
-        body = riding(attend_back_kernel, len(in_specs), len(out_specs))
-        in_specs.append(pl.BlockSpec(memory_space=pl.ANY))
-        out_specs.append(pl.BlockSpec(memory_space=pl.ANY))
-        out_shape.append(jax.ShapeDtypeStruct(blocks.shape, blocks.dtype))
-        args.append(blocks)
-        scratch = scratch + exchange_sems(blocks.shape[0])
-        extra = dict(collective_id=1, has_side_effects=True)
     return pl.pallas_call(
-        body,
-        out_shape=out_shape,
+        attend_back_kernel,
+        out_shape=jax.ShapeDtypeStruct((3, count, width), bf16),
         grid=(pairs,),
-        in_specs=in_specs,
-        out_specs=out_specs,
-        scratch_shapes=scratch,
-        compiler_params=params(40, **extra),
+        in_specs=[
+            pl.BlockSpec((count, LANES), lambda i: (0, i)),
+            pl.BlockSpec((count, LANES), lambda i: (0, i + pairs)),
+            pl.BlockSpec((count, LANES), lambda i: (0, i + 2 * pairs)),
+            pl.BlockSpec((count, LANES), lambda i: (0, i)),
+            pl.BlockSpec((count, LANES), lambda i: (0, i)),
+            pl.BlockSpec((1, 8, count), lambda i: (i, 0, 0)),
+        ],
+        out_specs=pl.BlockSpec((3, count, LANES), lambda i: (0, 0, i)),
+        scratch_shapes=[pltpu.VMEM((count, LANES), f32), pltpu.VMEM((count, LANES), f32)],
+        compiler_params=params(40),
         cost_estimate=cost(5 * 4 * count * count * width, 16 * count * width, 8 * count * count),
         name="attend_back",
-    )(*args)
+    )(qkv, qkv, qkv, mixed, d_mixed, lse)
+
+
+def back_reduce_kernel(
+    chips,
+    q_ref, k_ref, v_ref, o_ref, do_ref, lse_ref, datt_ref, norm_ref, mix_ref, moe_ref, dlog_ref, gm_ref, slot_ref,
+    out_ref, sum_ref, extra_ref, back_ref,
+    dk_sc, dv_sc, norm_t, mix_t, right, terms, firsts, sums, half0, half1, half2, half3, s_send, s_recv,
+    *ride_sems,
+):
+    halves = (half0, half1, half2, half3)
+    levels = chips.bit_length() - 1
+    count = k_ref.shape[0]
+    width = norm_ref.shape[1]
+    rows = terms.shape[3]
+    turn = pl.program_id(0)
+    pairs = sum_ref.shape[0]
+    me = lax.axis_index("dp")
+    chip, core = lax.div(me, 2), lax.rem(me, 2)
+    mate = 2 * chip + 1 - core
+    order0 = [1 << b for b in range(levels)]
+    order1 = list(order0)
+    order1[0], order1[1] = order0[1], order0[0]
+    order0[2:] = order0[2:][::-1]
+
+    def bit(mask):
+        return lax.rem(lax.div(chip, mask), 2)
+
+    own, peers = [], []
+    for level in range(levels):
+        b0, b1 = bit(order0[level]), bit(order1[level])
+        own.append(b0 + core * (b1 - b0))
+        p0 = order0[level] * (1 - 2 * b0)
+        p1 = order1[level] * (1 - 2 * b1)
+        peers.append(2 * (chip + p0 + core * (p1 - p0)) + core)
+    bases = [0]
+    for level in range(levels):
+        bases.append(bases[-1] + own[level] * (chips >> (level + 1)))
+
+    def remote(src, dst, c, level, device):
+        return pltpu.make_async_remote_copy(
+            src_ref=src, dst_ref=dst, send_sem=s_send.at[c, level], recv_sem=s_recv.at[c, level],
+            device_id=(device,), device_id_type=MESH,
+        )
+
+    def cols(c):
+        return pl.ds(0, LANES) if isinstance(c, int) else slice(None)
+
+    def swap(c):
+        return remote(
+            terms.at[c, :, 1 - core, :, cols(c)], firsts.at[c, :, :, cols(c)], c, levels, mate
+        )
+
+    def send(c, level):
+        span = chips >> (level + 1)
+        start = bases[level] + (1 - own[level]) * span
+        return remote(
+            sums.at[c, pl.ds(start, span), :, cols(c)], halves[level].at[c, :, :, cols(c)], c, level, peers[level]
+        )
+
+    def fold_swap(c):
+        swap(c).wait_recv()
+        for b in range(chips):
+            places = []
+            for order in (order0, order1):
+                place = 0
+                for level in range(levels):
+                    place += (b // order[level] % 2) * (chips >> (level + 1))
+                places.append(place)
+            at = places[0] + core * (places[1] - places[0])
+            total = terms[c, b, core, :, cols(c)].astype(f32) + firsts[c, b, :, cols(c)].astype(f32)
+            sums[c, at, :, cols(c)] = total.astype(bf16)
+
+    def fold(c, level):
+        send(c, level).wait()
+        for t in range(chips >> (level + 1)):
+            at = bases[level + 1] + t
+            total = sums[c, at, :, cols(c)].astype(f32) + halves[level][c, t, :, cols(c)].astype(f32)
+            if level < levels - 1:
+                sums[c, at, :, cols(c)] = total.astype(bf16)
+            elif isinstance(c, int):
+                extra_ref[...] = total
+            else:
+                sum_ref[c] = total
+
+    def stage(c, s):
+        if s == 1:
+            fold_swap(c)
+        else:
+            fold(c, s - 2)
+        if s - 1 < levels:
+            send(c, s - 1).start()
+
+    riders, ride = exchange_copies(slot_ref, back_ref, *ride_sems)
+    span = 256
+    per = span // (2 * rows)
+
+    @pl.when(turn == 0)
+    def _():
+        greet([mate] + riders)
+        for copy in ride:
+            copy.start()
+        norm_t[...] = jnp.transpose(norm_ref[...])
+        mix_t[...] = jnp.transpose(mix_ref[...])
+        for row in range(0, width, span):
+            extra = dot_tn(moe_ref[:, row : row + span], dlog_ref[...])
+            gain = jnp.transpose(jnp.sum(gm_ref[:, row : row + span], axis=0, keepdims=True))
+            extra = extra + jnp.where(iota(extra.shape, 1) == 64, gain, 0.0)
+            at = row // (2 * rows)
+            terms[pairs, at : at + per, :, :, 0:LANES] = extra.astype(bf16).reshape(per, 2, rows, LANES)
+        swap(pairs).start()
+
+    for s in range(levels + 1, 0, -1):
+        c = turn - s
+
+        @pl.when((c >= 0) & (c < pairs))
+        def _():
+            stage(c, s)
+
+        @pl.when(c == 0)
+        def _():
+            stage(pairs, s)
+
+    @pl.when(turn < pairs)
+    def _():
+        attend_back_kernel(q_ref, k_ref, v_ref, o_ref, do_ref, lse_ref, out_ref, dk_sc, dv_sc)
+        for i in range(3):
+            right[:, i * LANES : (i + 1) * LANES] = out_ref[i]
+        for row in range(0, width, span):
+            qkv_rows = dot_nn(norm_t[row : row + span, :], right[...])
+            out_rows = dot_nn(mix_t[row : row + span, :], datt_ref[...])
+            at = row // (2 * rows)
+            terms[turn, at : at + per, :, :, 0 : 3 * LANES] = (
+                qkv_rows.astype(bf16).reshape(per, 2, rows, 3 * LANES)
+            )
+            terms[turn, at : at + per, :, :, 3 * LANES :] = out_rows.astype(bf16).reshape(per, 2, rows, LANES)
+        swap(turn).start()
+
+    @pl.when(turn == pl.num_programs(0) - 1)
+    def _():
+        for c in range(pairs):
+            swap(jnp.int32(c)).wait_send()
+        swap(pairs).wait_send()
+        for copy in ride:
+            copy.wait()
+
+
+def attend_back_reduce(qkv, mixed, d_mixed, lse, d_attn, normed, moe_low, d_log, gain_rows, slot_rows, n_dev):
+    count, width = mixed.shape
+    pairs = width // LANES
+    chips = n_dev // 2
+    levels = chips.bit_length() - 1
+    rows = width // n_dev
+    wide = 4 * LANES
+    vmem, dma = pltpu.VMEM, pltpu.SemaphoreType.DMA
+    anywhere = pl.BlockSpec(memory_space=pl.ANY)
+
+    def column(offset=0):
+        return pl.BlockSpec((count, LANES), lambda i: (0, jnp.minimum(i, pairs - 1) + offset))
+
+    def whole(array):
+        return pl.BlockSpec(array.shape, lambda i: (0, 0), pipeline_mode=pl.Buffered(1))
+
+    d_qkv, sums, extra, back = pl.pallas_call(
+        functools.partial(back_reduce_kernel, chips),
+        out_shape=(
+            jax.ShapeDtypeStruct((3, count, width), bf16),
+            jax.ShapeDtypeStruct((pairs, rows, wide), f32),
+            jax.ShapeDtypeStruct((rows, LANES), f32),
+            jax.ShapeDtypeStruct(slot_rows.shape, bf16),
+        ),
+        grid=(pairs + levels + 1,),
+        in_specs=[
+            column(),
+            column(pairs),
+            column(2 * pairs),
+            column(),
+            column(),
+            pl.BlockSpec((1, 8, count), lambda i: (jnp.minimum(i, pairs - 1), 0, 0)),
+            column(),
+            whole(normed),
+            whole(mixed),
+            whole(moe_low),
+            whole(d_log),
+            whole(gain_rows),
+            anywhere,
+        ],
+        out_specs=(
+            pl.BlockSpec((3, count, LANES), lambda i: (0, 0, jnp.minimum(i, pairs - 1))),
+            pl.BlockSpec((pairs, rows, wide), lambda i: (0, 0, 0)),
+            pl.BlockSpec((rows, LANES), lambda i: (0, 0)),
+            anywhere,
+        ),
+        scratch_shapes=[
+            vmem((count, LANES), f32),
+            vmem((count, LANES), f32),
+            vmem((width, count), bf16),
+            vmem((width, count), bf16),
+            vmem((count, 3 * LANES), bf16),
+            vmem((pairs + 1, chips, 2, rows, wide), bf16),
+            vmem((pairs + 1, chips, rows, wide), bf16),
+            vmem((pairs + 1, chips, rows, wide), bf16),
+        ]
+        + [vmem((pairs + 1, chips >> (level + 1), rows, wide), bf16) for level in range(levels)]
+        + [dma((pairs + 1, levels + 1)), dma((pairs + 1, levels + 1))]
+        + exchange_sems(chips),
+        compiler_params=params(58, collective_id=1, has_side_effects=True),
+        cost_estimate=cost(5 * 4 * count * count * width, 40 * count * width, 8 * count * count),
+        name="attend_back_reduce",
+    )(qkv, qkv, qkv, mixed, d_mixed, lse, d_attn, normed, mixed, moe_low, d_log, gain_rows, slot_rows)
+    parts = sums.reshape(pairs, rows, 4, LANES)
+    parts = jnp.transpose(parts, (1, 2, 0, 3)).reshape(rows, 4 * width)
+    return d_qkv, parts[:, 0 : 3 * width], parts[:, 3 * width :], extra, back
 
 
 def middle_kernel(experts, mixed_ref, w_out_ref, tok_ref, gain_ref, wr_ref, col_ref, h_ref, low_ref, gate_ref):
@@ -498,7 +697,7 @@
 
 
 def expert_exchange_kernel(
-    group, x_ref, g_ref, wg_hbm, wu_hbm, wd_hbm, wr_ref,
+    group, window, x_ref, g_ref, wg_hbm, wu_hbm, wd_hbm, wr_ref,
     act_ref, dgp_ref, dup_ref, de_ref, xs_ref, slot_ref, back_ref,
     xb, gb, ds, rd, pd, sp, rp, pp, st_act, st_dgp, st_dup, st_de, wg_ref, wu_ref, wd_ref,
     w_sem, x_send, x_recv, f_send, f_recv, g_own, g_send, g_recv,
@@ -527,13 +726,18 @@
         )
 
     def own(buf, q, g):
-        return buf.at[q, g * pair : g * pair + capacity]
+        if isinstance(g, int):
+            return buf.at[q, g * pair : g * pair + capacity]
+        return buf.at[q, pl.ds(pl.multiple_of(g * pair, 16), capacity)]
 
     def theirs(buf, q, g):
         return buf.at[q, g * pair + capacity : (g + 1) * pair]
 
     def x_copy(place):
-        q, g = place // group, place % group
+        if isinstance(place, int):
+            q, g = place // group, place % group
+        else:
+            q, g = lax.div(place, group), lax.rem(place, group)
         peer = chip_at(place)
         return remote(x_ref.at[peer], own(xb, q, g), x_send.at[place], x_recv.at[place], 2 * peer + core)
 
@@ -592,16 +796,12 @@
         copy.start()
     self_x.start()
     greet([2 * chip_at(place) + core for place in range(1, experts)] + [mate])
-    for place in range(1, group):
+    for place in range(1, min(group + window, experts)):
         x_copy(place).start()
     for q in range(steps):
         for g in range(group):
             g_mine(q, g).start()
             g_mate(q, g).start()
-        for g in range(group):
-            place = (q + 1) * group + g
-            if place < experts:
-                x_copy(place).start()
     self_x.wait()
     forward(0, 0).start()
     for g in range(1, group):
@@ -682,6 +882,12 @@
             for g in range(group):
                 x_arrival(q + 1, g).wait_recv()
                 forward(q + 1, g).start()
+            for g in range(group):
+                place = (q + 1) * group + window + g
+
+                @pl.when(place < experts)
+                def _():
+                    x_copy(place).start()
 
         @pl.when(q >= 1)
         def _():
@@ -729,10 +935,9 @@
                 back_copy(q, g).wait()
 
 
-def expert_exchange(x, g, wg, wu, wd, wr):
+def expert_exchange(x, g, wg, wu, wd, wr, group=2, window=4):
     experts, capacity, width = x.shape
     ff = wg.shape[1]
-    group = 2
     steps = experts // group
     rows = 2 * capacity * group
     wide = width + LANES
@@ -741,7 +946,7 @@
     each = dma((experts,))
     count = rows * steps
     outs = pl.pallas_call(
-        functools.partial(expert_exchange_kernel, group),
+        functools.partial(expert_exchange_kernel, group, window),
         out_shape=(
             jax.ShapeDtypeStruct((steps, rows, ff), bf16),
             jax.ShapeDtypeStruct((steps, rows, ff), bf16),
@@ -893,7 +1098,7 @@
     )(col, gates, slot_rows, hidden)
 
 
-def input_kernel(d_ref, w_ref, tok_ref, gain_ref, dstate_ref, grad_ref, gterm_ref):
+def input_kernel(d_ref, w_ref, tok_ref, gain_ref, dstate_ref, grad_ref):
     rows, width = tok_ref.shape
     d_normed = dot_nt(d_ref[0], w_ref[:, 0:width])
     for i in range(1, 3):
@@ -904,13 +1109,6 @@
     scaled = gain_ref[...] * d_normed
     share = jnp.mean(normal * scaled, axis=1, keepdims=True)
     grad_ref[...] = dstate_ref[...] + inverse * (scaled - normal * share)
-    term = jnp.sum((normal * d_normed).reshape(rows // 8, 8, width), axis=0)
-
-    @pl.when(pl.program_id(0) == 0)
-    def _():
-        gterm_ref[...] = jnp.zeros_like(gterm_ref)
-
-    gterm_ref[...] += term
 
 
 def input_back(d_qkv, w_qkv, tokens, gain, d_state):
@@ -920,10 +1118,7 @@
     part = lambda i: (i, 0)
     return pl.pallas_call(
         input_kernel,
-        out_shape=(
-            jax.ShapeDtypeStruct((count, width), f32),
-            jax.ShapeDtypeStruct((8, width), f32),
-        ),
+        out_shape=jax.ShapeDtypeStruct((count, width), f32),
         grid=(count // rows,),
         in_specs=[
             pl.BlockSpec((3, rows, width), lambda i: (0, i, 0)),
@@ -932,7 +1127,7 @@
             pl.BlockSpec((1, width), whole),
             pl.BlockSpec((rows, width), part),
         ],
-        out_specs=(pl.BlockSpec((rows, width), part), pl.BlockSpec((8, width), whole)),
+        out_specs=pl.BlockSpec((rows, width), part),
         compiler_params=params(48),
         cost_estimate=cost(6 * count * width * width, 22 * count * width),
         name="input_back",
@@ -1034,24 +1229,27 @@
     d_state, d_attn, d_log, gain_moe_rows = state_back(
         col, gates, d_in_back, hidden, out_grad, gain_moe, wr
     )
-    out_term = dot_tn(mixed, d_attn)
-    router_term = dot_tn(moe_low, d_log)
-    gain_moe_term = jnp.sum(gain_moe_rows, axis=0)
     d_mixed = dot_nt(d_attn, w_out).astype(bf16)
     if direct:
-        d_qkv, slot_out = attend_back(qkv, mixed, d_mixed, lse, slot_part)
+        d_qkv, qkv_sum, out_rows, extra, slot_out = attend_back_reduce(
+            qkv, mixed, d_mixed, lse, d_attn, normed_low, moe_low, d_log, gain_moe_rows, slot_part, n_dev
+        )
         slot_out = slot_out.reshape(slots, -1)
+        router_sum, gain_moe_sum = extra[:, 0:experts], extra[:, 64]
     else:
-        (d_qkv,) = attend_back(qkv, mixed, d_mixed, lse)
-    tokens_grad, gain_attn_rows = input_back(d_qkv, w_qkv, tokens, gain_attn, d_state)
-    qkv_term = jnp.concatenate([dot_tn(normed_low, d_qkv[i]) for i in range(3)], axis=1)
-    gain_attn_term = jnp.sum(gain_attn_rows, axis=0)
-
-    lane = jnp.arange(LANES, dtype=jnp.int32)[None, :]
-    extra = jnp.where(lane == experts, gain_moe_term[:, None], router_term)
-    early = reduce_rows(jnp.concatenate([out_term, extra], axis=1))
-    late_extra = jnp.where(lane == 0, gain_attn_term[:, None], 0.0)
-    late = reduce_rows(jnp.concatenate([qkv_term, late_extra], axis=1))
+        d_qkv = attend_back(qkv, mixed, d_mixed, lse)
+        lane = jnp.arange(LANES, dtype=jnp.int32)[None, :]
+        gain_moe_term = jnp.sum(gain_moe_rows, axis=0)
+        extra = jnp.where(lane == experts, gain_moe_term[:, None], dot_tn(moe_low, d_log))
+        early = reduce_rows(jnp.concatenate([dot_tn(mixed, d_attn), extra], axis=1))
+        out_rows, router_sum, gain_moe_sum = (
+            early[:, 0:width], early[:, width : width + experts], early[:, width + experts]
+        )
+        qkv_sum = reduce_rows(jnp.concatenate([dot_tn(normed_low, d_qkv[i]) for i in range(3)], axis=1))
+    tokens_grad = input_back(d_qkv, w_qkv, tokens, gain_attn, d_state)
+    my_rows = width // n_dev
+    weight_rows = lax.dynamic_slice_in_dim(w_qkv, me * my_rows, my_rows, 0).astype(f32)
+    gain_attn_sum = jnp.sum(weight_rows * qkv_sum, axis=1) / lax.dynamic_slice_in_dim(gain_attn, me * my_rows, my_rows, 0)
 
     down_grad = dot_tn(act, d_rows)
     gate_grad = dot_tn(rows_in, d_pre)
@@ -1060,11 +1258,11 @@
     return (
         block_out,
         tokens_grad,
-        late[:, 3 * width],
-        late[:, 0 : 3 * width],
-        early[:, 0:width],
-        early[:, width + experts],
-        early[:, width : width + experts],
+        gain_attn_sum,
+        qkv_sum,
+        out_rows,
+        gain_moe_sum,
+        router_sum,
         gate_grad[None],
         up_grad[None],
         down_grad[None],

time: 524 us -> 450 us (0.86)
  the two profiles are of different devices: /device:TPU:12 before, /device:TPU:0 now
where the time goes in v3:
time: 450 us; the launch traced here: 442 us
  Pallas kernels  367 us (82%)
  matrix products  49 us (11%)
  local copies, waits for them, and re-layouts  17.4 us (4%)
  other arithmetic  6.97 us (2%)
    pallas_call x1, Pallas kernels, expert_exchange(): pl.pallas_call(functools.partial(expert_exchange_kernel, group, window),...  141 us
    pallas_call x1, Pallas kernels, attend_back_reduce(): pl.pallas_call(functools.partial(back_reduce_kernel, chips), out_shape=(j...  121 us
    pallas_call x1, Pallas kernels, attend(): pl.pallas_call(body, out_shape=out_shape, grid=(pairs,), in_specs=in_spec...  57.2 us
    dot_general x3, matrix products, dot_tn(): lax.dot_general(left, right, (((0,), (0,)), ((), ())), preferred_element_...  36.6 us
    unnamed x78, local copies, waits for them, and re-layouts  15.3 us
    pallas_call x1, Pallas kernels, input_back(): pl.pallas_call(input_kernel, out_shape=jax.ShapeDtypeStruct((count, width...  13 us
    pallas_call x1, Pallas kernels, state_back(): pl.pallas_call(state_kernel, out_shape=(jax.ShapeDtypeStruct((count, widt...  12.1 us

profile of v3, /device:TPU:0, one launch (start us, length us, event | category | flops | bytes accessed | tf_op | source)
XLA Modules:
  0.0 441.9 jit_solution(14319626504161685410)
XLA Ops:
  0.6 0.0 copy-start.30
  0.7 2.2 fusion
  2.9 2.3 fusion.2.norm_ref
  5.2 1.3 copy-done.25
  6.5 8.7 %convolution_convert_fusion.refs_0_.refs_1_.refs_2_.q_ref.k_ref.v_ref = bf16[1024,3072]{1,0:T(8,128)(2,1)} fusion(bf16[1024,1024]{1,0:T(8,128)(2,1)S(1)} %fusion.2.norm_ref, bf16[1024,3072]{1,0:T(8,128)(2,1)S(1)} %copy-done.30), kind=kOutput, calls=%fused_computation | convolution fusion | flops 6445596672 | bytes 14680064 | tf_op jit(solution)/shard_map/dot_general | solution.py:1207
  15.2 0.2 copy.27.ids_ref
  15.5 0.2 copy.28.rank_col_ref
  16.4 2.0 slots.1
  18.4 4.0 dispatch_grad.1
  22.4 2.8 copy-done.22
  25.2 57.2 %attend.1 = (bf16[1024,1024]{1,0:T(8,128)(2,1)S(1)}, f32[8,8,1024]{2,1,0:T(8,128)S(1)}, bf16[16,80,1152]{2,1,0:T(8,128)(2,1)S(1)}) custom-call(bf16[1024,3072]{1,0:T(8,128)(2,1)S(1)} %copy-done.22, bf16[1024,3072]{1,0:T(8,128)(2,1)S(1)} %copy-done.22, bf16[1024,3072]{1,0:T(8,128)(2,1)S(1)} %copy-done.22, bf16[16,80,1152]{2,1,0:T(8,128)(2,1)S(1)} %bitcast.40), custom_call_target="tpu_custom_call" | custom-call | flops 8589934592 | bytes 8388608 | tf_op jit(solution)/shard_map/attend/pallas_call | solution.py:282
  82.4 0.0 copy-start.19
  82.4 1.3 copy-done.19
  83.7 1.6 copy-done.23
  85.3 0.2 copy.29
  85.5 0.1 pad.4.wr_ref
  85.5 0.5 copy-done.24
  86.0 0.0 copy-start.12
  86.0 1.7 copy-done.12
  87.7 1.6 copy-done.20
  89.3 4.8 %middle.1 = (f32[1024,1024]{1,0:T(8,128)S(1)}, bf16[1024,1024]{1,0:T(8,128)(2,1)S(1)}, f32[1024,128]{1,0:T(8,128)S(1)}) custom-call(bf16[1024,1024]{1,0:T(8,128)(2,1)S(1)} %copy-done.20, bf16[1024,1024]{1,0:T(8,128)(2,1)S(1)} %copy-done.12, bf16[1024,1024]{1,0:T(8,128)(2,1)S(1)} %copy-done, f32[1,1024]{1,0:T(1,128)S(1)} %bitcast.38, ...), custom_call_target="tpu_custom_call" | custom-call | flops 2147483648 | bytes 12582912 | tf_op jit(solution)/shard_map/middle/pallas_call | solution.py:590
  94.1 0.0 copy-start.1
  94.1 3.7 dispatch.1
  97.8 0.0 copy-start.18
  97.9 1.5 copy-done.18
  99.3 141.1 %experts.1 = (bf16[8,320,1408]{2,1,0:T(8,128)(2,1)}, bf16[8,320,1408]{2,1,0:T(8,128)(2,1)}, bf16[8,320,1408]{2,1,0:T(8,128)(2,1)}, bf16[8,320,1024]{2,1,0:T(8,12...) custom-call(bf16[16,80,1024]{2,1,0:T(8,128)(2,1)} %bitcast.42, ...), custom_call_target="tpu_custom_call" | custom-call | flops 44291850240 | bytes 47841280 | tf_op jit(solution)/shard_map/experts/pallas_call | solution.py:948
  240.4 0.0 copy-start.4
  240.4 1.6 copy-done.4
  242.0 12.1 %state_back.1 = (f32[1024,1024]{1,0:T(8,128)}, bf16[1024,1024]{1,0:T(8,128)(2,1)S(1)}, bf16[1024,128]{1,0:T(8,128)(2,1)S(1)}, f32[8,1024]{1,0:T(8,128)S(1)}) custom-call(s32[1024,128]{1,0:T(8,128)S(1)} %copy-done.8, f32[1024,128]{1,0:T(8,128)S(1)} %get-tuple-element.36.gate_ref, bf16[1280,1152]{1,0:T(8,128)(2,1)} %bitcast.43, f32[1024,1024]{1,0:T(8,128)} %copy-done.1, ...), custom_call_target="tpu_custom_call" | custom-call | flops 2684354560 | bytes 14680064 | tf_op jit(solution)/shard_map/state_back/pallas_call | solution.py:1039
  254.1 3.7 convolution_convert_fusion.1.do_ref
  257.8 121.4 %attend_back_reduce.1 = (bf16[3,1024,1024]{2,1,0:T(8,128)(2,1)}, f32[8,32,512]{2,1,0:T(8,128)}, f32[32,128]{1,0:T(8,128)}, bf16[16,80,1024]{2,1,0:T(8,128)(2,1)}) custom-call(bf16[1024,3072]{1,0:T(8,128)(2,1)} %convolution_convert_fusion.refs_0_.refs_1_.refs_2_.q_ref.k_ref.v_ref, ...), custom_call_target="tpu_custom_call" | custom-call | flops 21474836480 | bytes 41943040 | tf_op jit(solution)/shard_map/attend_back_reduce/pallas_call | solution.py:514
  379.3 0.0 copy-start.2
  379.3 13.0 %input_back.1 = f32[1024,1024]{1,0:T(8,128)} custom-call(bf16[3,1024,1024]{2,1,0:T(8,128)(2,1)} %get-tuple-element.47.d_ref, bf16[1024,3072]{1,0:T(8,128)(2,1)} %w_ref.1, bf16[1024,1024]{1,0:T(8,128)(2,1)S(1)} %copy-done, f32[1,1024]{1,0:T(1,128)S(1)} %bitcast.37, f32[1024,1024]{1,0:T(8,128)} %get-tuple-element.48.dstate_ref), custom_call_target="tpu_custom_call" | custom-call | flops 6442450944 | bytes 23068672 | tf_op jit(solution)/shard_map/input_back/pallas_call | solution.py:1119
  392.3 7.3 %block_out.1 = bf16[1024,1024]{1,0:T(8,128)(2,1)} custom-call(s32[1024,128]{1,0:T(8,128)S(1)} %copy-done.8, f32[1024,128]{1,0:T(8,128)S(1)} %get-tuple-element.36.gate_ref, bf16[1280,1024]{1,0:T(8,128)(2,1)S(1)} %bitcast.41, f32[1024,1024]{1,0:T(8,128)S(1)} %copy-done.2), custom_call_target="tpu_custom_call" | custom-call | flops 5368709120 | bytes 9437184 | tf_op jit(solution)/shard_map/block_out/pallas_call | solution.py:1084
  399.7 0.2 reshape.66
  399.9 0.3 copy.30
  400.2 0.0 slice-start.4
  400.2 0.3 copy.34
  400.5 1.8 multiply_reduce_fusion
  402.3 0.6 dynamic-slice_divide_fusion
  402.9 0.7 slice.17
  403.6 0.7 copy.31
  404.3 0.7 slice_reduce_fusion
  405.0 14.1 %convolution_bitcast_fusion.1 = f32[1,1024,1408]{2,1,0:T(8,128)} fusion(bf16[8,320,1024]{2,1,0:T(8,128)(2,1)} %get-tuple-element.51, bf16[8,320,1408]{2,1,0:T(8,128)(2,1)} %get-tuple-element.53), kind=kOutput, calls=%fused_computation.4 | convolution fusion | flops 7381975040 | bytes 18219008 | tf_op jit(solution)/shard_map/dot_general | solution.py:32
  419.1 0.0 slice-start.1
  419.1 0.0 slice-start.3
  419.1 12.6 %convolution_bitcast_fusion.2 = f32[1,1024,1408]{2,1,0:T(8,128)} fusion(bf16[8,320,1024]{2,1,0:T(8,128)(2,1)S(1)} %bitcast.57, bf16[8,320,1408]{2,1,0:T(8,128)(2,1)} %get-tuple-element.52), kind=kOutput, calls=%fused_computation.5 | convolution fusion | flops 7381975040 | bytes 18219008 | tf_op jit(solution)/shard_map/dot_general | solution.py:32
  431.8 9.9 %convolution_bitcast_fusion = f32[1,1408,1024]{2,1,0:T(8,128)} fusion(bf16[8,320,1408]{2,1,0:T(8,128)(2,1)S(1)} %bitcast.53, bf16[8,320,1024]{2,1,0:T(8,128)(2,1)S(1)} %bitcast.55), kind=kOutput, calls=%fused_computation.3 | convolution fusion | flops 7381975040 | bytes 18219008 | tf_op jit(solution)/shard_map/dot_general | solution.py:32
  (59 shorter events, 0.1 us)
Async XLA Ops:
  0.6 5.9 %copy-start.30 = (bf16[1024,3072]{1,0:T(8,128)(2,1)S(1)}, bf16[1024,3072]{1,0:T(8,128)(2,1)}, u32[]{:S(2)}) copy-start(bf16[1024,3072]{1,0:T(8,128)(2,1)} %w_ref.1) | copy-start | bytes 18874372
  5.2 1.3 copy-start.25
  6.5 8.7 %copy-start.29 = (s32[1024,2]{0,1:T(2,128)S(1)}, s32[1024,2]{0,1:T(2,128)}, u32[]{:S(2)}) copy-start(s32[1024,2]{0,1:T(2,128)} %param.15) | copy-start | bytes 24580
  6.5 8.9 %copy-start.9 = (s32[1,1024]{1,0:T(1,128)S(1)}, s32[1,1024]{1,0:T(1,128)}, u32[]{:S(2)}) copy-start(s32[1,1024]{1,0:T(1,128)} %rank_row_ref.1) | copy-start | bytes 12292
  6.5 11.8 %copy-start.3 = (bf16[1024,1024]{1,0:T(8,128)(2,1)S(1)}, bf16[1024,1024]{1,0:T(8,128)(2,1)}, u32[]{:S(2)}) copy-start(bf16[1024,1024]{1,0:T(8,128)(2,1)} %og_ref.1) | copy-start | bytes 6291460
  18.4 4.0 copy-start.7
  22.4 2.8 copy-start.22
  25.2 60.1 %copy-start.28 = (bf16[1024,16]{0,1:T(8,128)(2,1)S(1)}, bf16[1024,16]{0,1:T(8,128)(2,1)}, u32[]{:S(2)}) copy-start(bf16[1024,16]{0,1:T(8,128)(2,1)} %param.21) | copy-start | bytes 98308
  25.2 60.8 %copy-start = (bf16[1024,1024]{1,0:T(8,128)(2,1)S(1)}, bf16[1024,1024]{1,0:T(8,128)(2,1)}, u32[]{:S(2)}) copy-start(bf16[1024,1024]{1,0:T(8,128)(2,1)} %tok_ref.3) | copy-start | bytes 6291460
  25.2 60.8 %copy-start.8 = (s32[1024,128]{1,0:T(8,128)S(1)}, s32[1024,128]{1,0:T(8,128)}, u32[]{:S(2)}) copy-start(s32[1024,128]{1,0:T(8,128)} %copy-done.7) | copy-start | bytes 1572868
  25.2 60.8 %copy-start.11 = (f32[1024]{0:T(1024)S(1)}, f32[1024]{0:T(1024)}, u32[]{:S(2)}) copy-start(f32[1024]{0:T(1024)} %param.20) | copy-start | bytes 12292
  82.4 1.3 copy-start.19
  83.7 1.6 copy-start.23
  85.3 0.7 copy-start.24
  86.0 11.8 %copy-start.5 = (bf16[1024,128]{1,0:T(8,128)(2,1)}, bf16[1024,128]{1,0:T(8,128)(2,1)S(1)}, u32[]{:S(2)}) copy-start(bf16[1024,128]{1,0:T(8,128)(2,1)S(1)} %pad.4.wr_ref) | copy-start | bytes 786436
  86.0 1.7 copy-start.12
  87.7 1.6 copy-start.20
  94.1 3.7 copy-start.1
  94.1 3.7 copy-start.21
  97.8 1.5 copy-start.18
  99.3 141.1 %copy-start.6 = (bf16[1024,128]{1,0:T(8,128)(2,1)S(1)}, bf16[1024,128]{1,0:T(8,128)(2,1)}, u32[]{:S(2)}) copy-start(bf16[1024,128]{1,0:T(8,128)(2,1)} %copy-done.5) | copy-start | bytes 786436
  240.4 1.6 copy-start.4
  242.0 12.1 %copy-start.13 = (bf16[1024,1024]{1,0:T(8,128)(2,1)S(1)}, bf16[1024,1024]{1,0:T(8,128)(2,1)}, u32[]{:S(2)}) copy-start(bf16[1024,1024]{1,0:T(8,128)(2,1)} %w_out_ref.1) | copy-start | bytes 6291460
  254.1 3.7 copy-start.14
  254.1 3.7 copy-start.15
  254.1 3.7 copy-start.16
  257.8 121.5 %copy-start.10 = (f32[1024]{0:T(1024)S(1)}, f32[1024]{0:T(1024)}, u32[]{:S(2)}) copy-start(f32[1024]{0:T(1024)} %param.17) | copy-start | bytes 12292
  379.3 13.0 %copy-start.2 = (f32[1024,1024]{1,0:T(8,128)S(1)}, f32[1024,1024]{1,0:T(8,128)}, u32[]{:S(2)}) copy-start(f32[1024,1024]{1,0:T(8,128)} %copy-done.1) | copy-start | bytes 12582916
  379.3 13.0 %copy-start.17 = (bf16[16,80,1024]{2,1,0:T(8,128)(2,1)S(1)}, bf16[16,80,1024]{2,1,0:T(8,128)(2,1)}, u32[]{:S(2)}) copy-start(bf16[16,80,1024]{2,1,0:T(8,128)(2,1)} %get-tuple-element.46) | copy-start | bytes 7864324
  392.3 7.4 %copy-start.26 = (f32[8,32,512]{2,1,0:T(8,128)S(1)}, f32[8,32,512]{2,1,0:T(8,128)}, u32[]{:S(2)}) copy-start(f32[8,32,512]{2,1,0:T(8,128)} %get-tuple-element.49) | copy-start | bytes 1572868
  399.7 3.9 copy-start.27
  400.2 18.9 %slice-start.4 = ((s8[5242880]{0:T(1024)(128)(4,1)}), s8[1048576]{0:T(1024)(128)(4,1)S(1)}, s32[]{:S(2)}) async-start(s8[5242880]{0:T(1024)(128)(4,1)} %bitcast.56), calls=%async_computation.4 | async-start | bytes 2097152
  404.9 14.2 %slice-start.5 = ((s8[5242880]{0:T(1024)(128)(4,1)}), s8[4194304]{0:T(1024)(128)(4,1)S(1)}, s32[]{:S(2)}) async-start(s8[5242880]{0:T(1024)(128)(4,1)} %bitcast.56), calls=%async_computation.5 | async-start | bytes 8388608
  404.9 26.8 %slice-start = ((s8[7208960]{0:T(1024)(128)(4,1)}), s8[4194304]{0:T(1024)(128)(4,1)S(1)}, s32[]{:S(2)}) async-start(s8[7208960]{0:T(1024)(128)(4,1)} %bitcast.52), calls=%async_computation | async-start | bytes 8388608
  405.0 26.8 %slice-start.2 = ((s8[5242880]{0:T(1024)(128)(4,1)}), s8[4194304]{0:T(1024)(128)(4,1)S(1)}, s32[]{:S(2)}) async-start(s8[5242880]{0:T(1024)(128)(4,1)} %bitcast.54), calls=%async_computation.2 | async-start | bytes 8388608
  419.1 12.6 %slice-start.1 = ((s8[7208960]{0:T(1024)(128)(4,1)}), s8[3014656]{0:T(1024)(128)(4,1)S(1)}, s32[]{:S(2)}) async-start(s8[7208960]{0:T(1024)(128)(4,1)} %bitcast.52), calls=%async_computation.1 | async-start | bytes 6029312
  419.1 12.6 %slice-start.3 = ((s8[5242880]{0:T(1024)(128)(4,1)}), s8[1048576]{0:T(1024)(128)(4,1)S(1)}, s32[]{:S(2)}) async-start(s8[5242880]{0:T(1024)(128)(4,1)} %bitcast.54), calls=%async_computation.3 | async-start | bytes 2097152

commit v4 on v3

--- a/solution.py
+++ b/solution.py
@@ -148,6 +148,45 @@
     )(row, data)
 
 
+def dispatch_pair_kernel(capacity, row_ref, data_ref, out_ref, other_ref):
+    count = data_ref.shape[0]
+    rows = out_ref.shape[0]
+    slot = pl.program_id(0) * rows + iota((rows, count), 0)
+    hot0 = jnp.where(slot == row_ref[0:1, :], 1.0, 0.0).astype(bf16)
+    hot1 = jnp.where(slot == row_ref[1:2, :], 1.0, 0.0).astype(bf16)
+    out_ref[...] = dot_nn(hot0 + hot1, data_ref[...]).astype(bf16)
+    ids = row_ref[...].astype(f32).astype(bf16)
+    other = dot_nt(ids, hot0)[3:4] + dot_nt(ids, hot1)[2:3]
+    other_ref[...] = jnp.zeros_like(other_ref)
+    for i in range(other_ref.shape[0]):
+        mine = other[:, i * capacity : (i + 1) * capacity]
+        other_ref[i, :, 0:capacity] = jnp.broadcast_to(mine, (8, capacity))
+
+
+def dispatch_pair(row, data, experts, capacity):
+    count, width = data.shape
+    each = 2
+    return pl.pallas_call(
+        functools.partial(dispatch_pair_kernel, capacity),
+        out_shape=(
+            jax.ShapeDtypeStruct((experts * capacity, width), bf16),
+            jax.ShapeDtypeStruct((experts, 8, LANES), f32),
+        ),
+        grid=(experts // each,),
+        in_specs=[
+            pl.BlockSpec((8, count), lambda i: (0, 0)),
+            pl.BlockSpec((count, width), lambda i: (0, 0)),
+        ],
+        out_specs=(
+            pl.BlockSpec((each * capacity, width), lambda i: (i, 0)),
+            pl.BlockSpec((each, 8, LANES), lambda i: (i, 0, 0)),
+        ),
+        compiler_params=params(40),
+        cost_estimate=cost(2 * experts * capacity * count * width, 2 * (experts * capacity + count) * width),
+        name="dispatch_pair",
+    )(row, data)
+
+
 MESH = pl.DeviceIdType.MESH
 
 
@@ -202,12 +241,16 @@
     ]
 
 
-def riding(body, n_in, n_out):
+def riding(body, n_in, n_out, n_ride):
     def kernel(*refs):
-        ins, src = refs[:n_in], refs[n_in]
-        outs, dst = refs[n_in + 1 : n_in + 1 + n_out], refs[n_in + 1 + n_out]
-        rest, sems = refs[n_in + n_out + 2 : -3], refs[-3:]
-        peers, copies = exchange_copies(src, dst, *sems)
+        ins, srcs = refs[:n_in], refs[n_in : n_in + n_ride]
+        outs = refs[n_in + n_ride : n_in + n_ride + n_out]
+        dsts = refs[n_in + n_ride + n_out : n_in + 2 * n_ride + n_out]
+        rest, sems = refs[n_in + 2 * n_ride + n_out : -3 * n_ride], refs[-3 * n_ride :]
+        copies = []
+        for r in range(n_ride):
+            peers, more = exchange_copies(srcs[r], dsts[r], *sems[3 * r : 3 * r + 3])
+            copies += more
 
         @pl.when(pl.program_id(0) == 0)
         def _():
@@ -253,7 +296,7 @@
         lse_ref[0, :, start:stop] = jnp.transpose(norm)[0:8, :]
 
 
-def attend(qkv, blocks=None):
+def attend(qkv, blocks=()):
     count, width3 = qkv.shape
     width = width3 // 3
     pairs = width // LANES
@@ -271,13 +314,14 @@
         jax.ShapeDtypeStruct((pairs, 8, count), f32),
     ]
     body, args, scratch, extra = attend_kernel, [qkv, qkv, qkv], [], {}
-    if blocks is not None:
-        body = riding(attend_kernel, len(in_specs), len(out_specs))
-        in_specs.append(pl.BlockSpec(memory_space=pl.ANY))
-        out_specs.append(pl.BlockSpec(memory_space=pl.ANY))
-        out_shape.append(jax.ShapeDtypeStruct(blocks.shape, blocks.dtype))
-        args.append(blocks)
-        scratch = exchange_sems(blocks.shape[0])
+    if blocks:
+        body = riding(attend_kernel, len(in_specs), len(out_specs), len(blocks))
+        for array in blocks:
+            in_specs.append(pl.BlockSpec(memory_space=pl.ANY))
+            out_specs.append(pl.BlockSpec(memory_space=pl.ANY))
+            out_shape.append(jax.ShapeDtypeStruct(array.shape, array.dtype))
+            args.append(array)
+            scratch = scratch + exchange_sems(array.shape[0])
         extra = dict(collective_id=0, has_side_effects=True)
     return pl.pallas_call(
         body,
@@ -351,6 +395,9 @@
     )(qkv, qkv, qkv, mixed, d_mixed, lse)
 
 
+RIDE_PER_TURN = 2
+
+
 def back_reduce_kernel(
     chips,
     q_ref, k_ref, v_ref, o_ref, do_ref, lse_ref, datt_ref, norm_ref, mix_ref, moe_ref, dlog_ref, gm_ref, slot_ref,
@@ -448,8 +495,6 @@
     @pl.when(turn == 0)
     def _():
         greet([mate] + riders)
-        for copy in ride:
-            copy.start()
         norm_t[...] = jnp.transpose(norm_ref[...])
         mix_t[...] = jnp.transpose(mix_ref[...])
         for row in range(0, width, span):
@@ -485,6 +530,13 @@
             )
             terms[turn, at : at + per, :, :, 3 * LANES :] = out_rows.astype(bf16).reshape(per, 2, rows, LANES)
         swap(turn).start()
+
+    for first in range(0, len(ride), RIDE_PER_TURN):
+
+        @pl.when(turn == first // RIDE_PER_TURN)
+        def _():
+            for copy in ride[first : first + RIDE_PER_TURN]:
+                copy.start()
 
     @pl.when(turn == pl.num_programs(0) - 1)
     def _():
@@ -697,15 +749,18 @@
 
 
 def expert_exchange_kernel(
-    group, window, x_ref, g_ref, wg_hbm, wu_hbm, wd_hbm, wr_ref,
-    act_ref, dgp_ref, dup_ref, de_ref, xs_ref, slot_ref, back_ref,
-    xb, gb, ds, rd, pd, sp, rp, pp, st_act, st_dgp, st_dup, st_de, wg_ref, wu_ref, wd_ref,
-    w_sem, x_send, x_recv, f_send, f_recv, g_own, g_send, g_recv,
-    d_send, d_recv, p_send, p_recv, b_send, b_recv, o_sem, s_sem, l_sem,
+    group, x_ref, g_ref, oth_ref, wg_hbm, wu_hbm, wd_hbm, wr_ref,
+    gg_ref, ug_ref, dg_ref, slot_ref, back_ref, pulls_ref, gm_ref,
+    xb, gb, oth, oth_mate, ds, rd, pd, sp, rp, pp, pt, pq, rq, act, dgp, dup, de, xt, acc_g, acc_u, acc_d,
+    wg_ref, wu_ref, wd_ref,
+    w_sem, x_send, x_recv, f_send, f_recv, g_load, g_send, g_recv,
+    d_send, d_recv, p_send, p_recv, q_send, q_recv, b_send, b_recv, t_send, t_recv, s_sem, l_sem, o_sem,
 ):
     experts, capacity, width = x_ref.shape
+    ff = wg_ref.shape[1]
     steps = experts // group
     pair = 2 * capacity
+    rows = group * pair
     half = experts // 2
     me = lax.axis_index("dp")
     chip, core = lax.div(me, 2), lax.rem(me, 2)
@@ -714,8 +769,7 @@
     def bits(place):
         if isinstance(place, int):
             return half + place // 2 if place % 2 else place // 2
-        odd = lax.rem(place, 2)
-        return odd * half + lax.div(place, 2)
+        return lax.rem(place, 2) * half + lax.div(place, 2)
 
     def chip_at(place):
         return flip(chip, bits(place), experts)
@@ -725,85 +779,103 @@
             src_ref=src, dst_ref=dst, send_sem=send, recv_sem=recv, device_id=(device,), device_id_type=MESH
         )
 
-    def own(buf, q, g):
-        if isinstance(g, int):
-            return buf.at[q, g * pair : g * pair + capacity]
-        return buf.at[q, pl.ds(pl.multiple_of(g * pair, 16), capacity)]
-
-    def theirs(buf, q, g):
-        return buf.at[q, g * pair + capacity : (g + 1) * pair]
+    def block(q, g, second):
+        start = q * rows + g * pair + second * capacity
+        return xb.at[pl.ds(start if isinstance(start, int) else pl.multiple_of(start, 16), capacity)]
 
     def x_copy(place):
-        if isinstance(place, int):
-            q, g = place // group, place % group
-        else:
-            q, g = lax.div(place, group), lax.rem(place, group)
         peer = chip_at(place)
-        return remote(x_ref.at[peer], own(xb, q, g), x_send.at[place], x_recv.at[place], 2 * peer + core)
+        own = block(place // group, place % group, 0)
+        return remote(x_ref.at[peer], own, x_send.at[place], x_recv.at[place], 2 * peer + core)
 
     def x_arrival(q, g):
         place = q * group + g
-        return remote(x_ref.at[chip], own(xb, q, g), x_send.at[place], x_recv.at[place], mate)
+        return remote(x_ref.at[chip], block(q, g, 0), x_send.at[place], x_recv.at[place], mate)
 
     def forward(q, g):
         place = q * group + g
-        return remote(own(xb, q, g), theirs(xb, q, g), f_send.at[place], f_recv.at[place], mate)
-
-    def g_mine(q, g):
-        place = q * group + g
-        return pltpu.make_async_copy(g_ref.at[chip_at(place)], own(gb, q, g), g_own.at[place])
+        return remote(block(q, g, 0), block(q, g, 1), f_send.at[place], f_recv.at[place], mate)
 
     def g_mate(q, g):
         place = q * group + g
-        return remote(g_ref.at[chip_at(place)], theirs(gb, q, g), g_send.at[place], g_recv.at[place], mate)
+        at = chip_at(place)
+        return remote(g_ref.at[at], gm_ref.at[at], g_send.at[place], g_recv.at[place], mate)
+
+    def g_loads(q, g):
+        slot, at = lax.rem(q, 2), chip_at(q * group + g)
+        first, second = g * pair, g * pair + capacity
+        return (
+            pltpu.make_async_copy(g_ref.at[at], gb.at[slot, first:second], g_load.at[slot, 2 * g]),
+            pltpu.make_async_copy(gm_ref.at[at], gb.at[slot, second : second + capacity], g_load.at[slot, 2 * g + 1]),
+        )
+
+    def load_g(q):
+        for g in range(group):
+            g_mate(q, g).wait_recv()
+            for copy in g_loads(q, g):
+                copy.start()
 
     def d_copy(q, g):
+        place, slot = q * group + g, lax.rem(q, 2)
+        return remote(pd.at[slot, g], rd.at[slot, g], d_send.at[place], d_recv.at[place], mate)
+
+    def p_copy(q, g):
+        place, slot = q * group + g, lax.rem(q, 2)
+        return remote(pp.at[slot, g], rp.at[slot, g], p_send.at[place], p_recv.at[place], mate)
+
+    def q_copy(q, g):
+        place, slot = q * group + g, lax.rem(q, 2)
+        return remote(pq.at[slot, g], rq.at[slot, g], q_send.at[place], q_recv.at[place], mate)
+
+    def back_copies(q, g):
         place = q * group + g
-        return remote(pd.at[lax.rem(q, 2), g], rd.at[place], d_send.at[place], d_recv.at[place], mate)
-
-    def p_copy(q, g):
-        place = q * group + g
-        return remote(pp.at[lax.rem(q, 2), g], rp.at[place], p_send.at[place], p_recv.at[place], mate)
-
-    def back_copy(q, g):
-        place = q * group + g
-        return remote(ds.at[place], back_ref.at[chip], b_send.at[place], b_recv.at[place], 2 * chip_at(place) + core)
+        device = 2 * chip_at(place) + core
+        return (
+            remote(pt.at[place], pulls_ref.at[chip], t_send.at[place], t_recv.at[place], device),
+            remote(ds.at[place], back_ref.at[chip], b_send.at[place], b_recv.at[place], device),
+        )
 
     def slot_copy(q, g):
         place = q * group + g
         return pltpu.make_async_copy(sp.at[place], slot_ref.at[chip_at(place)], s_sem.at[place])
-
-    def stage_copies(q):
-        slot = lax.rem(q, 2)
-        return (
-            pltpu.make_async_copy(st_act.at[slot], act_ref.at[q], o_sem.at[slot, 0]),
-            pltpu.make_async_copy(st_dgp.at[slot], dgp_ref.at[q], o_sem.at[slot, 1]),
-            pltpu.make_async_copy(st_dup.at[slot], dup_ref.at[q], o_sem.at[slot, 2]),
-            pltpu.make_async_copy(st_de.at[slot], de_ref.at[q], o_sem.at[slot, 3]),
-        )
-
-    def xs_copy(q):
-        return pltpu.make_async_copy(xb.at[q], xs_ref.at[q], l_sem.at[1 + q])
 
     weights = [
         pltpu.make_async_copy(src, dst, w_sem.at[i])
         for i, (src, dst) in enumerate(((wg_hbm, wg_ref), (wu_hbm, wu_ref), (wd_hbm, wd_ref)))
     ]
-    self_x = pltpu.make_async_copy(x_ref.at[chip], own(xb, 0, 0), l_sem.at[0])
-    self_back = pltpu.make_async_copy(ds.at[0], back_ref.at[chip], l_sem.at[1 + steps])
+    grads = [
+        pltpu.make_async_copy(src, dst, o_sem.at[i])
+        for i, (src, dst) in enumerate(((acc_g, gg_ref), (acc_u, ug_ref), (acc_d, dg_ref)))
+    ]
+    self_x = pltpu.make_async_copy(x_ref.at[chip], block(0, 0, 0), l_sem.at[0])
+    self_pull = pltpu.make_async_copy(pt.at[0], pulls_ref.at[chip], l_sem.at[1])
+    self_back = pltpu.make_async_copy(ds.at[0], back_ref.at[chip], l_sem.at[2])
+    oth_own = pltpu.make_async_copy(oth_ref, oth, l_sem.at[3])
+    oth_copy = remote(oth_ref, oth_mate, l_sem.at[4], l_sem.at[5], mate)
 
     for copy in weights:
         copy.start()
     self_x.start()
+    oth_own.start()
     greet([2 * chip_at(place) + core for place in range(1, experts)] + [mate])
-    for place in range(1, min(group + window, experts)):
+    oth_copy.start()
+    for place in range(1, group):
         x_copy(place).start()
     for q in range(steps):
         for g in range(group):
-            g_mine(q, g).start()
             g_mate(q, g).start()
+        for g in range(group):
+            if (q + 1) * group + g < experts:
+                x_copy((q + 1) * group + g).start()
+    for acc in (acc_g, acc_u, acc_d):
+        acc[...] = jnp.zeros_like(acc)
+    pt[...] = jnp.zeros_like(pt)
+    pq[...] = jnp.zeros_like(pq)
     self_x.wait()
     forward(0, 0).start()
+    oth_own.wait()
+    oth_copy.wait()
+    load_g(jnp.int32(0))
     for g in range(1, group):
         x_arrival(0, g).wait_recv()
         forward(0, g).start()
@@ -811,43 +883,69 @@
         copy.wait()
 
     def finish(q):
+        slot = lax.rem(q, 2)
         for g in range(group):
             place = q * group + g
+            q_copy(q, g).wait_recv()
             d_copy(q, g).wait_recv()
-            ds[place] = (ds[place].astype(f32) + rd[place].astype(f32)).astype(bf16)
+            pt[place] = pt[place] + rq[slot, g]
+            ds[place] = (ds[place].astype(f32) + rd[slot, g].astype(f32)).astype(bf16)
             if g == 0:
 
                 @pl.when(q == 0)
                 def _():
+                    self_pull.start()
                     self_back.start()
 
                 @pl.when(q > 0)
                 def _():
-                    back_copy(q, g).start()
+                    for copy in back_copies(q, g):
+                        copy.start()
 
             else:
-                back_copy(q, g).start()
+                for copy in back_copies(q, g):
+                    copy.start()
         for g in range(group):
             place = q * group + g
             p_copy(q, g).wait_recv()
-            sp[place] = (sp[place].astype(f32) + rp[place].astype(f32)).astype(bf16)
+            sp[place] = (sp[place].astype(f32) + rp[slot, g].astype(f32)).astype(bf16)
             slot_copy(q, g).start()
 
-    def step(q, carry):
+    def weight_grads(q):
+        xt[...] = jnp.transpose(xb[pl.ds(pl.multiple_of((q - 2) * rows, 16), 2 * rows), :])
+        span = 256
+        for row in range(0, width, span):
+            acc_g[row : row + span, :] += dot_nn(xt[row : row + span, :], dgp[...])
+            acc_u[row : row + span, :] += dot_nn(xt[row : row + span, :], dup[...])
+        for row in range(0, ff, LANES):
+            acc_d[row : row + LANES, :] += dot_tn(act[:, row : row + LANES], de[...])
+
+    def main(q):
+        slot = lax.rem(q, 2)
+        here = pl.ds(pl.multiple_of(slot * rows, 16), rows)
         for g in range(group):
-            g_mine(q, g).wait()
-            g_mate(q, g).wait_recv()
+            for copy in g_loads(q, g):
+                copy.wait()
             forward(q, g).wait_recv()
-        xs_copy(q).start()
-        x = xb[q]
-        rows = group * pair
+
+        @pl.when(q + 1 < steps)
+        def _():
+            load_g(q + 1)
+
+        x = xb[pl.ds(pl.multiple_of(q * rows, 16), rows), :]
         lane = iota((rows, LANES), 1)
         logits = dot_nn(x, wr_ref[...])
         mine = jnp.sum(jnp.where(lane == chip, logits, 0.0), axis=1, keepdims=True)
-        other = gb[q, :, width:].astype(f32).astype(jnp.int32)
+        ids = []
+        for g in range(group):
+            at = chip_at(q * group + g)
+            for table in (oth, oth_mate):
+                ids.append(jnp.transpose(table[at])[0:capacity, 0:1])
+        other = jnp.concatenate(ids, axis=0).astype(jnp.int32)
         alt = jnp.sum(jnp.where(lane == other, logits, 0.0), axis=1, keepdims=True)
         gate = 1.0 / (1.0 + jnp.exp(alt - mine))
-        d_rows = (gb[q, :, 0:width].astype(f32) * gate).astype(bf16)
+        d_rows = (gb[slot].astype(f32) * gate).astype(bf16)
+        de[here, :] = d_rows
         pre = dot_nn(x, wg_ref[...])
         up = dot_nn(x, wu_ref[...])
         d_hidden = dot_nt(d_rows, wd_ref[...])
@@ -856,75 +954,74 @@
         hill = 0.5 * (1.0 + bent)
         gelu = pre * hill
         slope = hill + 0.5 * pre * (1.0 - bent * bent) * (GELU_C * (1.0 + 3 * 0.044715 * square))
-        act = (gelu * up).astype(bf16)
-        dgp = (d_hidden * up * slope).astype(bf16)
-        dup = (d_hidden * gelu).astype(bf16)
-        pull = jnp.sum(act.astype(f32) * d_hidden, axis=1, keepdims=True)
-
-        @pl.when(q >= 2)
-        def _():
-            for copy in stage_copies(q - 2):
-                copy.wait()
-            for g in range(group):
-                d_copy(q - 2, g).wait_send()
-                p_copy(q - 2, g).wait_send()
-
-        slot = lax.rem(q, 2)
-        st_act[slot] = act
-        st_dgp[slot] = dgp
-        st_dup[slot] = dup
-        st_de[slot] = d_rows
-        for copy in stage_copies(q):
-            copy.start()
+        now = (gelu * up).astype(bf16)
+        act[here, :] = now
+        dgp[here, :] = (d_hidden * up * slope).astype(bf16)
+        dup[here, :] = (d_hidden * gelu).astype(bf16)
+        pull = jnp.sum(now.astype(f32) * d_hidden, axis=1, keepdims=True)
 
         @pl.when(q + 1 < steps)
         def _():
             for g in range(group):
                 x_arrival(q + 1, g).wait_recv()
                 forward(q + 1, g).start()
-            for g in range(group):
-                place = (q + 1) * group + window + g
-
-                @pl.when(place < experts)
-                def _():
-                    x_copy(place).start()
 
         @pl.when(q >= 1)
         def _():
             finish(q - 1)
 
-        d_in = (dot_nt(dgp, wg_ref[...]) + dot_nt(dup, wu_ref[...])).astype(bf16)
-        pull_high = pull.astype(bf16).astype(f32)
-        extra = jnp.where(lane == 2 * core, pull_high, 0.0)
-        extra = (extra + jnp.where(lane == 2 * core + 1, pull - pull_high, 0.0)).astype(bf16)
+        @pl.when(q >= 2)
+        def _():
+            for g in range(group):
+                q_copy(q - 2, g).wait_send()
+                d_copy(q - 2, g).wait_send()
+                p_copy(q - 2, g).wait_send()
+
+        d_in = (dot_nt(dgp[here, :], wg_ref[...]) + dot_nt(dup[here, :], wu_ref[...])).astype(bf16)
+        pull = jnp.broadcast_to(pull, (rows, LANES))
         for g in range(group):
             place = q * group + g
             low, mid, high = g * pair, g * pair + capacity, (g + 1) * pair
-            ds[place, :, 0:width] = d_in[low:mid]
-            ds[place, :, width:] = extra[low:mid]
-            pd[slot, g, :, 0:width] = d_in[mid:high]
-            pd[slot, g, :, width:] = extra[mid:high]
+            pt[place, :, 0:capacity] = jnp.transpose(pull[low:mid])[0:8, :]
+            pq[slot, g, :, 0:capacity] = jnp.transpose(pull[mid:high])[0:8, :]
+            ds[place] = d_in[low:mid]
+            pd[slot, g] = d_in[mid:high]
+            q_copy(q, g).start()
             d_copy(q, g).start()
-        partial = dot_nn(act, wd_ref[...]).astype(bf16)
+        partial = dot_nn(act[here, :], wd_ref[...]).astype(bf16)
         for g in range(group):
             place = q * group + g
             low, mid, high = g * pair, g * pair + capacity, (g + 1) * pair
             sp[place] = partial[low:mid]
             pp[slot, g] = partial[mid:high]
             p_copy(q, g).start()
+
+    def step(q, carry):
+        @pl.when(q == steps)
+        def _():
+            finish(q - 1)
+
+        @pl.when((q >= 2) & (lax.rem(q, 2) == 0))
+        def _():
+            weight_grads(q)
+
+        @pl.when(q < steps)
+        def _():
+            main(q)
+
         return carry
 
-    lax.fori_loop(0, steps, step, 0)
-    finish(steps - 1)
+    lax.fori_loop(0, steps + 1, step, 0)
+    for copy in grads:
+        copy.start()
     for q in (steps - 2, steps - 1):
-        for copy in stage_copies(q):
-            copy.wait()
         for g in range(group):
+            q_copy(q, g).wait_send()
             d_copy(q, g).wait_send()
             p_copy(q, g).wait_send()
+    self_pull.wait()
     self_back.wait()
     for q in range(steps):
-        xs_copy(q).wait()
         for g in range(group):
             place = q * group + g
             slot_copy(q, g).wait()
@@ -932,61 +1029,72 @@
             g_mate(q, g).wait_send()
             if place:
                 x_copy(place).wait_send()
-                back_copy(q, g).wait()
-
-
-def expert_exchange(x, g, wg, wu, wd, wr, group=2, window=4):
+                for copy in back_copies(q, g):
+                    copy.wait()
+    for copy in grads:
+        copy.wait()
+
+
+def expert_exchange(x, g, others, wg, wu, wd, wr, group=2):
     experts, capacity, width = x.shape
     ff = wg.shape[1]
     steps = experts // group
     rows = 2 * capacity * group
-    wide = width + LANES
     anywhere = pl.BlockSpec(memory_space=pl.ANY)
     vmem, dma = pltpu.VMEM, pltpu.SemaphoreType.DMA
     each = dma((experts,))
     count = rows * steps
     outs = pl.pallas_call(
-        functools.partial(expert_exchange_kernel, group, window),
+        functools.partial(expert_exchange_kernel, group),
         out_shape=(
-            jax.ShapeDtypeStruct((steps, rows, ff), bf16),
-            jax.ShapeDtypeStruct((steps, rows, ff), bf16),
-            jax.ShapeDtypeStruct((steps, rows, ff), bf16),
-            jax.ShapeDtypeStruct((steps, rows, width), bf16),
-            jax.ShapeDtypeStruct((steps, rows, width), bf16),
+            jax.ShapeDtypeStruct((width, ff), f32),
+            jax.ShapeDtypeStruct((width, ff), f32),
+            jax.ShapeDtypeStruct((ff, width), f32),
             jax.ShapeDtypeStruct((experts, capacity, width), bf16),
-            jax.ShapeDtypeStruct((experts, capacity, wide), bf16),
+            jax.ShapeDtypeStruct((experts, capacity, width), bf16),
+            jax.ShapeDtypeStruct((experts, 8, LANES), f32),
+            jax.ShapeDtypeStruct((experts, capacity, width), bf16),
         ),
-        in_specs=[anywhere] * 5 + [pl.BlockSpec(memory_space=vmem)],
+        in_specs=[anywhere] * 6 + [pl.BlockSpec(memory_space=vmem)],
         out_specs=(anywhere,) * 7,
         scratch_shapes=[
-            vmem((steps, rows, width), bf16),
-            vmem((steps, rows, wide), bf16),
-            vmem((experts, capacity, wide), bf16),
-            vmem((experts, capacity, wide), bf16),
-            vmem((2, group, capacity, wide), bf16),
-            vmem((experts, capacity, width), bf16),
+            vmem((steps * rows, width), bf16),
+            vmem((2, rows, width), bf16),
+            vmem((experts, 8, LANES), f32),
+            vmem((experts, 8, LANES), f32),
             vmem((experts, capacity, width), bf16),
             vmem((2, group, capacity, width), bf16),
-            vmem((2, rows, ff), bf16),
-            vmem((2, rows, ff), bf16),
-            vmem((2, rows, ff), bf16),
-            vmem((2, rows, width), bf16),
+            vmem((2, group, capacity, width), bf16),
+            vmem((experts, capacity, width), bf16),
+            vmem((2, group, capacity, width), bf16),
+            vmem((2, group, capacity, width), bf16),
+            vmem((experts, 8, LANES), f32),
+            vmem((2, group, 8, LANES), f32),
+            vmem((2, group, 8, LANES), f32),
+            vmem((2 * rows, ff), bf16),
+            vmem((2 * rows, ff), bf16),
+            vmem((2 * rows, ff), bf16),
+            vmem((2 * rows, width), bf16),
+            vmem((width, 2 * rows), bf16),
+            vmem((width, ff), f32),
+            vmem((width, ff), f32),
+            vmem((ff, width), f32),
             vmem((width, ff), bf16),
             vmem((width, ff), bf16),
             vmem((ff, width), bf16),
             dma((3,)),
-            each, each, each, each, each, each, each,
-            each, each, each, each, each, each,
-            dma((2, 4)),
-            each,
-            dma((2 + steps,)),
+            each, each, each, each,
+            dma((2, 2 * group)),
+            each, each,
+            each, each, each, each, each, each, each, each, each, each, each,
+            dma((6,)),
+            dma((3,)),
         ],
-        compiler_params=params(60, collective_id=2, has_side_effects=True),
-        cost_estimate=cost(12 * count * width * ff, 2 * count * (3 * ff + 5 * width), count * ff),
+        compiler_params=params(62, collective_id=2, has_side_effects=True),
+        cost_estimate=cost(18 * count * width * ff, 2 * count * 4 * width + 18 * width * ff, count * ff),
         name="experts",
-    )(x, g, wg, wu, wd, wr)
-    act, d_pre, d_up, d_rows, rows_in = (a.reshape(count, a.shape[-1]) for a in outs[:5])
-    return act, d_pre, d_up, d_rows, rows_in, outs[5], outs[6]
+    )(x, g, others, wg, wu, wd, wr)
+    return outs[:6]
 
 
 def hot_rows(col, k, rows, slots):
@@ -994,16 +1102,31 @@
 
 
 def state_kernel(
-    col_ref, gate_ref, din_ref, h_ref, og_ref, gain_ref, wr_ref, dstate_ref, dattn_ref, dlog_ref, gterm_ref
+    n_pull, col_ref, gate_ref, din_ref, h_ref, og_ref, gain_ref, wr_ref, *refs
 ):
+    dstate_ref, dattn_ref, dlog_ref, gterm_ref = refs[n_pull:]
     rows, width = h_ref.shape
     slots = din_ref.shape[0]
     col = col_ref[...]
     valid = col[:, 4:5].astype(f32)
     hot0, hot1 = hot_rows(col, 0, rows, slots), hot_rows(col, 1, rows, slots)
-    pulls = din_ref[:, width:]
-    pull0 = jnp.sum(dot_nn(hot0, pulls), axis=1, keepdims=True)
-    pull1 = jnp.sum(dot_nn(hot1, pulls), axis=1, keepdims=True)
+    if n_pull:
+        table = refs[0][:, 0, :]
+        experts = table.shape[0]
+        capacity = slots // experts
+
+        def pull_of(k):
+            chosen = jnp.where(iota((rows, experts), 1) == col[:, 2 + k : 3 + k], 1.0, 0.0)
+            values = dot_nn(chosen, table, precision=lax.Precision.HIGHEST)
+            slot = col[:, k : k + 1] - capacity * col[:, 2 + k : 3 + k]
+            here = (iota((rows, LANES), 1) == slot) & (col[:, k : k + 1] < slots)
+            return jnp.sum(jnp.where(here, values, 0.0), axis=1, keepdims=True)
+
+        pull0, pull1 = pull_of(0), pull_of(1)
+    else:
+        pulls = din_ref[:, width:]
+        pull0 = jnp.sum(dot_nn(hot0, pulls), axis=1, keepdims=True)
+        pull1 = jnp.sum(dot_nn(hot1, pulls), axis=1, keepdims=True)
     gathered = dot_nn(hot0 + hot1, din_ref[:, 0:width])
     gate0, gate1 = gate_ref[:, 0:1], gate_ref[:, 1:2]
     total = pull0 + pull1
@@ -1030,14 +1153,14 @@
     gterm_ref[...] += term
 
 
-def state_back(col, gates, din, hidden, out_grad, gain, wr):
+def state_back(col, gates, din, hidden, out_grad, gain, wr, pulls=()):
     count, width = hidden.shape
     slots = din.shape[0]
     rows = 256
     whole = lambda i: (0, 0)
     part = lambda i: (i, 0)
     return pl.pallas_call(
-        state_kernel,
+        functools.partial(state_kernel, len(pulls)),
         out_shape=(
             jax.ShapeDtypeStruct((count, width), f32),
             jax.ShapeDtypeStruct((count, width), bf16),
@@ -1048,12 +1171,13 @@
         in_specs=[
             pl.BlockSpec((rows, LANES), part),
             pl.BlockSpec((rows, LANES), part),
-            pl.BlockSpec((slots, width + LANES), whole),
+            pl.BlockSpec(din.shape, whole),
             pl.BlockSpec((rows, width), part),
             pl.BlockSpec((rows, width), part),
             pl.BlockSpec((1, width), whole),
             pl.BlockSpec((width, LANES), whole),
-        ],
+        ]
+        + [pl.BlockSpec(p.shape, lambda i: (0, 0, 0)) for p in pulls],
         out_specs=(
             pl.BlockSpec((rows, width), part),
             pl.BlockSpec((rows, width), part),
@@ -1063,7 +1187,7 @@
         compiler_params=params(48),
         cost_estimate=cost(2 * slots * count * width, 14 * count * width),
         name="state_back",
-    )(col, gates, din, hidden, out_grad, gain.reshape(1, width), wr)
+    )(col, gates, din, hidden, out_grad, gain.reshape(1, width), wr, *pulls)
 
 
 def block_out_kernel(col_ref, gate_ref, rows_ref, h_ref, out_ref):
@@ -1098,7 +1222,10 @@
     )(col, gates, slot_rows, hidden)
 
 
-def input_kernel(d_ref, w_ref, tok_ref, gain_ref, dstate_ref, grad_ref):
+def input_kernel(n_ride, d_ref, w_ref, tok_ref, gain_ref, dstate_ref, *refs):
+    srcs, grad_ref, dsts = refs[:n_ride], refs[n_ride], refs[n_ride + 1 :]
+    for src, dst in zip(srcs, dsts):
+        dst[...] = src[...]
     rows, width = tok_ref.shape
     d_normed = dot_nt(d_ref[0], w_ref[:, 0:width])
     for i in range(1, 3):
@@ -1111,27 +1238,31 @@
     grad_ref[...] = dstate_ref[...] + inverse * (scaled - normal * share)
 
 
-def input_back(d_qkv, w_qkv, tokens, gain, d_state):
+def input_back(d_qkv, w_qkv, tokens, gain, d_state, riders=()):
     count, width = tokens.shape
     rows = 256
+    steps = count // rows
     whole = lambda i: (0, 0)
     part = lambda i: (i, 0)
+    passed = [pl.BlockSpec((array.shape[0] // steps, array.shape[1]), part) for array in riders]
     return pl.pallas_call(
-        input_kernel,
-        out_shape=jax.ShapeDtypeStruct((count, width), f32),
-        grid=(count // rows,),
+        functools.partial(input_kernel, len(riders)),
+        out_shape=[jax.ShapeDtypeStruct((count, width), f32)]
+        + [jax.ShapeDtypeStruct(array.shape, array.dtype) for array in riders],
+        grid=(steps,),
         in_specs=[
             pl.BlockSpec((3, rows, width), lambda i: (0, i, 0)),
             pl.BlockSpec((width, 3 * width), whole),
             pl.BlockSpec((rows, width), part),
             pl.BlockSpec((1, width), whole),
             pl.BlockSpec((rows, width), part),
-        ],
-        out_specs=pl.BlockSpec((rows, width), part),
-        compiler_params=params(48),
+        ]
+        + passed,
+        out_specs=[pl.BlockSpec((rows, width), part)] + passed,
+        compiler_params=params(56),
         cost_estimate=cost(6 * count * width * width, 22 * count * width),
         name="input_back",
-    )(d_qkv, w_qkv, tokens, gain.reshape(1, width), d_state)
+    )(d_qkv, w_qkv, tokens, gain.reshape(1, width), d_state, *riders)
 
 
 def shards(
@@ -1199,25 +1330,26 @@
     wr = jnp.pad(w_router, ((0, 0), (0, LANES - experts)))
     col, row = make_slots(lengths, expert_ids, slot_order, experts, capacity)
     direct = split == 2 and experts & (experts - 1) == 0 and experts >= 4
-    grad_out = dispatch_grad(row, out_grad, slots)
 
     token_vals = tokens.astype(f32)
     inverse_attn = lax.rsqrt(jnp.mean(token_vals * token_vals, axis=-1, keepdims=True) + epsilon)
     normed_low = (token_vals * inverse_attn * gain_attn).astype(bf16)
     qkv = jnp.dot(normed_low, w_qkv, preferred_element_type=f32).astype(bf16)
     if direct:
-        mixed, lse, grad_in = attend(qkv, grad_out.reshape(experts, capacity, -1))
+        grad_out, others = dispatch_pair(row, out_grad, experts, capacity)
+        mixed, lse, grad_in, others = attend(qkv, (grad_out.reshape(experts, capacity, -1), others))
     else:
         mixed, lse = attend(qkv)
-        grad_in = send_in(grad_out)
+        grad_in = send_in(dispatch_grad(row, out_grad, slots))
     hidden, moe_low, gates = middle(mixed, w_out, tokens, gain_moe, wr, col, experts)
 
     rows_out = dispatch(row, moe_low, slots)
     if direct:
-        act, d_pre, d_up, d_rows, rows_in, slot_part, d_in_back = expert_exchange(
-            rows_out.reshape(experts, capacity, -1), grad_in, w_gate[0], w_up[0], w_down[0], wr
+        gate_grad, up_grad, down_grad, slot_part, d_in_back, pulls = expert_exchange(
+            rows_out.reshape(experts, capacity, -1), grad_in, others, w_gate[0], w_up[0], w_down[0], wr
         )
         d_in_back = d_in_back.reshape(slots, -1)
+        pulls = (pulls,)
     else:
         rows_in = send_in(rows_out)
         act, d_pre, d_up, d_rows, partial_out, d_in = expert_pass(
@@ -1225,9 +1357,13 @@
         )
         d_in_back = send_back(d_in)
         slot_out = send_back(partial_out)
+        pulls = ()
+        down_grad = dot_tn(act, d_rows)
+        gate_grad = dot_tn(rows_in, d_pre)
+        up_grad = dot_tn(rows_in, d_up)
 
     d_state, d_attn, d_log, gain_moe_rows = state_back(
-        col, gates, d_in_back, hidden, out_grad, gain_moe, wr
+        col, gates, d_in_back, hidden, out_grad, gain_moe, wr, pulls
     )
     d_mixed = dot_nt(d_attn, w_out).astype(bf16)
     if direct:
@@ -1246,14 +1382,16 @@
             early[:, 0:width], early[:, width : width + experts], early[:, width + experts]
         )
         qkv_sum = reduce_rows(jnp.concatenate([dot_tn(normed_low, d_qkv[i]) for i in range(3)], axis=1))
-    tokens_grad = input_back(d_qkv, w_qkv, tokens, gain_attn, d_state)
+    if direct:
+        tokens_grad, gate_grad, up_grad, down_grad = input_back(
+            d_qkv, w_qkv, tokens, gain_attn, d_state, (gate_grad, up_grad, down_grad)
+        )
+    else:
+        (tokens_grad,) = input_back(d_qkv, w_qkv, tokens, gain_attn, d_state)
     my_rows = width // n_dev
     weight_rows = lax.dynamic_slice_in_dim(w_qkv, me * my_rows, my_rows, 0).astype(f32)
     gain_attn_sum = jnp.sum(weight_rows * qkv_sum, axis=1) / lax.dynamic_slice_in_dim(gain_attn, me * my_rows, my_rows, 0)
 
-    down_grad = dot_tn(act, d_rows)
-    gate_grad = dot_tn(rows_in, d_pre)
-    up_grad = dot_tn(rows_in, d_up)
     block_out = make_block_out(col, gates, slot_out, hidden)
     return (
         block_out,

time: 450 us -> 413 us (0.918)
  the two profiles are of different devices: /device:TPU:0 before, /device:TPU:12 now
where the time goes in v4:
time: 413 us; the launch traced here: 406 us
  Pallas kernels  364 us (88%)
  local copies, waits for them, and re-layouts  23.1 us (6%)
  matrix products  12.4 us (3%)
  other arithmetic  4.13 us (1%)
    pallas_call x1, Pallas kernels, expert_exchange(): pl.pallas_call(functools.partial(expert_exchange_kernel, group), out_shap...  125 us
    pallas_call x1, Pallas kernels, attend_back_reduce(): pl.pallas_call(functools.partial(back_reduce_kernel, chips), out_shape=(j...  118 us
    pallas_call x1, Pallas kernels, attend(): pl.pallas_call(body, out_shape=out_shape, grid=(pairs,), in_specs=in_spec...  64.3 us
    pallas_call x1, Pallas kernels, input_back(): pl.pallas_call(functools.partial(input_kernel, len(riders)), out_shape=[j...  21 us
    unnamed x68, local copies, waits for them, and re-layouts  20.3 us
    pallas_call x1, Pallas kernels, state_back(): pl.pallas_call(functools.partial(state_kernel, len(pulls)), out_shape=(ja...  12 us
    dot_general x1, matrix products, shards(): qkv = jnp.dot(normed_low, w_qkv, preferred_element_type=f32).astype(bf16)  8.73 us

profile of v4, /device:TPU:12, one launch (start us, length us, event | category | flops | bytes accessed | tf_op | source)
XLA Modules:
  0.0 406.1 jit_solution(1342591348151885758)
XLA Ops:
  0.6 0.0 copy-start
  1.4 0.9 copy.27.ids_ref
  2.4 0.9 copy.28.rank_col_ref
  3.3 0.0 copy-start.10
  3.3 0.7 copy-done.10
  4.0 2.0 slots.1
  6.0 0.0 copy-start.26
  6.0 0.5 fusion
  6.5 0.3 copy-done.7
  6.8 0.5 fusion.2.norm_ref
  7.3 1.6 copy-done.26
  9.0 8.7 %convolution_convert_fusion.refs_0_.refs_1_.refs_2_.q_ref.k_ref.v_ref = bf16[1024,3072]{1,0:T(8,128)(2,1)} fusion(bf16[1024,1024]{1,0:T(8,128)(2,1)S(1)} %fusion.2.norm_ref, bf16[1024,3072]{1,0:T(8,128)(2,1)S(1)} %copy-done.26), kind=kOutput, calls=%fused_computation | convolution fusion | flops 6445596672 | bytes 14680064 | tf_op jit(solution)/shard_map/dot_general | solution.py:1337
  17.7 6.2 %dispatch_pair.1 = (bf16[1280,1024]{1,0:T(8,128)(2,1)S(1)}, f32[16,8,128]{2,1,0:T(8,128)S(1)}) custom-call(s32[8,1024]{1,0:T(8,128)S(1)} %get-tuple-element.40.row_ref, bf16[1024,1024]{1,0:T(8,128)(2,1)S(1)} %copy-done.3), custom_call_target="tpu_custom_call" | custom-call | flops 2684354560 | bytes 4718592 | tf_op jit(solution)/shard_map/dispatch_pair/pallas_call | solution.py:169
  23.9 2.8 copy-done.22
  26.7 64.3 %attend.1 = (bf16[1024,1024]{1,0:T(8,128)(2,1)S(1)}, f32[8,8,1024]{2,1,0:T(8,128)S(1)}, bf16[16,80,1024]{2,1,0:T(8,128)(2,1)S(1)}, f32[16,8,128]{2,1,0:T(8,128)S(1)}) custom-call(bf16[1024,3072]{1,0:T(8,128)(2,1)S(1)} %copy-done.22, bf16[1024,3072]{1,0:T(8,128)(2,1)S(1)} %copy-done.22, bf16[1024,3072]{1,0:T(8,128)(2,1)S(1)} %copy-done.22, ...), custom_call_target="tpu_custom_call" | custom-call | flops 8589934592 | bytes 8388608 | tf_op jit(solution)/shard_map/attend/pallas_call | solution.py:326
  91.1 0.0 copy-start.19
  91.1 1.3 copy-done.19
  92.4 1.5 copy-done.23
  93.9 0.7 copy-done.24
  94.6 0.2 copy.29
  94.8 0.5 copy-done.25
  95.2 0.1 pad.4.wr_ref
  95.3 0.0 copy-start.12
  95.3 1.6 copy-done.12
  96.9 1.6 copy-done.20
  98.5 4.9 %middle.1 = (f32[1024,1024]{1,0:T(8,128)S(1)}, bf16[1024,1024]{1,0:T(8,128)(2,1)S(1)}, f32[1024,128]{1,0:T(8,128)S(1)}) custom-call(bf16[1024,1024]{1,0:T(8,128)(2,1)S(1)} %copy-done.20, bf16[1024,1024]{1,0:T(8,128)(2,1)S(1)} %copy-done.12, bf16[1024,1024]{1,0:T(8,128)(2,1)S(1)} %copy-done, f32[1,1024]{1,0:T(1,128)S(1)} %bitcast.25, ...), custom_call_target="tpu_custom_call" | custom-call | flops 2147483648 | bytes 12582912 | tf_op jit(solution)/shard_map/middle/pallas_call | solution.py:642
  103.4 0.0 copy-start.1
  103.4 3.6 dispatch.1
  107.1 0.0 copy-start.18
  107.1 1.5 copy-done.18
  108.6 125.1 %experts.1 = (f32[1024,1408]{1,0:T(8,128)}, f32[1024,1408]{1,0:T(8,128)}, f32[1408,1024]{1,0:T(8,128)}, bf16[16,80,1024]{2,1,0:T(8,128)(2,1)}, bf16[16,80,1024]{...) custom-call(bf16[16,80,1024]{2,1,0:T(8,128)(2,1)} %bitcast.28, ...), custom_call_target="tpu_custom_call" | custom-call | flops 66437775360 | bytes 46923776 | tf_op jit(solution)/shard_map/experts/pallas_call | solution.py:1047
  233.7 0.0 copy-start.4
  233.7 1.6 copy-done.4
  235.3 0.8 copy-done.9
  236.1 12.0 %state_back.1 = (f32[1024,1024]{1,0:T(8,128)}, bf16[1024,1024]{1,0:T(8,128)(2,1)S(1)}, bf16[1024,128]{1,0:T(8,128)(2,1)S(1)}, f32[8,1024]{1,0:T(8,128)S(1)}) custom-call(s32[1024,128]{1,0:T(8,128)S(1)} %copy-done.8, f32[1024,128]{1,0:T(8,128)S(1)} %get-tuple-element.44.gate_ref, bf16[1280,1024]{1,0:T(8,128)(2,1)} %bitcast.30, f32[1024,1024]{1,0:T(8,128)} %copy-done.1, ...), custom_call_target="tpu_custom_call" | custom-call | flops 2684354560 | bytes 14680064 | tf_op jit(solution)/shard_map/state_back/pallas_call | solution.py:1162
  248.1 3.7 convolution_convert_fusion.1.do_ref
  251.8 118.2 %attend_back_reduce.1 = (bf16[3,1024,1024]{2,1,0:T(8,128)(2,1)}, f32[8,32,512]{2,1,0:T(8,128)}, f32[32,128]{1,0:T(8,128)}, bf16[16,80,1024]{2,1,0:T(8,128)(2,1)}) custom-call(bf16[1024,3072]{1,0:T(8,128)(2,1)} %convolution_convert_fusion.refs_0_.refs_1_.refs_2_.q_ref.k_ref.v_ref, ...), custom_call_target="tpu_custom_call" | custom-call | flops 21474836480 | bytes 41943040 | tf_op jit(solution)/shard_map/attend_back_reduce/pallas_call | solution.py:566
  370.1 1.7 copy-done.17
  371.8 7.2 %block_out.1 = bf16[1024,1024]{1,0:T(8,128)(2,1)} custom-call(s32[1024,128]{1,0:T(8,128)S(1)} %copy-done.8, f32[1024,128]{1,0:T(8,128)S(1)} %get-tuple-element.44.gate_ref, bf16[1280,1024]{1,0:T(8,128)(2,1)S(1)} %bitcast.27, f32[1024,1024]{1,0:T(8,128)S(1)} %copy-done.2), custom_call_target="tpu_custom_call" | custom-call | flops 5368709120 | bytes 9437184 | tf_op jit(solution)/shard_map/block_out/pallas_call | solution.py:1208
  378.9 21.0 %input_back.1 = (f32[1024,1024]{1,0:T(8,128)}, f32[1024,1408]{1,0:T(8,128)}, f32[1024,1408]{1,0:T(8,128)}, f32[1408,1024]{1,0:T(8,128)}) custom-call(bf16[3,1024,1024]{2,1,0:T(8,128)(2,1)} %get-tuple-element.57.d_ref, bf16[1024,3072]{1,0:T(8,128)(2,1)} %w_ref.1, bf16[1024,1024]{1,0:T(8,128)(2,1)} %tok_ref.3, f32[1,1024]{1,0:T(1,128)} %bitcast.36, ...), custom_call_target="tpu_custom_call" | custom-call | flops 6442450944 | bytes 23068672 | tf_op jit(solution)/shard_map/input_back/pallas_call | solution.py:1248
  399.9 0.2 reshape.61
  400.1 0.3 copy.30
  400.5 0.3 copy.34
  400.8 1.8 multiply_reduce_fusion
  402.6 1.3 dynamic-slice_divide_fusion
  403.9 0.7 slice.17
  404.5 0.7 slice_reduce_fusion
  405.2 0.7 copy.31
  (43 shorter events, 0.1 us)
Async XLA Ops:
  0.6 5.3 %copy-start = (bf16[1024,1024]{1,0:T(8,128)(2,1)S(1)}, bf16[1024,1024]{1,0:T(8,128)(2,1)}, u32[]{:S(2)}) copy-start(bf16[1024,1024]{1,0:T(8,128)(2,1)} %tok_ref.3) | copy-start | bytes 6291460
  3.3 0.7 copy-start.10
  4.0 2.8 copy-start.31
  6.0 0.8 copy-start.7
  6.0 3.0 copy-start.26
  9.0 8.7 %copy-start.27 = (bf16[1024,1024]{1,0:T(8,128)(2,1)}, bf16[1024,1024]{1,0:T(8,128)(2,1)S(1)}, u32[]{:S(2)}) copy-start(bf16[1024,1024]{1,0:T(8,128)(2,1)S(1)} %fusion.2.norm_ref) | copy-start | bytes 6291460
  9.0 8.7 %copy-start.3 = (bf16[1024,1024]{1,0:T(8,128)(2,1)S(1)}, bf16[1024,1024]{1,0:T(8,128)(2,1)}, u32[]{:S(2)}) copy-start(bf16[1024,1024]{1,0:T(8,128)(2,1)} %og_ref.1) | copy-start | bytes 6291460
  23.9 2.8 copy-start.22
  26.7 67.9 %copy-start.30 = (bf16[1024,16]{0,1:T(8,128)(2,1)S(1)}, bf16[1024,16]{0,1:T(8,128)(2,1)}, u32[]{:S(2)}) copy-start(bf16[1024,16]{0,1:T(8,128)(2,1)} %param.21) | copy-start | bytes 98308
  26.7 68.6 %copy-start.8 = (s32[1024,128]{1,0:T(8,128)S(1)}, s32[1024,128]{1,0:T(8,128)}, u32[]{:S(2)}) copy-start(s32[1024,128]{1,0:T(8,128)} %copy-done.7) | copy-start | bytes 1572868
  26.7 68.6 %copy-start.11 = (f32[1024]{0:T(1024)S(1)}, f32[1024]{0:T(1024)}, u32[]{:S(2)}) copy-start(f32[1024]{0:T(1024)} %param.20) | copy-start | bytes 12292
  91.1 1.3 copy-start.19
  92.4 1.5 copy-start.23
  93.9 0.7 copy-start.24
  94.6 0.6 copy-start.25
  95.3 1.6 copy-start.12
  96.9 1.6 copy-start.20
  98.5 4.9 %copy-start.5 = (bf16[1024,128]{1,0:T(8,128)(2,1)}, bf16[1024,128]{1,0:T(8,128)(2,1)S(1)}, u32[]{:S(2)}) copy-start(bf16[1024,128]{1,0:T(8,128)(2,1)S(1)} %pad.4.wr_ref) | copy-start | bytes 786436
  103.4 3.7 copy-start.1
  103.4 3.7 copy-start.21
  107.1 1.5 copy-start.18
  108.6 125.1 %copy-start.6 = (bf16[1024,128]{1,0:T(8,128)(2,1)S(1)}, bf16[1024,128]{1,0:T(8,128)(2,1)}, u32[]{:S(2)}) copy-start(bf16[1024,128]{1,0:T(8,128)(2,1)} %copy-done.5) | copy-start | bytes 786436
  233.7 1.6 copy-start.4
  235.3 0.8 copy-start.9
  236.1 12.0 %copy-start.13 = (bf16[1024,1024]{1,0:T(8,128)(2,1)S(1)}, bf16[1024,1024]{1,0:T(8,128)(2,1)}, u32[]{:S(2)}) copy-start(bf16[1024,1024]{1,0:T(8,128)(2,1)} %w_out_ref.1) | copy-start | bytes 6291460
  248.1 3.7 copy-start.14
  248.1 3.7 copy-start.15
  248.1 3.7 copy-start.16
  251.8 118.2 %copy-start.2 = (f32[1024,1024]{1,0:T(8,128)S(1)}, f32[1024,1024]{1,0:T(8,128)}, u32[]{:S(2)}) copy-start(f32[1024,1024]{1,0:T(8,128)} %copy-done.1) | copy-start | bytes 12582916
  370.0 1.7 copy-start.17
  378.9 21.0 %copy-start.28 = (f32[8,32,512]{2,1,0:T(8,128)S(1)}, f32[8,32,512]{2,1,0:T(8,128)}, u32[]{:S(2)}) copy-start(f32[8,32,512]{2,1,0:T(8,128)} %get-tuple-element.63) | copy-start | bytes 1572868
  399.9 4.6 %copy-start.29 = (f32[32,128]{1,0:T(8,128)S(1)}, f32[32,128]{1,0:T(8,128)}, u32[]{:S(2)}) copy-start(f32[32,128]{1,0:T(8,128)} %get-tuple-element.64) | copy-start | bytes 49156
